TPU v7x, 128 devices: a whole 4x4x4 slice. The times are simulated.
128 devices in a mesh: head: 16 (over y, z_hi, core), tail: 8 (over z_lo, x).
Axes of the slice: x: 4, y: 4, z: 4 (z_hi: 2, z_lo: 2; z = z_hi * 2 + z_lo), core: 2. Of those that a mesh axis runs over, the one named last changes fastest.
Arguments:
- head_emb: float32 [16, 512, 256], P('head'), may hold values from -1.5 to 1.5
- tail_emb: float32 [8, 2048, 256], P('tail'), may hold values from -1.5 to 1.5
- relations: float32 [4096, 256], P(('head', 'tail')), may hold values from -0.375 to 0.375
- head_index: int32 [16, 8, 2, 1, 512], P('head', 'tail'), may hold values from 0 to 511
- tail_index: int32 [16, 8, 2, 1, 512], P('head', 'tail'), may hold values from 0 to 2047
- rel_index: int32 [16, 8, 2, 1, 512], P('head', 'tail'), may hold values from 0 to 15
- neg_index: int32 [16, 8, 2, 1, 512], P('head', 'tail'), may hold values from 0 to 2047
Outputs:
- head_grad: float32 [16, 512, 256], P('head', 'tail')
- tail_grad: float32 [8, 2048, 256], P('tail', 'head')
- rel_grad: float32 [4096, 256], P(('head', 'tail'))
All inputs are finite; a program needn't handle non-finite values.
Results may differ from a plain program's by a relative error of at most 0.00028.
Values sent between devices are 32-bit elements; how exact they have to be, the bound alone decides.
No kernel may reach another device: no remote copies, remote signals or barrier semaphores. Data moves between devices by JAX's collectives and lax.ppermute only.
A program may use at most 128 MiB of HBM per device.

v0:
```python
import jax
import jax.numpy as jnp
from jax import lax
from jax.sharding import PartitionSpec as P


def from_behind(array, axis, by):
    devices = lax.axis_size(axis)
    return lax.ppermute(array, axis, [(i, (i + by) % devices) for i in range(devices)])


def per_device(head_emb, tail_emb, relations, head_index, tail_index, rel_index, neg_index):
    highest = lax.Precision.HIGHEST
    width = relations.shape[1]
    all_rel = lax.all_gather(relations, ("head", "tail"), axis=0, tiled=True)
    count_rel = all_rel.shape[0] // width
    rel_mats = all_rel.reshape(count_rel, width, width)
    rel_trans = jnp.transpose(rel_mats, (0, 2, 1))
    heads = head_emb[0]
    current = tail_emb[0]
    steps = head_index.shape[2]
    batch = head_index.shape[4]
    head_acc = jnp.zeros(heads.shape, jnp.float32)
    moving = jnp.zeros(current.shape, jnp.float32)
    spread_rows = []
    factors = []
    rel_ids = jnp.arange(count_rel, dtype=jnp.int32)
    for step in range(steps):
        if step > 0:
            current, moving = from_behind((current, moving), "tail", 1)
        local = jnp.zeros(current.shape, jnp.float32)
        order = jnp.argsort(rel_index[0, 0, step, 0], stable=True)
        rows_h = head_index[0, 0, step, 0][order]
        rows_t = tail_index[0, 0, step, 0][order]
        rows_r = rel_index[0, 0, step, 0][order]
        rows_n = neg_index[0, 0, step, 0]
        head_vec = jnp.take(heads, rows_h, axis=0)
        onehot = (rows_r[:, None] == rel_ids[None, :]).astype(jnp.float32)
        group_sizes = jnp.sum((rows_r[:, None] == rel_ids[None, :]).astype(jnp.int32), axis=0)
        query = lax.ragged_dot(
            head_vec, rel_mats, group_sizes, precision=highest, preferred_element_type=jnp.float32
        )
        tail_vec = jnp.take(current, rows_t, axis=0)
        negatives = jnp.take(current, rows_n, axis=0)
        positive = jnp.sum(query * tail_vec, axis=1)
        negative = jnp.einsum("be,ne->bn", query, negatives, precision=highest)
        coef = -jax.nn.sigmoid(-positive)
        weights = jax.nn.sigmoid(negative) / negatives.shape[0]
        factor = coef[:, None] * tail_vec + jnp.dot(weights, negatives, precision=highest)
        through = lax.ragged_dot(
            factor, rel_trans, group_sizes, precision=highest, preferred_element_type=jnp.float32
        )
        head_acc = head_acc.at[rows_h].add(through)
        local = local.at[rows_t].add(coef[:, None] * query)
        local = local.at[rows_n].add(jnp.einsum("bn,be->ne", weights, query, precision=highest))
        spread = (onehot[:, :, None] * head_vec[:, None, :]).reshape(batch, count_rel * width)
        spread_rows.append(spread)
        factors.append(factor)
        moving = moving + local
    back_home = from_behind(moving, "tail", -(steps - 1))
    tail_share = lax.psum_scatter(back_home, "head", scatter_dimension=0, tiled=True)
    head_share = lax.psum_scatter(head_acc, "tail", scatter_dimension=0, tiled=True)
    spread_all = jnp.concatenate(spread_rows, axis=0)
    factor_all = jnp.concatenate(factors, axis=0)
    rel_share = lax.psum_scatter(
        jnp.einsum("bk,be->ke", spread_all, factor_all, precision=highest),
        ("head", "tail"),
        scatter_dimension=0,
        tiled=True,
    )
    return (head_share[None], tail_share[None], rel_share)


def solution(mesh):
    placed = (
        P("head", None, None),
        P("tail", None, None),
        P(("head", "tail"), None),
        P("head", "tail", None, None, None),
        P("head", "tail", None, None, None),
        P("head", "tail", None, None, None),
        P("head", "tail", None, None, None),
    )
    return jax.shard_map(
        per_device,
        mesh=mesh,
        in_specs=placed,
        out_specs=(P("head", "tail", None), P("tail", "head", None), P(("head", "tail"), None)),
        check_vma=False,
    )
```

profile of v0, /device:TPU:0, one launch (start us, length us, event | category | flops | bytes accessed | tf_op | source)
XLA Modules:
  0.0 1247.2 jit_solution(13085485693688693857)
XLA Ops:
  8.0 1.6 collective-permute-start
  10.3 3.8 sort.31
  14.1 3.5 gather_fusion.1
  17.6 3.5 gather_fusion.2
  21.2 3.5 gather_fusion
  25.3 1.8 ragged-dot-metadata.1
  27.1 3.8 sort.32
  30.9 3.5 gather_fusion.4
  34.4 3.5 gather_fusion.5
  37.9 3.5 gather_fusion.3
  41.4 2.2 gather_fusion.8
  43.7 2.2 gather_fusion.7
  46.0 1.6 gather_fusion.6
  48.2 1.0 broadcast_select_fusion.1
  49.2 291.8 %all-gather.2.cloned.1.call-done = f32[4096,256]{1,0:T(8,128)} async-done(((f32[32,256]{1,0:T(8,128)}), f32[4096,256]{1,0:T(8,128)}) %all-gather.2.cloned.1.call-update) | async-done | bytes 4194320 | tf_op jit(solution)/shard_map/all_gather | solution.py:15
  341.0 15.3 %ragged-dot-none.3 = f32[512,256]{1,0:T(8,128)} custom-call(s32[1]{0:T(128)} %get-tuple-element.17, s32[17]{0:T(128)} %get-tuple-element.18, s32[17]{0:T(128)} %get-tuple-element.19, s32[17]{0:T(128)} %get-tuple-element.20, s32[1]{0:T(128)} %get-tuple-element.17, f32[512,256]{1,0:T(8,128)} %broadcast_select_fusion.1, f32[16,256,256]{2,1,0:T(8,128)} %bitcast.50), custom_call_target="tpu_custom_call" | custom-call | flops 67108864 | bytes 5242944 | tf_op jit(solution)/shard_map/ragged_dot_general/ragged-dot-none
  356.4 1.3 multiply_reduce_fusion.1
  357.7 4.7 scatter_custom_fusion.2
  362.4 2.3 fusion.11
  364.7 2.6 fusion.50
  367.3 4.6 scatter_fusion.1
  372.7 1.8 ragged-dot-metadata
  374.5 1.6 gather_fusion.9
  376.1 0.9 broadcast_select_fusion
  377.1 3.8 gather_fusion.11
  380.9 3.2 gather_fusion.10
  384.0 15.2 %ragged-dot-none.1 = f32[512,256]{1,0:T(8,128)} custom-call(s32[1]{0:T(128)} %get-tuple-element.9, s32[17]{0:T(128)} %get-tuple-element.10, s32[17]{0:T(128)} %get-tuple-element.11, s32[17]{0:T(128)} %get-tuple-element.12, s32[1]{0:T(128)} %get-tuple-element.9, f32[512,256]{1,0:T(8,128)} %broadcast_select_fusion, f32[16,256,256]{2,1,0:T(8,128)} %bitcast.51), custom_call_target="tpu_custom_call" | custom-call | flops 67108864 | bytes 5242944 | tf_op jit(solution)/shard_map/ragged_dot_general/ragged-dot-none
  399.3 1.3 multiply_reduce_fusion
  400.6 2.5 fusion.7
  403.1 2.6 fusion.51
  405.8 16.6 %collective-permute-done.1 = f32[2048,256]{1,0:T(8,128)} collective-permute-done((f32[2048,256]{1,0:T(8,128)S(1)}, f32[2048,256]{1,0:T(8,128)}, u32[]{:S(2)}, u32[]{:S(2)}) %collective-permute-start.1) | collective-permute-done | bytes 2097184 | tf_op jit(solution)/shard_map/ppermute | solution.py:9
  422.4 6.2 scatter_custom_fusion.4
  428.6 6.0 scatter_fusion.2
  434.6 5.5 copy.13
  440.1 1.9 convolution_add_fusion
  442.0 15.8 %ragged-dot-none.2 = f32[512,256]{1,0:T(8,128)} custom-call(s32[1]{0:T(128)} %get-tuple-element.17, s32[17]{0:T(128)} %get-tuple-element.18, s32[17]{0:T(128)} %get-tuple-element.19, s32[17]{0:T(128)} %get-tuple-element.20, s32[1]{0:T(128)} %get-tuple-element.17, f32[512,256]{1,0:T(8,128)} %convolution_add_fusion, f32[16,256,256]{2,1,0:T(8,128)} %bitcast.53), custom_call_target="tpu_custom_call" | custom-call | flops 67108864 | bytes 5242944 | tf_op jit(solution)/shard_map/ragged_dot_general/ragged-dot-none
  457.8 3.9 scatter_custom_fusion
  461.8 1.9 multiply_add_fusion
  463.7 15.0 %ragged-dot-none = f32[512,256]{1,0:T(8,128)} custom-call(s32[1]{0:T(128)} %get-tuple-element.9, s32[17]{0:T(128)} %get-tuple-element.10, s32[17]{0:T(128)} %get-tuple-element.11, s32[17]{0:T(128)} %get-tuple-element.12, s32[1]{0:T(128)} %get-tuple-element.9, f32[512,256]{1,0:T(8,128)} %multiply_add_fusion, f32[16,256,256]{2,1,0:T(8,128)} %bitcast.54), custom_call_target="tpu_custom_call" | custom-call | flops 67108864 | bytes 5242944 | tf_op jit(solution)/shard_map/ragged_dot_general/ragged-dot-none
  478.7 4.0 scatter_fusion
  482.7 0.8 copy-done.2
  484.8 1.3 broadcast_multiply_fusion
  486.0 8.1 copy.17
  494.2 1.5 broadcast_multiply_fusion.1
  495.7 11.3 copy.16
  507.0 31.6 %fusion = f32[4096,256]{1,0:T(8,128)} fusion(f32[512,4096]{1,0:T(8,128)S(1)} %bitcast.60, f32[512,4096]{1,0:T(8,128)} %bitcast.61, f32[512,256]{1,0:T(8,128)S(1)} %copy-done.16, f32[512,256]{1,0:T(8,128)S(1)} %copy-done.15), kind=kOutput, calls=%fused_computation.18 | convolution fusion | flops 12889358336 | bytes 22020096 | tf_op jit(solution)/shard_map/bk,be->ke/dot_general | solution.py:66
  538.6 56.2 %reduce-scatter.6.cloned.1.call-done = f32[128,256]{1,0:T(8,128)} async-done(((f32[2048,256]{1,0:T(8,128)}), f32[128,256]{1,0:T(8,128)}) %reduce-scatter.6.cloned.1.call-update) | async-done | bytes 131088 | tf_op jit(solution)/shard_map/reduce_scatter | solution.py:61
  594.9 645.4 %reduce-scatter.8.cloned.1.call-done = f32[32,256]{1,0:T(8,128)} async-done(((f32[4096,256]{1,0:T(8,128)}), f32[32,256]{1,0:T(8,128)}) %reduce-scatter.8.cloned.1.call-update) | async-done | bytes 32784 | tf_op jit(solution)/shard_map/reduce_scatter | solution.py:65
  (95 shorter events, 5.0 us)
Async XLA Ops:
  7.2 38.8 %copy-start = (f32[1,512,256]{2,1,0:T(8,128)S(1)}, f32[1,512,256]{2,1,0:T(8,128)}, u32[]{:S(2)}) copy-start(f32[1,512,256]{2,1,0:T(8,128)} %param.11) | copy-start | bytes 1572868
  7.2 10.4 copy-start.20
  7.2 333.8 %all-gather.2.cloned.1.call-start = ((), (), s32[]{:S(2)}) async-start(), calls=%async_computation.3 | async-start | bytes 4227072 | tf_op jit(solution)/shard_map/all_gather | solution.py:15
  7.9 530.7 %reduce-scatter.4.cloned.1.call-start = ((), (), s32[]{:S(2)}) async-start(), calls=%async_computation.4 | async-start | bytes 589824 | tf_op jit(solution)/shard_map/reduce_scatter | solution.py:62
  8.0 369.1 %collective-permute-start = (f32[2048,256]{1,0:T(8,128)}, f32[2048,256]{1,0:T(8,128)}, u32[]{:S(2)}, u32[]{:S(2)}) collective-permute-start(f32[2048,256]{1,0:T(8,128)} %bitcast.57), channel_id=1, source_target_pairs={{0,1},{1,2},{2,3},{3,4},{4,5},{5,6},{6,7},{7,0},{8,9},{9,10},{10,1... | collective-permute-start | bytes 6291464 | tf_op jit(solution)/shard_map/ppermute | solution.py:9
  14.1 7.0 copy-start.21
  34.4 7.0 copy-start.19
  34.4 7.1 copy-start.3
  341.0 15.3 %copy-start.8 = (f32[512,256]{1,0:T(8,128)S(1)}, f32[512,256]{1,0:T(8,128)}, u32[]{:S(2)}) copy-start(f32[512,256]{1,0:T(8,128)} %gather_fusion.7) | copy-start | bytes 1572868
  356.4 6.0 copy-start.4
  364.7 2.6 copy-start.10
  371.9 50.5 %collective-permute-start.1 = (f32[2048,256]{1,0:T(8,128)S(1)}, f32[2048,256]{1,0:T(8,128)}, u32[]{:S(2)}, u32[]{:S(2)}) collective-permute-start(f32[2048,256]{1,0:T(8,128)S(1)} %scatter_fusion.1), channel_id=1, source_target_pairs={{0,1},{1,2},{2,3},{3,4},{4,5},{5,6},{6,7},{7,0},{8,9},{9,10},{10,1... | collective-permute-start | bytes 6291464 | tf_op jit(solution)/shard_map/ppermute | solution.py:9
  400.6 2.5 copy-start.5
  403.1 19.3 %copy-start.12 = (f32[512,512]{1,0:T(8,128)}, f32[512,512]{1,0:T(8,128)S(1)}, u32[]{:S(2)}) copy-start(f32[512,512]{1,0:T(8,128)S(1)} %fusion.7) | copy-start | bytes 3145732
  422.4 6.2 copy-start.18
  434.6 49.0 %collective-permute-start.2 = (f32[2048,256]{1,0:T(8,128)}, f32[2048,256]{1,0:T(8,128)}, u32[]{:S(2)}, u32[]{:S(2)}) collective-permute-start(f32[2048,256]{1,0:T(8,128)} %scatter_fusion.2), channel_id=1, source_target_pairs={{0,7},{1,0},{2,1},{3,2},{4,3},{5,4},{6,5},{7,6},{8,15},{9,8},{10,9... | collective-permute-start | bytes 6291464 | tf_op jit(solution)/shard_map/ppermute | solution.py:9
  434.6 5.5 copy-start.9
  434.6 5.5 copy-start.11
  434.6 5.5 copy-start.14
  442.0 19.8 %copy-start.13 = (f32[512,512]{1,0:T(8,128)S(1)}, f32[512,512]{1,0:T(8,128)}, u32[]{:S(2)}) copy-start(f32[512,512]{1,0:T(8,128)} %copy-done.12) | copy-start | bytes 3145732
  442.0 19.8 %copy-start.17 = (f32[512,256]{1,0:T(8,128)S(1)}, f32[512,256]{1,0:T(8,128)}, u32[]{:S(2)}) copy-start(f32[512,256]{1,0:T(8,128)} %gather_fusion.11) | copy-start | bytes 1572868
  482.7 0.8 copy-start.2
  482.7 2.0 copy-start.7
  483.5 111.3 %reduce-scatter.6.cloned.1.call-start = ((), (), s32[]{:S(2)}) async-start(), calls=%async_computation.5 | async-start | bytes 2228224 | tf_op jit(solution)/shard_map/reduce_scatter | solution.py:61
  484.3 756.0 %reduce-scatter.8.cloned.1.call-start = ((), (), s32[]{:S(2)}) async-start(), calls=%async_computation.6 | async-start | bytes 4227072 | tf_op jit(solution)/shard_map/reduce_scatter | solution.py:65
  486.0 8.1 copy-start.6
  495.6 11.4 copy-start.15
  495.6 11.4 copy-start.16
  538.6 701.7 %copy-start.1 = (f32[1,512,256]{2,1,0:T(8,128)S(1)}, f32[1,512,256]{2,1,0:T(8,128)}, u32[]{:S(2)}) copy-start(f32[1,512,256]{2,1,0:T(8,128)} %param.11) | copy-start | bytes 1572868
Sparse Core Ops, SparseCore 0:
  9.7 331.2 all-gather.1
  483.6 36.4 reduce-scatter.3
  525.1 69.6 reduce-scatter.5
  597.8 642.4 reduce-scatter.7
where the time goes:
time: 1260 us; the launch traced here: 1250 us
  waiting for transfers between devices  1010 us (80%)
  Pallas kernels  64.9 us (5%)
  local copies, waits for them, and re-layouts  62.3 us (5%)
  other arithmetic  45.5 us (4%)
  matrix products  45.5 us (4%)
  between operations  14.8 us (1%)
    reduce_scatter x1, waiting for transfers between devices, per_device(): lax.psum_scatter(jnp.einsum('bk,be->ke', spread_all, factor_all, precisio...  645 us
    all_gather x1, waiting for transfers between devices, per_device(): all_rel = lax.all_gather(relations, ('head', 'tail'), axis=0, tiled=True)  292 us
    another operation x4, Pallas kernels  61.4 us
    reduce_scatter x1, waiting for transfers between devices, per_device(): lax.psum_scatter(back_home, 'head', scatter_dimension=0, tiled=True)  56.2 us
    dot_general x1, matrix products, per_device(): jnp.einsum('bk,be->ke', spread_all, factor_all, precision=highest)  31.6 us
  transfers between devices with their start and end apart: 7, of which 4 were waited for; matrix products, arithmetic and copies ran while one was open for 11% of the time, Pallas kernels for 5%

commit v1 on v0

v1 whole, which is shorter than its diff:
```python
import functools

import jax
import jax.numpy as jnp
from jax import lax
from jax.experimental import pallas as pl
from jax.experimental.pallas import tpu as pltpu
from jax.sharding import Mesh, PartitionSpec as P

BF = jnp.bfloat16
F32 = jnp.float32
CHIPS = ("y", "zh", "zl", "x")
HEAD = ("y", "zh", "c")
HEAD_CHIPS = ("y", "zh")
TAIL = ("zl", "x")
SWAP = [(0, 1), (1, 0)]
VMEM_LIMIT = 60 << 20
NN = (((1,), (0,)), ((), ()))
NT = (((1,), (1,)), ((), ()))
TN = (((0,), (0,)), ((), ()))


def split(value):
    high = value.astype(BF)
    return high, (value - high.astype(F32)).astype(BF)


def dot(a, b, dims=NN):
    return lax.dot_general(a, b, dims, preferred_element_type=F32)


def dot3(a, b, dims=NN):
    return dot(a[0], b[0], dims) + dot(a[0], b[1], dims) + dot(a[1], b[0], dims)


def ones_where(mask):
    return jnp.where(mask, 1.0, 0.0).astype(BF)


def call(body, out_shape, scratch, args, smem=0):
    in_specs = [pl.BlockSpec(memory_space=pltpu.SMEM)] * smem
    in_specs += [pl.BlockSpec(memory_space=pltpu.VMEM)] * (len(args) - smem)
    return pl.pallas_call(
        body,
        out_shape=out_shape,
        in_specs=in_specs,
        out_specs=jax.tree.map(lambda _: pl.BlockSpec(memory_space=pltpu.VMEM), out_shape),
        scratch_shapes=scratch,
        compiler_params=pltpu.CompilerParams(vmem_limit_bytes=VMEM_LIMIT),
    )(*args)


def gather_body(cols, head, tail, hv_hi, hv_lo, hvt_hi, hvt_lo, tv, n_hi, n_lo, head_hl, tail_hl):
    width = head.shape[1]
    high, low = split(head[...])
    head_hl[:, :width] = high
    head_hl[:, width:] = low
    high, low = split(tail[...])
    tail_hl[:, :width] = high
    tail_hl[:, width:] = low
    step = 256

    def chunk(i, carry):
        rows = pl.ds(pl.multiple_of(i * step, step), step)
        part = cols[rows, :]

        def pick(column, table):
            count = table.shape[0]
            ids = lax.broadcasted_iota(jnp.int32, (step, count), 1)
            return dot(ones_where(part[:, column : column + 1] == ids), table[...])

        both = pick(0, head_hl)
        high, low = both[:, :width], both[:, width:]
        hv_hi[rows, :] = high.astype(BF)
        hv_lo[rows, :] = low.astype(BF)
        hvt_hi[:, rows] = jnp.transpose(high).astype(BF)
        hvt_lo[:, rows] = jnp.transpose(low).astype(BF)
        both = pick(1, tail_hl)
        tv[rows, :] = both[:, :width] + both[:, width:]
        both = pick(3, tail_hl)
        n_hi[rows, :] = both[:, :width].astype(BF)
        n_lo[rows, :] = both[:, width:].astype(BF)
        return carry

    lax.fori_loop(0, cols.shape[0] // step, chunk, 0)


def rel_id(core, half, j):
    return 2 * j + (core if half == 0 else 1 - core)


def factor_body(core_ref, cols, hv_hi, hv_lo, tv, n_hi, n_lo, own, other, f_hi, f_lo, d_hl, query):
    core = core_ref[0]
    width = own.shape[1]
    rels = cols[:, 2:3]
    query[...] = jnp.zeros_like(query)

    def one(j, carry):
        rows = pl.ds(pl.multiple_of(j * width, width), width)
        total = query[...]
        for half, mats in ((0, own), (1, other)):
            mask = ones_where(rels == rel_id(core, half, j))
            total += dot3((hv_hi[...] * mask, hv_lo[...] * mask), split(mats[rows, :]))
        query[...] = total
        return carry

    lax.fori_loop(0, own.shape[0] // width, one, 0)
    triples = cols.shape[0]
    batch = triples // 2
    for s in range(2):
        rows = slice(s * batch, (s + 1) * batch)
        q = query[rows, :]
        q2 = split(q)
        n2 = (n_hi[rows, :], n_lo[rows, :])
        weights = split(jax.nn.sigmoid(dot3(q2, n2, NT)) * (1.0 / batch))
        vec = tv[rows, :]
        coef = -jax.nn.sigmoid(-jnp.sum(q * vec, axis=1, keepdims=True))
        high, low = split(coef * vec + dot3(weights, n2))
        f_hi[rows, :] = high
        f_lo[rows, :] = low
        high, low = split(coef * q)
        d_hl[rows, :width] = high
        d_hl[rows, width:] = low
        high, low = split(dot3(weights, q2, TN))
        below = slice(triples + s * batch, triples + (s + 1) * batch)
        d_hl[below, :width] = high
        d_hl[below, width:] = low


def rel_body(half, core_ref, rows_ref, hvt_hi, hvt_lo, f_hi, f_lo, out):
    core = core_ref[0]
    width = f_hi.shape[1]
    rels = rows_ref[2:3, :]

    def one(j, carry):
        mask = ones_where(rels == rel_id(core, half, j))
        rows = pl.ds(pl.multiple_of(j * width, width), width)
        out[rows, :] = dot3((hvt_hi[...] * mask, hvt_lo[...] * mask), (f_hi[...], f_lo[...]))
        return carry

    lax.fori_loop(0, out.shape[0] // width, one, 0)


def tail_body(core_ref, rows_ref, d_hl, mine, theirs):
    core = core_ref[0]
    width = mine.shape[1]
    ids = jnp.concatenate([rows_ref[1:2, :], rows_ref[3:4, :]], axis=1)
    step = 512
    block = 128

    for half, out in ((0, mine), (1, theirs)):
        parity = rel_id(core, half, 0)

        def chunk(i, carry, parity=parity, out=out):
            place = i * step + lax.broadcasted_iota(jnp.int32, (step, ids.shape[1]), 0)
            row = (place // block) * (2 * block) + parity * block + place % block
            both = dot(ones_where(row == ids), d_hl[...])
            rows = pl.ds(pl.multiple_of(i * step, step), step)
            out[rows, :] = both[:, :width] + both[:, width:]
            return carry

        lax.fori_loop(0, out.shape[0] // step, chunk, 0)


def head_body(core_ref, cols, rows_ref, f_hi, f_lo, own, other, out, through, th_hl):
    core = core_ref[0]
    width = own.shape[1]
    rels = cols[:, 2:3]
    through[...] = jnp.zeros_like(through)

    def one(j, carry):
        rows = pl.ds(pl.multiple_of(j * width, width), width)
        total = through[...]
        for half, mats in ((0, own), (1, other)):
            mask = ones_where(rels == rel_id(core, half, j))
            total += dot3((f_hi[...] * mask, f_lo[...] * mask), split(mats[rows, :]), NT)
        through[...] = total
        return carry

    lax.fori_loop(0, own.shape[0] // width, one, 0)
    high, low = split(through[...])
    th_hl[:, :width] = high
    th_hl[:, width:] = low
    ids = rows_ref[0:1, :]
    place = lax.broadcasted_iota(jnp.int32, (out.shape[0], ids.shape[1]), 0)
    both = dot(ones_where(place == ids), th_hl[...])
    out[...] = both[:, :width] + both[:, width:]


def shape(*dims, dtype=F32):
    return jax.ShapeDtypeStruct(dims, dtype)


def exchange_sum(value, axes):
    devices = lax.axis_size(axes)
    pieces = value.reshape(devices, value.shape[0] // devices, value.shape[1])
    return jnp.sum(lax.all_to_all(pieces, axes, split_axis=0, concat_axis=0), axis=0)


def per_device(head_emb, tail_emb, relations, head_index, tail_index, rel_index, neg_index):
    width = relations.shape[1]
    heads = head_emb[0]
    tails = tail_emb[0]
    batch = head_index.shape[4]
    triples = 2 * batch
    index = jnp.stack([a[0, 0, :, 0] for a in (head_index, tail_index, rel_index, neg_index)], axis=1)
    behind = lax.axis_size(TAIL)
    next_index = lax.ppermute(index[1], TAIL, [(i, (i - 1) % behind) for i in range(behind)])
    rows = jnp.concatenate([index[0], next_index], axis=1)
    cols = jnp.transpose(rows)
    core = lax.axis_index("c").astype(jnp.int32).reshape(1)

    chips = lax.axis_size(CHIPS)
    spread = jnp.broadcast_to(relations[None], (chips,) + relations.shape)
    own = lax.all_to_all(spread, CHIPS, split_axis=0, concat_axis=0).reshape(-1, width)
    other = lax.ppermute(own, "c", SWAP)

    hv_hi, hv_lo, hvt_hi, hvt_lo, tv, n_hi, n_lo = call(
        gather_body,
        [shape(triples, width, dtype=BF)] * 2
        + [shape(width, triples, dtype=BF)] * 2
        + [shape(triples, width)]
        + [shape(triples, width, dtype=BF)] * 2,
        [pltpu.VMEM((heads.shape[0], 2 * width), BF), pltpu.VMEM((tails.shape[0], 2 * width), BF)],
        (cols, heads, tails),
    )
    f_hi, f_lo, d_hl = call(
        factor_body,
        [shape(triples, width, dtype=BF)] * 2 + [shape(2 * triples, 2 * width, dtype=BF)],
        [pltpu.VMEM((triples, width), F32)],
        (core, cols, hv_hi, hv_lo, tv, n_hi, n_lo, own, other),
        smem=1,
    )
    rel_args = (core, rows, hvt_hi, hvt_lo, f_hi, f_lo)
    rel_other = call(functools.partial(rel_body, 1), shape(*own.shape), [], rel_args, smem=1)
    rel_own = call(functools.partial(rel_body, 0), shape(*own.shape), [], rel_args, smem=1)
    rel_share = exchange_sum(rel_own + lax.ppermute(rel_other, "c", SWAP), CHIPS)

    tail_mine, tail_theirs = call(
        tail_body, [shape(tails.shape[0] // 2, width)] * 2, [], (core, rows, d_hl), smem=1
    )
    tail_share = exchange_sum(tail_mine + lax.ppermute(tail_theirs, "c", SWAP), HEAD_CHIPS)

    head_grad = call(
        head_body,
        shape(*heads.shape),
        [pltpu.VMEM((triples, width), F32), pltpu.VMEM((triples, 2 * width), BF)],
        (core, cols, rows, f_hi, f_lo, own, other),
        smem=1,
    )
    head_share = exchange_sum(head_grad, TAIL)
    return (head_share[None], tail_share[None], rel_share)


def solution(mesh):
    fine = Mesh(mesh.devices.reshape(4, 2, 2, 2, 4), ("y", "zh", "c", "zl", "x"))
    placed = (
        P(HEAD, None, None),
        P(TAIL, None, None),
        P(HEAD + TAIL, None),
        P(HEAD, TAIL, None, None, None),
        P(HEAD, TAIL, None, None, None),
        P(HEAD, TAIL, None, None, None),
        P(HEAD, TAIL, None, None, None),
    )
    return jax.shard_map(
        per_device,
        mesh=fine,
        in_specs=placed,
        out_specs=(P(HEAD, TAIL, None), P(TAIL, HEAD, None), P(HEAD + TAIL, None)),
        check_vma=False,
    )
```

time: 1260 us -> 176 us (0.14)
  waiting for transfers between devices: 1010 us -> 44 us
  local copies, waits for them, and re-layouts: 62.3 us -> 2.9 us
  matrix products: 45.5 us -> 0 us
  blocking collectives: 0 us -> 41.9 us
  other arithmetic: 45.5 us -> 9.65 us
  between operations: 14.8 us -> 0.75 us
    reduce_scatter x3 -> x0, waiting for transfers between devices: 702 us -> none  [the longest x1 645 us: per_device(): lax.psum_scatter(jnp.einsum('bk,be->ke', spread_all, factor_all, precisio...]
    all_gather x1 -> x0, waiting for transfers between devices: 292 us -> none  [per_device(): all_rel = lax.all_gather(relations, ('head', 'tail'), axis=0, tiled=True)]
    pallas_call x0 -> x6, Pallas kernels: none -> 62 us  [call(): pl.pallas_call(body, out_shape=out_shape, in_specs=in_specs, out_specs=ja...]
    another operation x4 -> x0, Pallas kernels: 61.4 us -> none
    dot_general x7 -> x0, matrix products: 45.5 us -> none  [the longest x1 31.6 us: per_device(): jnp.einsum('bk,be->ke', spread_all, factor_all, precision=highest)]
    all_to_all x0 -> x1, blocking collectives: none -> 41.9 us  [per_device(): lax.all_to_all(spread, CHIPS, split_axis=0, concat_axis=0)]
    all_to_all x0 -> x3, waiting for transfers between devices: none -> 40.4 us  [exchange_sum(): lax.all_to_all(pieces, axes, split_axis=0, concat_axis=0)]
    gather x12 -> x0, local copies, waits for them, and re-layouts: 35.5 us -> none  [the longest x2 6.98 us: per_device(): rows_t = tail_index[0, 0, step, 0][order]]
  transfers between devices with their start and end apart: 7 -> 7, of which waited for: 4 -> 4; matrix products, arithmetic and copies ran while one was open for 11% -> 6% of each run, Pallas kernels for 5% -> 22%
where the time goes in v1:
time: 176 us; the launch traced here: 175 us
  Pallas kernels  62 us (35%)
  waiting for transfers between devices  44 us (25%)
  blocking collectives  41.9 us (24%)
  starting transfers between devices  14.2 us (8%)
  other arithmetic  9.65 us (5%)
  local copies, waits for them, and re-layouts  2.9 us (2%)
    pallas_call x6, Pallas kernels, call(): pl.pallas_call(body, out_shape=out_shape, in_specs=in_specs, out_specs=ja...  62 us
    all_to_all x1, blocking collectives, per_device(): lax.all_to_all(spread, CHIPS, split_axis=0, concat_axis=0)  41.9 us
    all_to_all x3, waiting for transfers between devices, exchange_sum(): lax.all_to_all(pieces, axes, split_axis=0, concat_axis=0)  40.4 us
    all_to_all x3, starting transfers between devices, exchange_sum(): lax.all_to_all(pieces, axes, split_axis=0, concat_axis=0)  13.6 us
    ppermute x1, waiting for transfers between devices, per_device(): lax.ppermute(index[1], TAIL, [(i, (i - 1) % behind) for i in range(behind)])  3.63 us
  transfers between devices with their start and end apart: 7, of which 4 were waited for; matrix products, arithmetic and copies ran while one was open for 6% of the time, Pallas kernels for 22%

profile of v1, /device:TPU:0, one launch (start us, length us, event | category | flops | bytes accessed | tf_op | source)
XLA Modules:
  0.0 175.5 jit_solution(8288645552083772025)
XLA Ops:
  0.6 1.0 broadcast_in_dim.12
  1.6 0.0 copy-start.2
  1.6 0.0 copy-start.3
  1.7 0.0 copy-start.4
  1.7 0.0 copy-start.5
  1.7 41.9 %all_to_all.20 = f32[64,32,256]{2,1,0:T(8,128)S(1)} all-to-all(f32[64,32,256]{2,1,0:T(8,128)S(1)} %broadcast_in_dim.12), channel_id=1, replica_groups=mesh['y'=4,'zh'=2,'c'=2,'zl'=2,'x'=4] {'y','zh','zl','x'}, dimensions={0} | all-to-all | bytes 4194304 | tf_op jit(solution)/shard_map/all_to_all | solution.py:215
  43.6 0.0 copy-start
  43.6 0.0 collective-permute-start.1
  43.6 0.0 copy-done.2
  43.6 0.0 copy-done.3
  43.6 0.0 copy-done.4
  43.6 0.0 copy-done.5
  43.7 0.1 collective-permute-start
  43.8 3.6 %collective-permute-done = s32[4,512]{1,0:T(4,128)S(1)} collective-permute-done((s32[4,512]{1,0:T(4,128)S(1)}, s32[4,512]{1,0:T(4,128)S(1)}, u32[]{:S(2)}, u32[]{:S(2)}) %collective-permute-start) | collective-permute-done | bytes 8224 | tf_op jit(solution)/shard_map/ppermute | solution.py:208
  47.4 0.6 pad_add_fusion.1
  48.0 1.1 copy.12.cols
  49.1 9.8 %shard_map.94 = (bf16[1024,256]{1,0:T(8,128)(2,1)}, bf16[1024,256]{1,0:T(8,128)(2,1)}, bf16[256,1024]{1,0:T(8,128)(2,1)}, bf16[256,1024]{1,0:T(8,128)(2,1)}, f32...) custom-call(s32[1024,4]{1,0:T(8,128)} %copy.12.cols, f32[512,256]{1,0:T(8,128)} %bitcast.24, ...), custom_call_target="tpu_custom_call" | custom-call | tf_op jit(solution)/shard_map/pallas_call | solution.py:43
  58.8 0.0 collective-permute-done.1.other
  58.8 0.0 copy-done
  58.8 16.4 %shard_map.95 = (bf16[1024,256]{1,0:T(8,128)(2,1)}, bf16[1024,256]{1,0:T(8,128)(2,1)}, bf16[2048,512]{1,0:T(8,128)(2,1)}) custom-call(s32[1]{0:T(128)} %bitcast.core_ref, s32[1024,4]{1,0:T(8,128)} %copy.12.cols, bf16[1024,256]{1,0:T(8,128)(2,1)} %get-tuple-element.15.hv_hi, bf16[1024,256]{1,0:T(8,128)(2,1)} %get-tuple-element.16.hv_lo, ...), custom_call_target="tpu_custom_call" | custom-call | tf_op jit(solution)/shard_map/pallas_call | solution.py:43
  75.3 7.5 %shard_map.99 = f32[2048,256]{1,0:T(8,128)} custom-call(s32[1]{0:T(128)} %bitcast.core_ref, s32[4,1024]{1,0:T(4,128)} %get-tuple-element.27.rows_ref, bf16[256,1024]{1,0:T(8,128)(2,1)} %get-tuple-element.25.hvt_hi, bf16[256,1024]{1,0:T(8,128)(2,1)} %get-tuple-element.26.hvt_lo, bf16[1024,256]{1,0:T(8,128)(2,1)} %get-tuple-element.20.f_hi, ...), custom_call_target="tpu_custom_call" | custom-call | tf_op jit(solution)/shard_map/pallas_call | solution.py:43
  82.7 0.0 collective-permute-start.3
  82.7 8.0 %shard_map.97 = (f32[1024,256]{1,0:T(8,128)}, f32[1024,256]{1,0:T(8,128)}) custom-call(s32[1]{0:T(128)} %bitcast.core_ref, s32[4,1024]{1,0:T(4,128)} %get-tuple-element.27.rows_ref, bf16[2048,512]{1,0:T(8,128)(2,1)} %get-tuple-element.22.d_hl), custom_call_target="tpu_custom_call" | custom-call | tf_op jit(solution)/shard_map/pallas_call | solution.py:43
  90.7 0.5 collective-permute-start.2
  91.2 13.0 %shard_map.96 = f32[512,256]{1,0:T(8,128)} custom-call(s32[1]{0:T(128)} %bitcast.core_ref, s32[1024,4]{1,0:T(8,128)} %copy.12.cols, s32[4,1024]{1,0:T(4,128)} %get-tuple-element.27.rows_ref, bf16[1024,256]{1,0:T(8,128)(2,1)} %get-tuple-element.20.f_hi, bf16[1024,256]{1,0:T(8,128)(2,1)} %get-tuple-element.21.f_lo, f32[2048,256]{1,0:T(8,128)} %bitcast.21, ...), custom_call_target="tpu_custom_call" | custom-call | tf_op jit(solution)/shard_map/pallas_call | solution.py:43
  104.2 4.0 %all-to-all-start.1 = ((f32[8,64,256]{2,1,0:T(8,128)}), f32[8,64,256]{2,1,0:T(8,128)S(1)}, u32[]{:S(2)}, u32[]{:S(2)}) async-start(f32[8,64,256]{2,1,0:T(8,128)} %bitcast.22), calls=%async_computation.1 | async-start | bytes 1048576 | tf_op jit(solution)/shard_map/all_to_all | solution.py:197
  108.1 0.0 collective-permute-done.2
  108.2 2.7 %add.6 = f32[1024,256]{1,0:T(8,128)} add(f32[1024,256]{1,0:T(8,128)} %get-tuple-element.23, f32[1024,256]{1,0:T(8,128)} %collective-permute-done.2) | non-fusion elementwise | flops 262144 | bytes 3145728 | tf_op jit(solution)/shard_map/add | solution.py:242
  110.8 7.6 %all-to-all-done.1 = f32[8,64,256]{2,1,0:T(8,128)S(1)} async-done(((f32[8,64,256]{2,1,0:T(8,128)}), f32[8,64,256]{2,1,0:T(8,128)S(1)}, u32[]{:S(2)}, u32[]{:S(2)}) %all-to-all-start.1) | async-done | bytes 524320 | tf_op jit(solution)/shard_map/all_to_all | solution.py:197
  118.4 0.0 copy-start.1
  118.4 0.8 copy-done.1
  119.2 4.2 %all-to-all-start.2 = ((f32[8,128,256]{2,1,0:T(8,128)}), f32[8,128,256]{2,1,0:T(8,128)S(1)}, u32[]{:S(2)}, u32[]{:S(2)}) async-start(f32[8,128,256]{2,1,0:T(8,128)} %bitcast.13), calls=%async_computation.2 | async-start | bytes 2097152 | tf_op jit(solution)/shard_map/all_to_all | solution.py:197
  123.4 7.5 %shard_map.98 = f32[2048,256]{1,0:T(8,128)} custom-call(s32[1]{0:T(128)} %bitcast.core_ref, s32[4,1024]{1,0:T(4,128)} %get-tuple-element.27.rows_ref, bf16[256,1024]{1,0:T(8,128)(2,1)} %get-tuple-element.25.hvt_hi, bf16[256,1024]{1,0:T(8,128)(2,1)} %get-tuple-element.26.hvt_lo, bf16[1024,256]{1,0:T(8,128)(2,1)} %get-tuple-element.20.f_hi, ...), custom_call_target="tpu_custom_call" | custom-call | tf_op jit(solution)/shard_map/pallas_call | solution.py:43
  130.9 0.0 collective-permute-done.3
  130.9 3.2 %add.7 = f32[2048,256]{1,0:T(8,128)} add(f32[2048,256]{1,0:T(8,128)} %shard_map.98, f32[2048,256]{1,0:T(8,128)S(1)} %collective-permute-done.3) | non-fusion elementwise | flops 524288 | bytes 6291456 | tf_op jit(solution)/shard_map/add | solution.py:237
  134.0 5.0 %all-to-all-done.2 = f32[8,128,256]{2,1,0:T(8,128)S(1)} async-done(((f32[8,128,256]{2,1,0:T(8,128)}), f32[8,128,256]{2,1,0:T(8,128)S(1)}, u32[]{:S(2)}, u32[]{:S(2)}) %all-to-all-start.2) | async-done | bytes 1048608 | tf_op jit(solution)/shard_map/all_to_all | solution.py:197
  139.0 5.4 %all-to-all-start.3 = ((f32[64,32,256]{2,1,0:T(8,128)}), f32[64,32,256]{2,1,0:T(8,128)S(1)}, u32[]{:S(2)}, u32[]{:S(2)}) async-start(f32[64,32,256]{2,1,0:T(8,128)} %bitcast.15), calls=%async_computation.3 | async-start | bytes 4194304 | tf_op jit(solution)/shard_map/all_to_all | solution.py:197
  144.5 1.7 reduce_sum.27
  146.2 0.7 reduce_sum.28
  146.9 27.8 %all-to-all-done.3 = f32[64,32,256]{2,1,0:T(8,128)S(1)} async-done(((f32[64,32,256]{2,1,0:T(8,128)}), f32[64,32,256]{2,1,0:T(8,128)S(1)}, u32[]{:S(2)}, u32[]{:S(2)}) %all-to-all-start.3) | async-done | bytes 2097184 | tf_op jit(solution)/shard_map/all_to_all | solution.py:197
  174.7 0.8 reduce_sum.29
  (2 shorter events, 0.0 us)
Async XLA Ops:
  1.6 42.0 %copy-start.2 = (s32[1,1,2,1,512]{4,3,2,1,0:T(1,128)S(1)}, s32[1,1,2,1,512]{4,3,2,1,0:T(1,128)}, u32[]{:S(2)}) copy-start(s32[1,1,2,1,512]{4,3,2,1,0:T(1,128)} %param.13) | copy-start | bytes 12292
  1.6 42.0 %copy-start.3 = (s32[1,1,2,1,512]{4,3,2,1,0:T(1,128)S(1)}, s32[1,1,2,1,512]{4,3,2,1,0:T(1,128)}, u32[]{:S(2)}) copy-start(s32[1,1,2,1,512]{4,3,2,1,0:T(1,128)} %param.12) | copy-start | bytes 12292
  1.7 42.0 %copy-start.4 = (s32[1,1,2,1,512]{4,3,2,1,0:T(1,128)S(1)}, s32[1,1,2,1,512]{4,3,2,1,0:T(1,128)}, u32[]{:S(2)}) copy-start(s32[1,1,2,1,512]{4,3,2,1,0:T(1,128)} %param.11) | copy-start | bytes 12292
  1.7 42.0 %copy-start.5 = (s32[1,1,2,1,512]{4,3,2,1,0:T(1,128)S(1)}, s32[1,1,2,1,512]{4,3,2,1,0:T(1,128)}, u32[]{:S(2)}) copy-start(s32[1,1,2,1,512]{4,3,2,1,0:T(1,128)} %param.10) | copy-start | bytes 12292
  43.6 15.2 %copy-start = (f32[64,32,256]{2,1,0:T(8,128)}, f32[64,32,256]{2,1,0:T(8,128)S(1)}, u32[]{:S(2)}) copy-start(f32[64,32,256]{2,1,0:T(8,128)S(1)} %all_to_all.20) | copy-start | bytes 6291460
  43.6 15.2 %collective-permute-start.1 = (f32[2048,256]{1,0:T(8,128)S(1)}, f32[2048,256]{1,0:T(8,128)}, u32[]{:S(2)}, u32[]{:S(2)}) collective-permute-start(f32[2048,256]{1,0:T(8,128)S(1)} %bitcast.19), channel_id=1, source_target_pairs={{0,8},{8,0},{1,9},{9,1},{2,10},{10,2},{3,11},{11,3},{4,12},{12,4},... | collective-permute-start | bytes 6291464 | tf_op jit(solution)/shard_map/ppermute | solution.py:216
  43.7 3.7 %collective-permute-start = (s32[4,512]{1,0:T(4,128)S(1)}, s32[4,512]{1,0:T(4,128)S(1)}, u32[]{:S(2)}, u32[]{:S(2)}) collective-permute-start(s32[4,512]{1,0:T(4,128)S(1)} %get-tuple-element.30), channel_id=1, source_target_pairs={{0,7},{1,0},{2,1},{3,2},{4,3},{5,4},{6,5},{7,6},{8,15},{9,8},{10,9... | collective-permute-start | bytes 24584 | tf_op jit(solution)/shard_map/ppermute | solution.py:208
  82.7 48.2 %collective-permute-start.3 = (f32[2048,256]{1,0:T(8,128)}, f32[2048,256]{1,0:T(8,128)S(1)}, u32[]{:S(2)}, u32[]{:S(2)}) collective-permute-start(f32[2048,256]{1,0:T(8,128)} %shard_map.99), channel_id=1, source_target_pairs={{0,8},{8,0},{1,9},{9,1},{2,10},{10,2},{3,11},{11,3},{4,12},{12,4},... | collective-permute-start | bytes 6291464 | tf_op jit(solution)/shard_map/ppermute | solution.py:237
  90.7 17.5 %collective-permute-start.2 = (f32[1024,256]{1,0:T(8,128)}, f32[1024,256]{1,0:T(8,128)}, u32[]{:S(2)}, u32[]{:S(2)}) collective-permute-start(f32[1024,256]{1,0:T(8,128)} %get-tuple-element.24), channel_id=1, source_target_pairs={{0,8},{8,0},{1,9},{9,1},{2,10},{10,2},{3,11},{11,3},{4,12},{12,4},... | collective-permute-start | bytes 3145736 | tf_op jit(solution)/shard_map/ppermute | solution.py:242
  104.2 14.2 %all-to-all-start.1 = ((f32[8,64,256]{2,1,0:T(8,128)}), f32[8,64,256]{2,1,0:T(8,128)S(1)}, u32[]{:S(2)}, u32[]{:S(2)}) async-start(f32[8,64,256]{2,1,0:T(8,128)} %bitcast.22), calls=%async_computation.1 | async-start | bytes 1048576 | tf_op jit(solution)/shard_map/all_to_all | solution.py:197
  118.4 0.8 copy-start.1
  119.2 19.8 %all-to-all-start.2 = ((f32[8,128,256]{2,1,0:T(8,128)}), f32[8,128,256]{2,1,0:T(8,128)S(1)}, u32[]{:S(2)}, u32[]{:S(2)}) async-start(f32[8,128,256]{2,1,0:T(8,128)} %bitcast.13), calls=%async_computation.2 | async-start | bytes 2097152 | tf_op jit(solution)/shard_map/all_to_all | solution.py:197
  139.0 35.7 %all-to-all-start.3 = ((f32[64,32,256]{2,1,0:T(8,128)}), f32[64,32,256]{2,1,0:T(8,128)S(1)}, u32[]{:S(2)}, u32[]{:S(2)}) async-start(f32[64,32,256]{2,1,0:T(8,128)} %bitcast.15), calls=%async_computation.3 | async-start | bytes 4194304 | tf_op jit(solution)/shard_map/all_to_all | solution.py:197

commit v2 on v1

--- a/solution.py
+++ b/solution.py
@@ -89,22 +89,29 @@
     return 2 * j + (core if half == 0 else 1 - core)
 
 
-def factor_body(core_ref, cols, hv_hi, hv_lo, tv, n_hi, n_lo, own, other, f_hi, f_lo, d_hl, query):
+def add_query(half, core_ref, cols, hv_hi, hv_lo, mats, query):
     core = core_ref[0]
-    width = own.shape[1]
+    width = mats.shape[1]
     rels = cols[:, 2:3]
-    query[...] = jnp.zeros_like(query)
 
     def one(j, carry):
         rows = pl.ds(pl.multiple_of(j * width, width), width)
-        total = query[...]
-        for half, mats in ((0, own), (1, other)):
-            mask = ones_where(rels == rel_id(core, half, j))
-            total += dot3((hv_hi[...] * mask, hv_lo[...] * mask), split(mats[rows, :]))
-        query[...] = total
+        mask = ones_where(rels == rel_id(core, half, j))
+        query[...] += dot3((hv_hi[...] * mask, hv_lo[...] * mask), split(mats[rows, :]))
         return carry
 
-    lax.fori_loop(0, own.shape[0] // width, one, 0)
+    lax.fori_loop(0, mats.shape[0] // width, one, 0)
+
+
+def query_body(half, core_ref, cols, hv_hi, hv_lo, mats, query):
+    query[...] = jnp.zeros_like(query)
+    add_query(half, core_ref, cols, hv_hi, hv_lo, mats, query)
+
+
+def factor_body(core_ref, cols, hv_hi, hv_lo, tv, n_hi, n_lo, partial, other, f_hi, f_lo, d_hl, query):
+    width = other.shape[1]
+    query[...] = partial[...]
+    add_query(1, core_ref, cols, hv_hi, hv_lo, other, query)
     triples = cols.shape[0]
     batch = triples // 2
     for s in range(2):
@@ -197,6 +204,17 @@
     return jnp.sum(lax.all_to_all(pieces, axes, split_axis=0, concat_axis=0), axis=0)
 
 
+def permute_sum(value, axes):
+    devices = lax.axis_size(axes)
+    me = lax.axis_index(axes)
+    pieces = value.reshape(devices, value.shape[0] // devices, value.shape[1])
+    total = lax.dynamic_index_in_dim(pieces, me, 0, keepdims=False)
+    for k in range(1, devices):
+        piece = lax.dynamic_index_in_dim(pieces, me ^ k, 0, keepdims=False)
+        total += lax.ppermute(piece, axes, [(i, i ^ k) for i in range(devices)])
+    return total
+
+
 def per_device(head_emb, tail_emb, relations, head_index, tail_index, rel_index, neg_index):
     width = relations.shape[1]
     heads = head_emb[0]
@@ -206,16 +224,15 @@
     index = jnp.stack([a[0, 0, :, 0] for a in (head_index, tail_index, rel_index, neg_index)], axis=1)
     behind = lax.axis_size(TAIL)
     next_index = lax.ppermute(index[1], TAIL, [(i, (i - 1) % behind) for i in range(behind)])
+    core = lax.axis_index("c").astype(jnp.int32).reshape(1)
+
+    chips = lax.axis_size(CHIPS)
+    spread = jnp.broadcast_to(relations[None], (chips,) + relations.shape)
+    spread, next_index = lax.optimization_barrier((spread, next_index))
     rows = jnp.concatenate([index[0], next_index], axis=1)
     cols = jnp.transpose(rows)
-    core = lax.axis_index("c").astype(jnp.int32).reshape(1)
-
-    chips = lax.axis_size(CHIPS)
-    spread = jnp.broadcast_to(relations[None], (chips,) + relations.shape)
     own = lax.all_to_all(spread, CHIPS, split_axis=0, concat_axis=0).reshape(-1, width)
-    other = lax.ppermute(own, "c", SWAP)
-
-    hv_hi, hv_lo, hvt_hi, hvt_lo, tv, n_hi, n_lo = call(
+    gathered = call(
         gather_body,
         [shape(triples, width, dtype=BF)] * 2
         + [shape(width, triples, dtype=BF)] * 2
@@ -224,22 +241,37 @@
         [pltpu.VMEM((heads.shape[0], 2 * width), BF), pltpu.VMEM((tails.shape[0], 2 * width), BF)],
         (cols, heads, tails),
     )
+    (hv_hi, hv_lo, hvt_hi, hvt_lo, tv, n_hi, n_lo), own = lax.optimization_barrier((gathered, own))
+    other = lax.ppermute(own, "c", SWAP)
+    partial = call(
+        functools.partial(query_body, 0), shape(triples, width), [], (core, cols, hv_hi, hv_lo, own), smem=1
+    )
     f_hi, f_lo, d_hl = call(
         factor_body,
         [shape(triples, width, dtype=BF)] * 2 + [shape(2 * triples, 2 * width, dtype=BF)],
         [pltpu.VMEM((triples, width), F32)],
-        (core, cols, hv_hi, hv_lo, tv, n_hi, n_lo, own, other),
+        (core, cols, hv_hi, hv_lo, tv, n_hi, n_lo, partial, other),
         smem=1,
     )
-    rel_args = (core, rows, hvt_hi, hvt_lo, f_hi, f_lo)
-    rel_other = call(functools.partial(rel_body, 1), shape(*own.shape), [], rel_args, smem=1)
-    rel_own = call(functools.partial(rel_body, 0), shape(*own.shape), [], rel_args, smem=1)
-    rel_share = exchange_sum(rel_own + lax.ppermute(rel_other, "c", SWAP), CHIPS)
 
     tail_mine, tail_theirs = call(
         tail_body, [shape(tails.shape[0] // 2, width)] * 2, [], (core, rows, d_hl), smem=1
     )
-    tail_share = exchange_sum(tail_mine + lax.ppermute(tail_theirs, "c", SWAP), HEAD_CHIPS)
+    tail_came = lax.ppermute(tail_theirs, "c", SWAP)
+    f_hi, tail_mine = lax.optimization_barrier((f_hi, tail_mine))
+
+    def rel_part(half):
+        args = (core, rows, hvt_hi, hvt_lo, f_hi, f_lo)
+        return call(functools.partial(rel_body, half), shape(*own.shape), [], args, smem=1)
+
+    rel_other = rel_part(1)
+    rel_came = lax.ppermute(rel_other, "c", SWAP)
+    f_hi, tail_sum, rel_other = lax.optimization_barrier((f_hi, tail_mine + tail_came, rel_other))
+    tail_share = exchange_sum(tail_sum, HEAD_CHIPS)
+
+    rel_own = rel_part(0)
+    f_hi, rel_sum = lax.optimization_barrier((f_hi, rel_own + rel_came))
+    rel_share = exchange_sum(rel_sum, CHIPS)
 
     head_grad = call(
         head_body,
@@ -248,7 +280,7 @@
         (core, cols, rows, f_hi, f_lo, own, other),
         smem=1,
     )
-    head_share = exchange_sum(head_grad, TAIL)
+    head_share = permute_sum(head_grad, TAIL)
     return (head_share[None], tail_share[None], rel_share)
 
 

time: 176 us -> 160 us (0.909)
  blocking collectives: 41.9 us -> 0 us
  starting transfers between devices: 14.2 us -> 35.2 us
  Pallas kernels: 62 us -> 66.9 us
  local copies, waits for them, and re-layouts: 2.9 us -> 6.42 us
  waiting for transfers between devices: 44 us -> 41.1 us
    all_to_all x1 -> x0, blocking collectives: 41.9 us -> none  [per_device(): lax.all_to_all(spread, CHIPS, split_axis=0, concat_axis=0)]
    all_to_all x3 -> x2, waiting for transfers between devices: 40.4 us -> 6.4 us  [exchange_sum(): lax.all_to_all(pieces, axes, split_axis=0, concat_axis=0)]
    all_to_all x0 -> x1, waiting for transfers between devices: none -> 17.7 us  [per_device(): lax.all_to_all(spread, CHIPS, split_axis=0, concat_axis=0)]
    ppermute x2 -> x9, waiting for transfers between devices: 0.01 us -> 15.6 us  [the longest x7 10.3 us: permute_sum(): total += lax.ppermute(piece, axes, [(i, i ^ k) for i in range(devices)])]
    all_to_all x0 -> x1, starting transfers between devices: none -> 11.4 us  [per_device(): lax.all_to_all(spread, CHIPS, split_axis=0, concat_axis=0)]
    ppermute x2 -> x9, starting transfers between devices: 0.51 us -> 10.6 us  [the longest x7 10.1 us: permute_sum(): total += lax.ppermute(piece, axes, [(i, i ^ k) for i in range(devices)])]
    pallas_call x6 -> x7, Pallas kernels: 62 us -> 66.9 us  [call(): pl.pallas_call(body, out_shape=out_shape, in_specs=in_specs, out_specs=ja...]
    all_to_all x3 -> x2, starting transfers between devices: 13.6 us -> 8.91 us  [exchange_sum(): lax.all_to_all(pieces, axes, split_axis=0, concat_axis=0)]
  transfers between devices with their start and end apart: 7 -> 14, of which waited for: 4 -> 9; matrix products, arithmetic and copies ran while one was open for 6% -> 6% of each run, Pallas kernels for 22% -> 24%
where the time goes in v2:
time: 160 us; the launch traced here: 159 us
  Pallas kernels  66.9 us (42%)
  waiting for transfers between devices  41.1 us (26%)
  starting transfers between devices  35.2 us (22%)
  other arithmetic  8.92 us (6%)
  local copies, waits for them, and re-layouts  6.42 us (4%)
    pallas_call x7, Pallas kernels, call(): pl.pallas_call(body, out_shape=out_shape, in_specs=in_specs, out_specs=ja...  66.9 us
    all_to_all x1, waiting for transfers between devices, per_device(): lax.all_to_all(spread, CHIPS, split_axis=0, concat_axis=0)  17.7 us
    all_to_all x1, starting transfers between devices, per_device(): lax.all_to_all(spread, CHIPS, split_axis=0, concat_axis=0)  11.4 us
    ppermute x7, waiting for transfers between devices, permute_sum(): total += lax.ppermute(piece, axes, [(i, i ^ k) for i in range(devices)])  10.3 us
    ppermute x7, starting transfers between devices, permute_sum(): total += lax.ppermute(piece, axes, [(i, i ^ k) for i in range(devices)])  10.1 us
    all_to_all x2, starting transfers between devices, exchange_sum(): lax.all_to_all(pieces, axes, split_axis=0, concat_axis=0)  8.91 us
    all_to_all x2, waiting for transfers between devices, exchange_sum(): lax.all_to_all(pieces, axes, split_axis=0, concat_axis=0)  6.4 us
    ppermute x1, waiting for transfers between devices, per_device(): tail_came = lax.ppermute(tail_theirs, 'c', SWAP)  5.36 us
  transfers between devices with their start and end apart: 14, of which 9 were waited for; matrix products, arithmetic and copies ran while one was open for 6% of the time, Pallas kernels for 24%

profile of v2, /device:TPU:0, one launch (start us, length us, event | category | flops | bytes accessed | tf_op | source)
XLA Modules:
  0.0 159.3 jit_solution(15521653666608240076)
XLA Ops:
  0.6 0.8 pad_add_fusion
  1.4 4.3 %collective-permute-start = (s32[4,512]{1,0:T(4,128)S(1)}, s32[4,512]{1,0:T(4,128)S(1)}, u32[]{:S(2)}, u32[]{:S(2)}) collective-permute-start(s32[4,512]{1,0:T(4,128)S(1)} %get-tuple-element.69), channel_id=1, source_target_pairs={{0,7},{1,0},{2,1},{3,2},{4,3},{5,4},{6,5},{7,6},{8,15},{9,8},{10,9... | collective-permute-start | bytes 24584 | tf_op jit(solution)/shard_map/ppermute | solution.py:226
  5.7 1.4 collective-permute-done
  7.0 2.4 %broadcast_in_dim.12 = f32[64,32,256]{2,1,0:T(8,128)} broadcast(f32[32,256]{1,0:T(8,128)} %param.9), dimensions={1,2} | broadcast | bytes 2129920 | tf_op jit(solution)/shard_map/broadcast_in_dim | solution.py:230
  9.4 11.4 %all-to-all-start = ((f32[64,32,256]{2,1,0:T(8,128)}), f32[64,32,256]{2,1,0:T(8,128)S(1)}, u32[]{:S(2)}, u32[]{:S(2)}) async-start(f32[64,32,256]{2,1,0:T(8,128)} %broadcast_in_dim.12), calls=%async_computation | async-start | bytes 4194304 | tf_op jit(solution)/shard_map/all_to_all | solution.py:234
  20.8 0.6 pad_add_fusion.1
  21.4 1.0 copy.13.cols
  22.5 9.7 %shard_map.94 = (bf16[1024,256]{1,0:T(8,128)(2,1)}, bf16[1024,256]{1,0:T(8,128)(2,1)}, bf16[256,1024]{1,0:T(8,128)(2,1)}, bf16[256,1024]{1,0:T(8,128)(2,1)}, f32...) custom-call(s32[1024,4]{1,0:T(8,128)} %copy.13.cols, f32[512,256]{1,0:T(8,128)} %bitcast.56, ...), custom_call_target="tpu_custom_call" | custom-call | tf_op jit(solution)/shard_map/pallas_call | solution.py:43
  32.2 17.7 %all-to-all-done = f32[64,32,256]{2,1,0:T(8,128)S(1)} async-done(((f32[64,32,256]{2,1,0:T(8,128)}), f32[64,32,256]{2,1,0:T(8,128)S(1)}, u32[]{:S(2)}, u32[]{:S(2)}) %all-to-all-start) | async-done | bytes 2097184 | tf_op jit(solution)/shard_map/all_to_all | solution.py:234
  49.9 0.0 copy-start
  49.9 0.0 collective-permute-start.1
  49.9 1.3 copy-done
  51.2 8.4 %shard_map.95.partial = f32[1024,256]{1,0:T(8,128)} custom-call(s32[1]{0:T(128)} %bitcast.core_ref, s32[1024,4]{1,0:T(8,128)} %copy.13.cols, bf16[1024,256]{1,0:T(8,128)(2,1)} %get-tuple-element.40.hv_hi, bf16[1024,256]{1,0:T(8,128)(2,1)} %get-tuple-element.41.hv_lo, f32[2048,256]{1,0:T(8,128)} %bitcast.51), custom_call_target="tpu_custom_call" | custom-call | tf_op jit(solution)/shard_map/pallas_call | solution.py:43
  59.6 0.0 collective-permute-done.1.other
  59.6 12.7 %shard_map.96 = (bf16[1024,256]{1,0:T(8,128)(2,1)}, bf16[1024,256]{1,0:T(8,128)(2,1)}, bf16[2048,512]{1,0:T(8,128)(2,1)}) custom-call(s32[1]{0:T(128)} %bitcast.core_ref, s32[1024,4]{1,0:T(8,128)} %copy.13.cols, bf16[1024,256]{1,0:T(8,128)(2,1)} %get-tuple-element.40.hv_hi, bf16[1024,256]{1,0:T(8,128)(2,1)} %get-tuple-element.41.hv_lo, ...), custom_call_target="tpu_custom_call" | custom-call | tf_op jit(solution)/shard_map/pallas_call | solution.py:43
  72.3 8.1 %shard_map.97 = (f32[1024,256]{1,0:T(8,128)}, f32[1024,256]{1,0:T(8,128)}) custom-call(s32[1]{0:T(128)} %bitcast.core_ref, s32[4,1024]{1,0:T(4,128)} %get-tuple-element.66.rows_ref, bf16[2048,512]{1,0:T(8,128)(2,1)} %get-tuple-element.47.d_hl), custom_call_target="tpu_custom_call" | custom-call | tf_op jit(solution)/shard_map/pallas_call | solution.py:43
  80.3 7.6 %shard_map.98 = f32[2048,256]{1,0:T(8,128)} custom-call(s32[1]{0:T(128)} %bitcast.core_ref, s32[4,1024]{1,0:T(4,128)} %get-tuple-element.66.rows_ref, bf16[256,1024]{1,0:T(8,128)(2,1)} %get-tuple-element.52.hvt_hi, bf16[256,1024]{1,0:T(8,128)(2,1)} %get-tuple-element.53.hvt_lo, bf16[1024,256]{1,0:T(8,128)(2,1)} %get-tuple-element.56.f_hi, ...), custom_call_target="tpu_custom_call" | custom-call | tf_op jit(solution)/shard_map/pallas_call | solution.py:43
  87.9 0.0 collective-permute-start.3
  87.9 0.5 collective-permute-start.2
  88.4 5.4 %collective-permute-done.2 = f32[1024,256]{1,0:T(8,128)S(1)} collective-permute-done((f32[1024,256]{1,0:T(8,128)}, f32[1024,256]{1,0:T(8,128)S(1)}, u32[]{:S(2)}, u32[]{:S(2)}) %collective-permute-start.2) | collective-permute-done | bytes 1048608 | tf_op jit(solution)/shard_map/ppermute | solution.py:260
  93.8 0.0 copy-done.1
  93.8 1.2 add.55
  95.0 3.6 %all-to-all-start.1 = ((f32[8,128,256]{2,1,0:T(8,128)}), f32[8,128,256]{2,1,0:T(8,128)S(1)}, u32[]{:S(2)}, u32[]{:S(2)}) async-start(f32[8,128,256]{2,1,0:T(8,128)} %bitcast.21), calls=%async_computation.1 | async-start | bytes 2097152 | tf_op jit(solution)/shard_map/all_to_all | solution.py:204
  98.6 7.5 %shard_map.99 = f32[2048,256]{1,0:T(8,128)} custom-call(s32[1]{0:T(128)} %bitcast.core_ref, s32[4,1024]{1,0:T(4,128)} %get-tuple-element.66.rows_ref, bf16[256,1024]{1,0:T(8,128)(2,1)} %get-tuple-element.52.hvt_hi, bf16[256,1024]{1,0:T(8,128)(2,1)} %get-tuple-element.53.hvt_lo, bf16[1024,256]{1,0:T(8,128)(2,1)} %get-tuple-element.56.f_hi, ...), custom_call_target="tpu_custom_call" | custom-call | tf_op jit(solution)/shard_map/pallas_call | solution.py:43
  106.1 0.0 collective-permute-done.3
  106.1 3.2 %add.56 = f32[2048,256]{1,0:T(8,128)} add(f32[2048,256]{1,0:T(8,128)} %shard_map.99, f32[2048,256]{1,0:T(8,128)S(1)} %collective-permute-done.3) | non-fusion elementwise | flops 524288 | bytes 6291456 | tf_op jit(solution)/shard_map/add | solution.py:273
  109.3 6.4 %all-to-all-done.1 = f32[8,128,256]{2,1,0:T(8,128)S(1)} async-done(((f32[8,128,256]{2,1,0:T(8,128)}), f32[8,128,256]{2,1,0:T(8,128)S(1)}, u32[]{:S(2)}, u32[]{:S(2)}) %all-to-all-start.1) | async-done | bytes 1048608 | tf_op jit(solution)/shard_map/all_to_all | solution.py:204
  115.7 5.3 %all-to-all-start.2 = ((f32[64,32,256]{2,1,0:T(8,128)}), f32[64,32,256]{2,1,0:T(8,128)S(1)}, u32[]{:S(2)}, u32[]{:S(2)}) async-start(f32[64,32,256]{2,1,0:T(8,128)} %bitcast.23), calls=%async_computation.2 | async-start | bytes 4194304 | tf_op jit(solution)/shard_map/all_to_all | solution.py:204
  121.1 13.0 %shard_map.100 = f32[512,256]{1,0:T(8,128)} custom-call(s32[1]{0:T(128)} %bitcast.core_ref, s32[1024,4]{1,0:T(8,128)} %copy.13.cols, s32[4,1024]{1,0:T(4,128)} %get-tuple-element.66.rows_ref, bf16[1024,256]{1,0:T(8,128)(2,1)} %get-tuple-element.56.f_hi, bf16[1024,256]{1,0:T(8,128)(2,1)} %get-tuple-element.54.f_lo, f32[2048,256]{1,0:T(8,128)} %bitcast.52, ...), custom_call_target="tpu_custom_call" | custom-call | tf_op jit(solution)/shard_map/pallas_call | solution.py:43
  134.1 1.7 %dynamic-slice_bitcast_fusion.6 = (f32[64,256]{1,0:T(8,128)S(1)}, f32[64,256]{1,0:T(8,128)S(1)}, f32[64,256]{1,0:T(8,128)}, f32[64,256]{1,0:T(8,128)S(1)}, f32[6...) fusion(f32[8,64,256]{2,1,0:T(8,128)} %bitcast.54, s32[]{:T(128)S(6)} %select_n.26, ...), kind=kLoop, calls=%fused_computation.14 | loop fusion | bytes 917532 | tf_op jit(solution)/shard_map/jit(dynamic_index_in_dim)/squeeze | solution.py:213
  135.8 1.6 collective-permute-start.4
  137.4 3.0 %collective-permute-start.10 = (f32[64,256]{1,0:T(8,128)S(1)}, f32[64,256]{1,0:T(8,128)S(1)}, u32[]{:S(2)}, u32[]{:S(2)}) collective-permute-start(f32[64,256]{1,0:T(8,128)S(1)} %get-tuple-element.60), channel_id=1, source_target_pairs={{0,7},{1,6},{2,5},{3,4},{4,3},{5,2},{6,1},{7,0},{8,15},{9,14},{10,... | collective-permute-start | bytes 196616 | tf_op jit(solution)/shard_map/ppermute | solution.py:214
  140.3 0.6 collective-permute-start.9
  140.9 2.3 %collective-permute-start.8 = (f32[64,256]{1,0:T(8,128)S(1)}, f32[64,256]{1,0:T(8,128)}, u32[]{:S(2)}, u32[]{:S(2)}) collective-permute-start(f32[64,256]{1,0:T(8,128)S(1)} %get-tuple-element.62), channel_id=1, source_target_pairs={{0,5},{1,4},{2,7},{3,6},{4,1},{5,0},{6,3},{7,2},{8,13},{9,12},{10,... | collective-permute-start | bytes 196616 | tf_op jit(solution)/shard_map/ppermute | solution.py:214
  143.3 0.6 collective-permute-start.7
  143.8 3.8 %collective-permute-done.4 = f32[64,256]{1,0:T(8,128)S(1)} collective-permute-done((f32[64,256]{1,0:T(8,128)S(1)}, f32[64,256]{1,0:T(8,128)S(1)}, u32[]{:S(2)}, u32[]{:S(2)}) %collective-permute-start.4) | collective-permute-done | bytes 65568 | tf_op jit(solution)/shard_map/ppermute | solution.py:214
  147.6 2.1 %collective-permute-start.6 = (f32[64,256]{1,0:T(8,128)S(1)}, f32[64,256]{1,0:T(8,128)}, u32[]{:S(2)}, u32[]{:S(2)}) collective-permute-start(f32[64,256]{1,0:T(8,128)S(1)} %get-tuple-element.64), channel_id=1, source_target_pairs={{0,3},{1,2},{2,1},{3,0},{4,7},{5,6},{6,5},{7,4},{8,11},{9,10},{10,... | collective-permute-start | bytes 196616 | tf_op jit(solution)/shard_map/ppermute | solution.py:214
  149.7 1.3 collective-permute-done.10
  151.0 0.0 collective-permute-start.5
  151.0 0.7 reduce_sum.18
  151.7 0.2 collective-permute-done.9
  151.9 0.0 collective-permute-done.8
  151.9 1.4 collective-permute-done.7
  153.3 0.0 collective-permute-done.6
  153.3 3.6 %collective-permute-done.5 = f32[64,256]{1,0:T(8,128)} collective-permute-done((f32[64,256]{1,0:T(8,128)S(1)}, f32[64,256]{1,0:T(8,128)}, u32[]{:S(2)}, u32[]{:S(2)}) %collective-permute-start.5) | collective-permute-done | bytes 65568 | tf_op jit(solution)/shard_map/ppermute | solution.py:214
  156.9 1.7 %fusion.6 = f32[1,64,256]{2,1,0:T(8,128)} fusion(f32[64,256]{1,0:T(8,128)S(1)} %collective-permute-done.10, f32[64,256]{1,0:T(8,128)} %collective-permute-done.9, f32[64,256]{1,0:T(8,128)} %collective-permute-done.8, f32[64,256]{1,0:T(8,128)} %collective-permute-done.7, f32[64,256]{1,0:T(8,128)} %collective-permute-done.6, ...), kind=kLoop, calls=%fused_computation.7 | loop fusion | flops 114688 | bytes 589828 | tf_op jit(solution)/shard_map/broadcast_in_dim | solution.py:284
  158.6 0.0 all-to-all-done.2
  158.6 0.8 reduce_sum.19
  (2 shorter events, 0.0 us)
Async XLA Ops:
  1.4 5.6 %collective-permute-start = (s32[4,512]{1,0:T(4,128)S(1)}, s32[4,512]{1,0:T(4,128)S(1)}, u32[]{:S(2)}, u32[]{:S(2)}) collective-permute-start(s32[4,512]{1,0:T(4,128)S(1)} %get-tuple-element.69), channel_id=1, source_target_pairs={{0,7},{1,0},{2,1},{3,2},{4,3},{5,4},{6,5},{7,6},{8,15},{9,8},{10,9... | collective-permute-start | bytes 24584 | tf_op jit(solution)/shard_map/ppermute | solution.py:226
  9.4 40.5 %all-to-all-start = ((f32[64,32,256]{2,1,0:T(8,128)}), f32[64,32,256]{2,1,0:T(8,128)S(1)}, u32[]{:S(2)}, u32[]{:S(2)}) async-start(f32[64,32,256]{2,1,0:T(8,128)} %broadcast_in_dim.12), calls=%async_computation | async-start | bytes 4194304 | tf_op jit(solution)/shard_map/all_to_all | solution.py:234
  49.9 1.3 copy-start
  49.9 9.7 %collective-permute-start.1 = (f32[2048,256]{1,0:T(8,128)S(1)}, f32[2048,256]{1,0:T(8,128)}, u32[]{:S(2)}, u32[]{:S(2)}) collective-permute-start(f32[2048,256]{1,0:T(8,128)S(1)} %bitcast.50), channel_id=1, source_target_pairs={{0,8},{8,0},{1,9},{9,1},{2,10},{10,2},{3,11},{11,3},{4,12},{12,4},... | collective-permute-start | bytes 6291464 | tf_op jit(solution)/shard_map/ppermute | solution.py:245
  80.3 13.5 %copy-start.1 = (f32[1024,256]{1,0:T(8,128)S(1)}, f32[1024,256]{1,0:T(8,128)}, u32[]{:S(2)}) copy-start(f32[1024,256]{1,0:T(8,128)} %get-tuple-element.50) | copy-start | bytes 3145732
  87.9 18.1 %collective-permute-start.3 = (f32[2048,256]{1,0:T(8,128)}, f32[2048,256]{1,0:T(8,128)S(1)}, u32[]{:S(2)}, u32[]{:S(2)}) collective-permute-start(f32[2048,256]{1,0:T(8,128)} %shard_map.98), channel_id=1, source_target_pairs={{0,8},{8,0},{1,9},{9,1},{2,10},{10,2},{3,11},{11,3},{4,12},{12,4},... | collective-permute-start | bytes 6291464 | tf_op jit(solution)/shard_map/ppermute | solution.py:268
  87.9 5.9 %collective-permute-start.2 = (f32[1024,256]{1,0:T(8,128)}, f32[1024,256]{1,0:T(8,128)S(1)}, u32[]{:S(2)}, u32[]{:S(2)}) collective-permute-start(f32[1024,256]{1,0:T(8,128)} %get-tuple-element.51), channel_id=1, source_target_pairs={{0,8},{8,0},{1,9},{9,1},{2,10},{10,2},{3,11},{11,3},{4,12},{12,4},... | collective-permute-start | bytes 3145736 | tf_op jit(solution)/shard_map/ppermute | solution.py:260
  95.0 20.7 %all-to-all-start.1 = ((f32[8,128,256]{2,1,0:T(8,128)}), f32[8,128,256]{2,1,0:T(8,128)S(1)}, u32[]{:S(2)}, u32[]{:S(2)}) async-start(f32[8,128,256]{2,1,0:T(8,128)} %bitcast.21), calls=%async_computation.1 | async-start | bytes 2097152 | tf_op jit(solution)/shard_map/all_to_all | solution.py:204
  115.7 42.9 %all-to-all-start.2 = ((f32[64,32,256]{2,1,0:T(8,128)}), f32[64,32,256]{2,1,0:T(8,128)S(1)}, u32[]{:S(2)}, u32[]{:S(2)}) async-start(f32[64,32,256]{2,1,0:T(8,128)} %bitcast.23), calls=%async_computation.2 | async-start | bytes 4194304 | tf_op jit(solution)/shard_map/all_to_all | solution.py:204
  135.8 11.8 %collective-permute-start.4 = (f32[64,256]{1,0:T(8,128)S(1)}, f32[64,256]{1,0:T(8,128)S(1)}, u32[]{:S(2)}, u32[]{:S(2)}) collective-permute-start(f32[64,256]{1,0:T(8,128)S(1)} %get-tuple-element.59), channel_id=1, source_target_pairs={{0,1},{1,0},{2,3},{3,2},{4,5},{5,4},{6,7},{7,6},{8,9},{9,8},{10,11... | collective-permute-start | bytes 196616 | tf_op jit(solution)/shard_map/ppermute | solution.py:214
  137.4 13.6 %collective-permute-start.10 = (f32[64,256]{1,0:T(8,128)S(1)}, f32[64,256]{1,0:T(8,128)S(1)}, u32[]{:S(2)}, u32[]{:S(2)}) collective-permute-start(f32[64,256]{1,0:T(8,128)S(1)} %get-tuple-element.60), channel_id=1, source_target_pairs={{0,7},{1,6},{2,5},{3,4},{4,3},{5,2},{6,1},{7,0},{8,15},{9,14},{10,... | collective-permute-start | bytes 196616 | tf_op jit(solution)/shard_map/ppermute | solution.py:214
  140.3 11.6 %collective-permute-start.9 = (f32[64,256]{1,0:T(8,128)}, f32[64,256]{1,0:T(8,128)}, u32[]{:S(2)}, u32[]{:S(2)}) collective-permute-start(f32[64,256]{1,0:T(8,128)} %get-tuple-element.61), channel_id=1, source_target_pairs={{0,6},{1,7},{2,4},{3,5},{4,2},{5,3},{6,0},{7,1},{8,14},{9,15},{10,... | collective-permute-start | bytes 196616 | tf_op jit(solution)/shard_map/ppermute | solution.py:214
  140.9 11.0 %collective-permute-start.8 = (f32[64,256]{1,0:T(8,128)S(1)}, f32[64,256]{1,0:T(8,128)}, u32[]{:S(2)}, u32[]{:S(2)}) collective-permute-start(f32[64,256]{1,0:T(8,128)S(1)} %get-tuple-element.62), channel_id=1, source_target_pairs={{0,5},{1,4},{2,7},{3,6},{4,1},{5,0},{6,3},{7,2},{8,13},{9,12},{10,... | collective-permute-start | bytes 196616 | tf_op jit(solution)/shard_map/ppermute | solution.py:214
  143.3 10.0 %collective-permute-start.7 = (f32[64,256]{1,0:T(8,128)S(1)}, f32[64,256]{1,0:T(8,128)}, u32[]{:S(2)}, u32[]{:S(2)}) collective-permute-start(f32[64,256]{1,0:T(8,128)S(1)} %get-tuple-element.63), channel_id=1, source_target_pairs={{0,4},{1,5},{2,6},{3,7},{4,0},{5,1},{6,2},{7,3},{8,12},{9,13},{10,... | collective-permute-start | bytes 196616 | tf_op jit(solution)/shard_map/ppermute | solution.py:214
  147.6 5.7 %collective-permute-start.6 = (f32[64,256]{1,0:T(8,128)S(1)}, f32[64,256]{1,0:T(8,128)}, u32[]{:S(2)}, u32[]{:S(2)}) collective-permute-start(f32[64,256]{1,0:T(8,128)S(1)} %get-tuple-element.64), channel_id=1, source_target_pairs={{0,3},{1,2},{2,1},{3,0},{4,7},{5,6},{6,5},{7,4},{8,11},{9,10},{10,... | collective-permute-start | bytes 196616 | tf_op jit(solution)/shard_map/ppermute | solution.py:214
  151.0 5.9 %collective-permute-start.5 = (f32[64,256]{1,0:T(8,128)S(1)}, f32[64,256]{1,0:T(8,128)}, u32[]{:S(2)}, u32[]{:S(2)}) collective-permute-start(f32[64,256]{1,0:T(8,128)S(1)} %get-tuple-element.65), channel_id=1, source_target_pairs={{0,2},{1,3},{2,0},{3,1},{4,6},{5,7},{6,4},{7,5},{8,10},{9,11},{10,... | collective-permute-start | bytes 196616 | tf_op jit(solution)/shard_map/ppermute | solution.py:214

commit v3 on v1

v3 whole, which is shorter than its diff:
```python
import functools

import jax
import jax.numpy as jnp
from jax import lax
from jax.experimental import pallas as pl
from jax.experimental.pallas import tpu as pltpu
from jax.sharding import Mesh, PartitionSpec as P

BF = jnp.bfloat16
F32 = jnp.float32
CHIPS = ("y", "zh", "zl", "x")
HEAD = ("y", "zh", "c")
HEAD_CHIPS = ("y", "zh")
TAIL = ("zl", "x")
SWAP = [(0, 1), (1, 0)]
NN = (((1,), (0,)), ((), ()))
NT = (((1,), (1,)), ((), ()))
TN = (((0,), (0,)), ((), ()))


def split(value):
    high = value.astype(BF)
    return high, (value - high.astype(F32)).astype(BF)


def dot(a, b, dims=NN):
    return lax.dot_general(a, b, dims, preferred_element_type=F32)


def dot3(a, b, dims=NN):
    return dot(a[0], b[0], dims) + dot(a[0], b[1], dims) + dot(a[1], b[0], dims)


def ones_where(mask):
    return jnp.where(mask, 1.0, 0.0).astype(BF)


def call(body, out_shape, scratch, args, smem=0, hbm=0, vmem=20):
    spaces = [pltpu.SMEM] * smem + [pltpu.HBM] * hbm
    spaces += [pltpu.VMEM] * (len(args) - smem - hbm)
    if hbm:
        fetched = [pltpu.with_memory_space_constraint(a, pltpu.HBM) for a in args[smem : smem + hbm]]
        args = tuple(args[:smem]) + tuple(fetched) + tuple(args[smem + hbm :])
        scratch = [pltpu.SemaphoreType.DMA((hbm,))] + [pltpu.VMEM(a.shape, a.dtype) for a in fetched] + scratch
    return pl.pallas_call(
        body,
        out_shape=out_shape,
        in_specs=[pl.BlockSpec(memory_space=space) for space in spaces],
        out_specs=jax.tree.map(lambda _: pl.BlockSpec(memory_space=pltpu.VMEM), out_shape),
        scratch_shapes=scratch,
        compiler_params=pltpu.CompilerParams(vmem_limit_bytes=vmem << 20),
    )(*args)


def fetch(sources, places, sems):
    copies = [pltpu.make_async_copy(a, b, sems.at[i]) for i, (a, b) in enumerate(zip(sources, places))]
    for copy in copies:
        copy.start()
    return copies


def slot_of(rel, core):
    return (rel >> 1) + jnp.where((rel & 1) == core, 0, 8)


def gather_body(
    core_ref, cols, rows_ref, head, tail,
    hv_hi, hv_lo, hvt_hi, hvt_lo, tv, n_hi, n_lo, rank_col, meta, head_hl, tail_hl, head_col,
):
    core = core_ref[0]
    width = head.shape[1]
    triples = cols.shape[0]
    high, low = split(head[...])
    head_hl[:, :width] = high
    head_hl[:, width:] = low
    high, low = split(tail[...])
    tail_hl[:, :width] = high
    tail_hl[:, width:] = low
    step = 256
    chunks = triples // step
    lanes = lax.broadcasted_iota(jnp.int32, (1, triples), 1)
    sublanes = lax.broadcasted_iota(jnp.int32, (step, 1), 0)
    key_row = slot_of(rows_ref[2:3, :], core) * triples + lanes
    rank_row = jnp.zeros((1, triples), F32)
    for i in range(chunks):
        part = slice(i * step, (i + 1) * step)
        key_col = slot_of(cols[part, 2:3], core) * triples + sublanes + i * step
        rank_row += jnp.sum(jnp.where(key_col < key_row, 1.0, 0.0), axis=0, keepdims=True)
        rank = jnp.sum(jnp.where(key_row < key_col, 1.0, 0.0), axis=1, keepdims=True)
        rank_col[part, :] = rank.astype(jnp.int32)
    rank_row = rank_row.astype(jnp.int32)
    head_row = jnp.zeros((1, triples), F32)
    head_ids = rows_ref[0:1, :].astype(F32)
    for i in range(chunks):
        part = slice(i * step, (i + 1) * step)
        here = rank_col[part, :] == lanes
        head_row += jnp.sum(jnp.where(here, cols[part, 0:1].astype(F32), 0.0), axis=0, keepdims=True)
        here = sublanes + i * step == rank_row
        head_col[part, :] = jnp.sum(jnp.where(here, head_ids, 0.0), axis=1, keepdims=True).astype(jnp.int32)
    meta[0:1, :] = rank_row
    meta[1:2, :] = head_row.astype(jnp.int32)

    def chunk(i, carry):
        rows = pl.ds(pl.multiple_of(i * step, step), step)
        part = cols[rows, :]

        def pick(index, table):
            ids = lax.broadcasted_iota(jnp.int32, (step, table.shape[0]), 1)
            return dot(ones_where(index == ids), table[...])

        both = pick(head_col[rows, :], head_hl)
        high, low = both[:, :width], both[:, width:]
        hv_hi[rows, :] = high.astype(BF)
        hv_lo[rows, :] = low.astype(BF)
        hvt_hi[:, rows] = jnp.transpose(high).astype(BF)
        hvt_lo[:, rows] = jnp.transpose(low).astype(BF)
        both = pick(part[:, 1:2], tail_hl)
        tv[rows, :] = both[:, :width] + both[:, width:]
        both = pick(part[:, 3:4], tail_hl)
        n_hi[rows, :] = both[:, :width].astype(BF)
        n_lo[rows, :] = both[:, width:].astype(BF)
        return carry

    lax.fori_loop(0, chunks, chunk, 0)


def split_rels(own, other, r_hi, r_lo, copies=None):
    count = own.shape[0]
    for half, mats in enumerate((own, other)):
        if copies:
            copies[half].wait()
        high, low = split(mats[...])
        r_hi[half * count : (half + 1) * count, :] = high
        r_lo[half * count : (half + 1) * count, :] = low


def visits(segs, tile, total, one, low=0, high=None):
    group = 4

    def some(g, carry):
        for k in range(group):
            v = g * group + k
            first = segs[0, v]
            one(pl.multiple_of(jnp.minimum(first // tile, total // tile - 1) * tile, tile), first, segs[1, v], segs[2, v])
        return carry

    lax.fori_loop(low, segs.shape[1] // group if high is None else high, some, 0)


def by_relation(segs, a_hi, a_lo, r_hi, r_lo, out, dims):
    width = r_hi.shape[1]
    tile = 128
    out[...] = jnp.zeros_like(out)

    def one(start, first, last, slot):
        rows = pl.ds(start, tile)
        place = start + lax.broadcasted_iota(jnp.int32, (tile, 1), 0)
        mask = ones_where((place >= first) & (place < last))
        high = a_hi[rows, :] * mask
        both = jnp.concatenate([high, a_lo[rows, :] * mask], axis=0)
        mat = pl.ds(pl.multiple_of(slot * width, width), width)
        main = dot(both, r_hi[mat, :], dims)
        out[rows, :] += main[:tile] + main[tile:] + dot(high, r_lo[mat, :], dims)

    visits(segs, tile, out.shape[0], one)


def factor_body(
    segs, own_at, other_at, hv_hi_at, hv_lo_at, rank_at, tv_at, n_hi_at, n_lo_at, meta,
    f_hi, f_lo, d_hl, sems, own, other, hv_hi, hv_lo, rank_col, tv, n_hi, n_lo, r_hi, r_lo, query, pair, f_hl,
):
    width = own.shape[1]
    triples = tv.shape[0]
    batch = triples // 2
    copies = fetch(
        (own_at, other_at, hv_hi_at, hv_lo_at, rank_at, tv_at, n_hi_at, n_lo_at),
        (own, other, hv_hi, hv_lo, rank_col, tv, n_hi, n_lo),
        sems,
    )
    split_rels(own, other, r_hi, r_lo, copies)
    for copy in copies[2:]:
        copy.wait()
    by_relation(segs, hv_hi, hv_lo, r_hi, r_lo, query, NN)
    high, low = split(query[...])
    pair[:, :width] = high
    pair[:, width:] = low
    for s in range(2):
        rows = slice(s * batch, (s + 1) * batch)
        ids = lax.broadcasted_iota(jnp.int32, (batch, triples), 1)
        both = dot(ones_where(rank_col[rows, :] == ids), pair[...])
        high, low = both[:, :width], both[:, width:]
        q = high + low
        q2 = (high.astype(BF), low.astype(BF))
        n2 = (n_hi[rows, :], n_lo[rows, :])
        weights = split(jax.nn.sigmoid(dot3(q2, n2, NT)) * (1.0 / batch))
        vec = tv[rows, :]
        coef = -jax.nn.sigmoid(-jnp.sum(q * vec, axis=1, keepdims=True))
        high, low = split(coef * vec + dot3(weights, n2))
        f_hl[rows, :width] = high
        f_hl[rows, width:] = low
        high, low = split(coef * q)
        d_hl[rows, :width] = high
        d_hl[rows, width:] = low
        high, low = split(dot3(weights, q2, TN))
        below = slice(triples + s * batch, triples + (s + 1) * batch)
        d_hl[below, :width] = high
        d_hl[below, width:] = low
    rank_row = meta[0:1, :]
    for s in range(2):
        rows = slice(s * batch, (s + 1) * batch)
        ids = lax.broadcasted_iota(jnp.int32, (batch, triples), 0) + s * batch
        both = dot(ones_where(ids == rank_row), f_hl[...])
        f_hi[rows, :] = both[:, :width].astype(BF)
        f_lo[rows, :] = both[:, width:].astype(BF)


def rel_body(half, segs, bounds, hvt_hi, hvt_lo, f_hi, f_lo, out):
    width = f_hi.shape[1]
    tile = 256
    count = out.shape[0] // width
    out[...] = jnp.zeros_like(out)

    def one(start, first, last, slot):
        part = pl.ds(start, tile)
        mine = (slot < count) if half == 0 else (slot >= count)
        last = jnp.where(mine, last, first)
        slot = jnp.minimum(slot, count - 1) if half == 0 else jnp.maximum(slot - count, 0)
        place = start + lax.broadcasted_iota(jnp.int32, (1, tile), 1)
        mask = ones_where((place >= first) & (place < last))
        high = hvt_hi[:, part] * mask
        both = jnp.concatenate([high, hvt_lo[:, part] * mask], axis=0)
        main = dot(both, f_hi[part, :])
        rows = pl.ds(pl.multiple_of(slot * width, width), width)
        out[rows, :] += main[:width] + main[width:] + dot(high, f_lo[part, :])

    visits(segs, tile, f_hi.shape[0], one, bounds[half, 0], bounds[half, 1])


def own_body(
    by_column, bounds, by_row, hvt_hi_at, hvt_lo_at, f_hi_at, f_lo_at, own_at, other_at, meta,
    rel_own, head_grad, sems, hvt_hi, hvt_lo, f_hi, f_lo, own, other, r_hi, r_lo, through, th_hl,
):
    copies = fetch(
        (hvt_hi_at, hvt_lo_at, f_hi_at, f_lo_at, own_at, other_at),
        (hvt_hi, hvt_lo, f_hi, f_lo, own, other),
        sems,
    )
    for copy in copies[:4]:
        copy.wait()
    rel_body(0, by_column, bounds, hvt_hi, hvt_lo, f_hi, f_lo, rel_own)
    split_rels(own, other, r_hi, r_lo, copies[4:])
    head_part(by_row, meta, f_hi, f_lo, head_grad, r_hi, r_lo, through, th_hl)


def tail_body(half, core_ref, rows_ref, d_hl, out):
    core = core_ref[0]
    width = out.shape[1]
    ids = jnp.concatenate([rows_ref[1:2, :], rows_ref[3:4, :]], axis=1)
    step = 512
    block = 128
    parity = core if half == 0 else 1 - core

    def chunk(i, carry):
        place = i * step + lax.broadcasted_iota(jnp.int32, (step, ids.shape[1]), 0)
        row = (place >> 7) * (2 * block) + parity * block + (place & (block - 1))
        both = dot(ones_where(row == ids), d_hl[...])
        rows = pl.ds(pl.multiple_of(i * step, step), step)
        out[rows, :] = both[:, :width] + both[:, width:]
        return carry

    lax.fori_loop(0, out.shape[0] // step, chunk, 0)


def head_part(segs, meta, f_hi, f_lo, out, r_hi, r_lo, through, th_hl):
    width = out.shape[1]
    by_relation(segs, f_hi, f_lo, r_hi, r_lo, through, NT)
    high, low = split(through[...])
    th_hl[:, :width] = high
    th_hl[:, width:] = low
    ids = meta[1:2, :]
    place = lax.broadcasted_iota(jnp.int32, (out.shape[0], ids.shape[1]), 0)
    both = dot(ones_where(place == ids), th_hl[...])
    out[...] = both[:, :width] + both[:, width:]


def shape(*dims, dtype=F32):
    return jax.ShapeDtypeStruct(dims, dtype)


def after(value, earlier):
    return lax.optimization_barrier((value, earlier))[0]


def exchange_sum(value, axes):
    devices = lax.axis_size(axes)
    pieces = value.reshape(devices, value.shape[0] // devices, value.shape[1])
    return jnp.sum(lax.all_to_all(pieces, axes, split_axis=0, concat_axis=0), axis=0)


def segments(starts, tile, total):
    edges = jnp.concatenate([jnp.arange(0, total, tile, dtype=jnp.int32), starts[1:]])
    count = edges.shape[0]
    place = jnp.arange(count)
    ahead = (edges[None, :] < edges[:, None]) | (
        (edges[None, :] == edges[:, None]) & (place[None, :] < place[:, None])
    )
    rank = jnp.sum(ahead.astype(jnp.int32), axis=1)
    padded = -(-count // 4) * 4
    at = jnp.arange(padded + 1)
    ordered = jnp.sum(jnp.where(rank[None, :] == at[:, None], edges[None, :], 0), axis=1)
    ordered = jnp.where(at < count, ordered, total)
    first = ordered[:padded]
    slot = jnp.sum((starts[None, 1:] <= first[:, None]).astype(jnp.int32), axis=1)
    return jnp.stack([first, ordered[1:], slot]).astype(jnp.int32)


def permute_sum(value, axis):
    devices = lax.axis_size(axis)
    me = lax.axis_index(axis)
    total = lax.dynamic_index_in_dim(value, me, 0, keepdims=False)
    for k in range(1, devices):
        piece = lax.dynamic_index_in_dim(value, me ^ k, 0, keepdims=False)
        total += lax.ppermute(piece, axis, [(i, i ^ k) for i in range(devices)])
    return total


def per_device(head_emb, tail_emb, relations, head_index, tail_index, rel_index, neg_index):
    width = relations.shape[1]
    heads = head_emb[0]
    tails = tail_emb[0]
    batch = head_index.shape[4]
    triples = 2 * batch
    index = jnp.stack([a[0, 0, :, 0] for a in (head_index, tail_index, rel_index, neg_index)], axis=1)
    behind = lax.axis_size(TAIL)
    next_index = lax.ppermute(index[1], TAIL, [(i, (i - 1) % behind) for i in range(behind)])
    core = lax.axis_index("c").astype(jnp.int32).reshape(1)

    chips = lax.axis_size(CHIPS)
    spread = jnp.broadcast_to(relations[None], (chips,) + relations.shape)
    spread, next_index = lax.optimization_barrier((spread, next_index))
    rows = jnp.concatenate([index[0], next_index], axis=1)
    cols = jnp.transpose(rows)
    own = lax.all_to_all(spread, CHIPS, split_axis=0, concat_axis=0).reshape(-1, width)
    slots = slot_of(rows[2], core)
    rel_count = chips * relations.shape[0] * 2 // width
    starts = jnp.sum((slots[None, :] < jnp.arange(rel_count)[:, None]).astype(jnp.int32), axis=1)
    by_row = segments(starts, 128, triples)
    by_column = segments(starts, 256, triples)
    middle = jnp.sum((by_column[0] < starts[rel_count // 2]).astype(jnp.int32))
    groups = jnp.full_like(middle, by_column.shape[1] // 4)
    zero = jnp.zeros_like(middle)
    bounds = jnp.stack([jnp.stack([zero, (middle + 3) // 4]), jnp.stack([middle // 4, groups])])
    wide = shape(triples, width, dtype=BF)
    high = shape(width, triples, dtype=BF)
    gathered = call(
        gather_body,
        [wide, wide, high, high, shape(triples, width), wide, wide]
        + [shape(triples, 1, dtype=jnp.int32), shape(2, triples, dtype=jnp.int32)],
        [
            pltpu.VMEM((heads.shape[0], 2 * width), BF),
            pltpu.VMEM((tails.shape[0], 2 * width), BF),
            pltpu.VMEM((triples, 1), jnp.int32),
        ],
        (core, cols, rows, heads, tails),
        smem=1,
    )
    hv_hi, hv_lo, hvt_hi, hvt_lo, tv, n_hi, n_lo, rank_col, meta = gathered
    meta, own, by_row, by_column, bounds = lax.optimization_barrier((meta, own, by_row, by_column, bounds))
    other = lax.ppermute(own, "c", SWAP)
    rel_scratch = [pltpu.VMEM((2 * own.shape[0], width), BF)] * 2
    f_hi, f_lo, d_hl = call(
        factor_body,
        [wide, wide, shape(2 * triples, 2 * width, dtype=BF)],
        rel_scratch + [pltpu.VMEM((triples, width), F32)] + [pltpu.VMEM((triples, 2 * width), BF)] * 2,
        (by_row, own, other, hv_hi, hv_lo, rank_col, tv, n_hi, n_lo, meta),
        smem=1,
        hbm=8,
        vmem=32,
    )

    def tail_part(half, core):
        out = shape(tails.shape[0] // 2, width)
        return call(functools.partial(tail_body, half), out, [], (core, rows, d_hl), smem=1)

    tail_theirs = tail_part(1, core)
    tail_came = lax.ppermute(tail_theirs, "c", SWAP)
    tail_mine = tail_part(0, after(core, tail_theirs))
    tail_sum = tail_mine + tail_came
    bounds = after(bounds, tail_sum)
    tail_share = exchange_sum(tail_sum, HEAD_CHIPS)

    rel_other = call(
        functools.partial(rel_body, 1),
        shape(*own.shape),
        [],
        (by_column, bounds, hvt_hi, hvt_lo, f_hi, f_lo),
        smem=2,
    )
    rel_came = lax.ppermute(rel_other, "c", SWAP)
    bounds = after(bounds, rel_other)
    rel_own, head_grad = call(
        own_body,
        [shape(*own.shape), shape(*heads.shape)],
        rel_scratch + [pltpu.VMEM((triples, width), F32), pltpu.VMEM((triples, 2 * width), BF)],
        (by_column, bounds, by_row, hvt_hi, hvt_lo, f_hi, f_lo, own, other, meta),
        smem=3,
        hbm=6,
        vmem=32,
    )
    rel_share = exchange_sum(rel_own + rel_came, CHIPS)
    pieces = head_grad.reshape(lax.axis_size("zl"), lax.axis_size("x"), -1, width)
    pieces = permute_sum(jnp.swapaxes(pieces, 0, 1), "x")
    head_share = permute_sum(after(pieces, tail_share), "zl")
    return (head_share[None], tail_share[None], rel_share)


def solution(mesh):
    fine = Mesh(mesh.devices.reshape(4, 2, 2, 2, 4), ("y", "zh", "c", "zl", "x"))
    placed = (
        P(HEAD, None, None),
        P(TAIL, None, None),
        P(HEAD + TAIL, None),
        P(HEAD, TAIL, None, None, None),
        P(HEAD, TAIL, None, None, None),
        P(HEAD, TAIL, None, None, None),
        P(HEAD, TAIL, None, None, None),
    )
    return jax.shard_map(
        per_device,
        mesh=fine,
        in_specs=placed,
        out_specs=(P(HEAD, TAIL, None), P(TAIL, HEAD, None), P(HEAD + TAIL, None)),
        check_vma=False,
    )
```

time: 176 us -> 144 us (0.82)
  blocking collectives: 41.9 us -> 0 us
  Pallas kernels: 62 us -> 37.7 us
  starting transfers between devices: 14.2 us -> 31 us
  local copies, waits for them, and re-layouts: 2.9 us -> 13.5 us
  between operations: 0.75 us -> 4.09 us
  waiting for transfers between devices: 44 us -> 45.8 us
    all_to_all x1 -> x0, blocking collectives: 41.9 us -> none  [per_device(): lax.all_to_all(spread, CHIPS, split_axis=0, concat_axis=0)]
    all_to_all x3 -> x2, waiting for transfers between devices: 40.4 us -> 5.52 us  [exchange_sum(): lax.all_to_all(pieces, axes, split_axis=0, concat_axis=0)]
    ppermute x2 -> x6, waiting for transfers between devices: 0.01 us -> 29.2 us  [the longest x4 29.2 us: permute_sum(): total += lax.ppermute(piece, axis, [(i, i ^ k) for i in range(devices)])]
    pallas_call x6, Pallas kernels: 62 us -> 37.7 us  [call(): pl.pallas_call(body, out_shape=out_shape, in_specs=[pl.BlockSpec(memory_s...]
    all_to_all x0 -> x1, starting transfers between devices: none -> 11.8 us  [per_device(): lax.all_to_all(spread, CHIPS, split_axis=0, concat_axis=0)]
    unnamed x12 -> x30, local copies, waits for them, and re-layouts: 0.84 us -> 9.35 us
    ppermute x2 -> x6, starting transfers between devices: 0.51 us -> 6.22 us  [the longest x4 5.64 us: permute_sum(): total += lax.ppermute(piece, axis, [(i, i ^ k) for i in range(devices)])]
    all_to_all x0 -> x1, waiting for transfers between devices: none -> 5.36 us  [per_device(): lax.all_to_all(spread, CHIPS, split_axis=0, concat_axis=0)]
  transfers between devices with their start and end apart: 7 -> 11, of which waited for: 4 -> 6; matrix products, arithmetic and copies ran while one was open for 6% -> 7% of each run, Pallas kernels for 22% -> 14%
where the time goes in v3:
time: 144 us; the launch traced here: 143 us
  waiting for transfers between devices  45.8 us (32%)
  Pallas kernels  37.7 us (26%)
  starting transfers between devices  31 us (22%)
  local copies, waits for them, and re-layouts  13.5 us (9%)
  other arithmetic  11 us (8%)
  between operations  4.09 us (3%)
    pallas_call x6, Pallas kernels, call(): pl.pallas_call(body, out_shape=out_shape, in_specs=[pl.BlockSpec(memory_s...  37.7 us
    ppermute x4, waiting for transfers between devices, permute_sum(): total += lax.ppermute(piece, axis, [(i, i ^ k) for i in range(devices)])  29.2 us
    all_to_all x1, starting transfers between devices, per_device(): lax.all_to_all(spread, CHIPS, split_axis=0, concat_axis=0)  11.8 us
    unnamed x30, local copies, waits for them, and re-layouts  9.35 us
    all_to_all x2, starting transfers between devices, exchange_sum(): lax.all_to_all(pieces, axes, split_axis=0, concat_axis=0)  8.66 us
    ppermute x4, starting transfers between devices, permute_sum(): total += lax.ppermute(piece, axis, [(i, i ^ k) for i in range(devices)])  5.64 us
    all_to_all x2, waiting for transfers between devices, exchange_sum(): lax.all_to_all(pieces, axes, split_axis=0, concat_axis=0)  5.52 us
    all_to_all x1, waiting for transfers between devices, per_device(): lax.all_to_all(spread, CHIPS, split_axis=0, concat_axis=0)  5.36 us
  transfers between devices with their start and end apart: 11, of which 6 were waited for; matrix products, arithmetic and copies ran while one was open for 7% of the time, Pallas kernels for 14%

profile of v3, /device:TPU:0, one launch (start us, length us, event | category | flops | bytes accessed | tf_op | source)
XLA Modules:
  0.0 143.0 jit_solution(8025583282821554018)
XLA Ops:
  0.6 0.8 pad_add_fusion.1
  1.4 4.3 %collective-permute-start = (s32[4,512]{1,0:T(4,128)S(1)}, s32[4,512]{1,0:T(4,128)S(1)}, u32[]{:S(2)}, u32[]{:S(2)}) collective-permute-start(s32[4,512]{1,0:T(4,128)S(1)} %get-tuple-element.59), channel_id=1, source_target_pairs={{0,7},{1,0},{2,1},{3,2},{4,3},{5,4},{6,5},{7,6},{8,15},{9,8},{10,9... | collective-permute-start | bytes 24584 | tf_op jit(solution)/shard_map/ppermute | solution.py:336
  5.7 1.4 collective-permute-done
  7.0 2.3 %broadcast_in_dim.41 = f32[64,32,256]{2,1,0:T(8,128)} broadcast(f32[32,256]{1,0:T(8,128)} %param.9), dimensions={1,2} | broadcast | bytes 2129920 | tf_op jit(solution)/shard_map/broadcast_in_dim | solution.py:340
  9.4 11.8 %all-to-all-start = ((f32[64,32,256]{2,1,0:T(8,128)}), f32[64,32,256]{2,1,0:T(8,128)}, u32[]{:S(2)}, u32[]{:S(2)}) async-start(f32[64,32,256]{2,1,0:T(8,128)} %broadcast_in_dim.41), calls=%async_computation | async-start | bytes 4194304 | tf_op jit(solution)/shard_map/all_to_all | solution.py:344
  21.2 0.1 convert_reduce_fusion
  21.5 0.2 convert_reduce_fusion.1
  21.7 0.1 select_reduce_fusion
  21.8 0.6 slice.38
  22.4 1.3 fusion.9
  26.9 1.0 copy.11.cols
  28.0 1.0 copy-done.5
  29.0 1.0 copy-done.12
  30.0 9.0 %shard_map.94 = (bf16[1024,256]{1,0:T(8,128)(2,1)S(1)}, bf16[1024,256]{1,0:T(8,128)(2,1)S(1)}, bf16[256,1024]{1,0:T(8,128)(2,1)S(1)}, bf16[256,1024]{1,0:T(8,128...) custom-call(s32[1]{0:T(128)} %bitcast.core_ref, ...), custom_call_target="tpu_custom_call" | custom-call | tf_op jit(solution)/shard_map/pallas_call | solution.py:46
  39.0 1.0 copy-done.6
  40.0 0.8 copy-done.7
  40.8 0.8 copy-done.8
  41.6 0.8 copy-done.9
  42.4 0.8 copy-done.10
  43.2 0.8 copy-done.11
  44.2 0.2 convert_reduce_fusion.2
  44.3 0.1 select_reduce_fusion.1
  44.6 0.1 convert_reduce_fusion.3
  44.7 5.4 %all-to-all-done = f32[64,32,256]{2,1,0:T(8,128)} async-done(((f32[64,32,256]{2,1,0:T(8,128)}), f32[64,32,256]{2,1,0:T(8,128)}, u32[]{:S(2)}, u32[]{:S(2)}) %all-to-all-start) | async-done | bytes 2097184 | tf_op jit(solution)/shard_map/all_to_all | solution.py:344
  50.1 4.4 %collective-permute-done.1.other_at = f32[2048,256]{1,0:T(8,128)S(1)} collective-permute-done((f32[2048,256]{1,0:T(8,128)}, f32[2048,256]{1,0:T(8,128)S(1)}, u32[]{:S(2)}, u32[]{:S(2)}) %collective-permute-start.1) | collective-permute-done | bytes 2097184 | tf_op jit(solution)/shard_map/ppermute | solution.py:370
  54.5 1.3 copy-done.13
  55.8 11.4 %shard_map.95 = (bf16[1024,256]{1,0:T(8,128)(2,1)S(1)}, bf16[1024,256]{1,0:T(8,128)(2,1)S(1)}, bf16[2048,512]{1,0:T(8,128)(2,1)S(1)}) custom-call(s32[3,24]{1,0:T(4,128)S(1)} %pad_add_fusion.2.segs.by_row, f32[2048,256]{1,0:T(8,128)} %bitcast.10.own_at, f32[2048,256]{1,0:T(8,128)} %copy-done.13, bf16[1024,256]{1,0:T(8,128)(2,1)} %copy-done.7, ...), custom_call_target="tpu_custom_call" | custom-call | tf_op jit(solution)/shard_map/pallas_call | solution.py:46
  67.2 2.5 %shard_map.96 = f32[1024,256]{1,0:T(8,128)S(1)} custom-call(s32[1]{0:T(128)} %bitcast.core_ref, s32[4,1024]{1,0:T(4,128)S(1)} %get-tuple-element.56.rows_ref, bf16[2048,512]{1,0:T(8,128)(2,1)S(1)} %get-tuple-element.42.d_hl), custom_call_target="tpu_custom_call" | custom-call | tf_op jit(solution)/shard_map/pallas_call | solution.py:46
  69.7 0.2 collective-permute-start.2
  69.9 2.5 %shard_map.97 = f32[1024,256]{1,0:T(8,128)S(1)} custom-call(s32[1]{0:T(128)} %bitcast.core_ref, s32[4,1024]{1,0:T(4,128)S(1)} %get-tuple-element.56.rows_ref, bf16[2048,512]{1,0:T(8,128)(2,1)S(1)} %get-tuple-element.42.d_hl), custom_call_target="tpu_custom_call" | custom-call | tf_op jit(solution)/shard_map/pallas_call | solution.py:46
  72.5 1.2 add.49
  73.7 3.9 %shard_map.98 = f32[2048,256]{1,0:T(8,128)} custom-call(s32[3,20]{1,0:T(4,128)S(1)} %pad_add_fusion.3.segs.by_column, s32[2,2]{1,0:T(2,128)S(1)} %pad_add_fusion.4.bounds, bf16[256,1024]{1,0:T(8,128)(2,1)S(1)} %get-tuple-element.45.hvt_hi.hvt_hi_at, bf16[256,1024]{1,0:T(8,128)(2,1)S(1)} %get-tuple-element.46.hvt_lo.hvt_lo_at, ...), custom_call_target="tpu_custom_call" | custom-call | tf_op jit(solution)/shard_map/pallas_call | solution.py:46
  77.6 0.4 collective-permute-start.7
  78.0 3.6 %all-to-all-start.1 = ((f32[8,128,256]{2,1,0:T(8,128)}), f32[8,128,256]{2,1,0:T(8,128)S(1)}, u32[]{:S(2)}, u32[]{:S(2)}) async-start(f32[8,128,256]{2,1,0:T(8,128)} %bitcast.60), calls=%async_computation.1 | async-start | bytes 2097152 | tf_op jit(solution)/shard_map/all_to_all | solution.py:298
  81.5 8.4 %shard_map.99 = (f32[2048,256]{1,0:T(8,128)S(1)}, f32[512,256]{1,0:T(8,128)S(1)}) custom-call(s32[3,20]{1,0:T(4,128)S(1)} %pad_add_fusion.3.segs.by_column, s32[2,2]{1,0:T(2,128)S(1)} %pad_add_fusion.4.bounds, s32[3,24]{1,0:T(4,128)S(1)} %pad_add_fusion.2.segs.by_row, bf16[256,1024]{1,0:T(8,128)(2,1)} %copy-done, bf16[256,1024]{1,0:T(8,128)(2,1)} %copy-done.1, ...), custom_call_target="tpu_custom_call" | custom-call | tf_op jit(solution)/shard_map/pallas_call | solution.py:46
  90.0 3.2 %add.60 = f32[2048,256]{1,0:T(8,128)} add(f32[2048,256]{1,0:T(8,128)S(1)} %get-tuple-element.52, f32[2048,256]{1,0:T(8,128)} %collective-permute-done.7) | non-fusion elementwise | flops 524288 | bytes 6291456 | tf_op jit(solution)/shard_map/add | solution.py:411
  93.2 5.5 %all-to-all-done.1 = f32[8,128,256]{2,1,0:T(8,128)S(1)} async-done(((f32[8,128,256]{2,1,0:T(8,128)}), f32[8,128,256]{2,1,0:T(8,128)S(1)}, u32[]{:S(2)}, u32[]{:S(2)}) %all-to-all-start.1) | async-done | bytes 1048608 | tf_op jit(solution)/shard_map/all_to_all | solution.py:298
  98.7 1.0 copy-done.14
  99.7 5.1 %all-to-all-start.2 = ((f32[64,32,256]{2,1,0:T(8,128)}), f32[64,32,256]{2,1,0:T(8,128)S(1)}, u32[]{:S(2)}, u32[]{:S(2)}) async-start(f32[64,32,256]{2,1,0:T(8,128)} %bitcast.33), calls=%async_computation.2 | async-start | bytes 4194304 | tf_op jit(solution)/shard_map/all_to_all | solution.py:298
  104.8 2.9 %collective-permute-start.5 = (f32[2,64,256]{2,1,0:T(8,128)S(1)}, f32[2,64,256]{2,1,0:T(8,128)S(1)}, u32[]{:S(2)}, u32[]{:S(2)}) collective-permute-start(f32[2,64,256]{2,1,0:T(8,128)S(1)} %get-tuple-element.54), channel_id=1, source_target_pairs={{0,3},{1,2},{2,1},{3,0},{4,7},{5,6},{6,5},{7,4},{8,11},{9,10},{10,... | collective-permute-start | bytes 393224 | tf_op jit(solution)/shard_map/ppermute | solution.py:324
  107.7 0.9 collective-permute-start.4
  108.6 0.5 collective-permute-start.3
  109.0 26.4 %collective-permute-done.5 = f32[2,64,256]{2,1,0:T(8,128)S(1)} collective-permute-done((f32[2,64,256]{2,1,0:T(8,128)S(1)}, f32[2,64,256]{2,1,0:T(8,128)S(1)}, u32[]{:S(2)}, u32[]{:S(2)}) %collective-permute-start.5) | collective-permute-done | bytes 131104 | tf_op jit(solution)/shard_map/ppermute | solution.py:324
  135.4 2.0 %reduce_sum.98 = f32[128,256]{1,0:T(8,128)} reduce(f32[8,128,256]{2,1,0:T(8,128)} %copy-done.14, f32[]{:T(128)} %constant.73.clone.1), dimensions={0}, to_apply=%region_8.9 | reduce | flops 229376 | bytes 1179652 | tf_op jit(solution)/shard_map/reduce_sum | solution.py:298
  137.4 1.5 %collective-permute-start.6 = (f32[64,256]{1,0:T(8,128)S(1)}, f32[64,256]{1,0:T(8,128)S(1)}, u32[]{:S(2)}, u32[]{:S(2)}) collective-permute-start(f32[64,256]{1,0:T(8,128)S(1)} %dynamic-slice_bitcast_fusion.3), channel_id=1, source_target_pairs={{0,4},{4,0},{1,5},{5,1},{2,6},{6,2},{3,7},{7,3},{8,12},{12,8},{9,1... | collective-permute-start | bytes 196616 | tf_op jit(solution)/shard_map/ppermute | solution.py:324
  138.8 2.8 %collective-permute-done.6 = f32[64,256]{1,0:T(8,128)S(1)} collective-permute-done((f32[64,256]{1,0:T(8,128)S(1)}, f32[64,256]{1,0:T(8,128)S(1)}, u32[]{:S(2)}, u32[]{:S(2)}) %collective-permute-start.6) | collective-permute-done | bytes 65568 | tf_op jit(solution)/shard_map/ppermute | solution.py:324
  141.6 0.6 fusion.2
  142.3 0.8 reduce_sum.99
  (45 shorter events, 0.7 us)
Async XLA Ops:
  1.4 5.6 %collective-permute-start = (s32[4,512]{1,0:T(4,128)S(1)}, s32[4,512]{1,0:T(4,128)S(1)}, u32[]{:S(2)}, u32[]{:S(2)}) collective-permute-start(s32[4,512]{1,0:T(4,128)S(1)} %get-tuple-element.59), channel_id=1, source_target_pairs={{0,7},{1,0},{2,1},{3,2},{4,3},{5,4},{6,5},{7,6},{8,15},{9,8},{10,9... | collective-permute-start | bytes 24584 | tf_op jit(solution)/shard_map/ppermute | solution.py:336
  9.3 18.6 %copy-start.4 = (f32[1,2048,256]{2,1,0:T(8,128)S(1)}, f32[1,2048,256]{2,1,0:T(8,128)}, u32[]{:S(2)}) copy-start(f32[1,2048,256]{2,1,0:T(8,128)} %param.8) | copy-start | bytes 6291460
  9.4 40.7 %all-to-all-start = ((f32[64,32,256]{2,1,0:T(8,128)}), f32[64,32,256]{2,1,0:T(8,128)}, u32[]{:S(2)}, u32[]{:S(2)}) async-start(f32[64,32,256]{2,1,0:T(8,128)} %broadcast_in_dim.41), calls=%async_computation | async-start | bytes 4194304 | tf_op jit(solution)/shard_map/all_to_all | solution.py:344
  28.0 1.0 copy-start.5
  29.0 1.0 copy-start.12
  39.0 1.0 copy-start.6
  40.0 0.8 copy-start.7
  40.8 0.8 copy-start.8
  41.6 0.8 copy-start.9
  42.4 0.8 copy-start.10
  43.2 0.8 copy-start.11
  44.0 29.7 %copy-start = (bf16[256,1024]{1,0:T(8,128)(2,1)}, bf16[256,1024]{1,0:T(8,128)(2,1)S(1)}, u32[]{:S(2)}) copy-start(bf16[256,1024]{1,0:T(8,128)(2,1)S(1)} %get-tuple-element.45.hvt_hi.hvt_hi_at) | copy-start | bytes 1572868
  44.0 29.7 %copy-start.1 = (bf16[256,1024]{1,0:T(8,128)(2,1)}, bf16[256,1024]{1,0:T(8,128)(2,1)S(1)}, u32[]{:S(2)}) copy-start(bf16[256,1024]{1,0:T(8,128)(2,1)S(1)} %get-tuple-element.46.hvt_lo.hvt_lo_at) | copy-start | bytes 1572868
  50.1 4.4 %collective-permute-start.1 = (f32[2048,256]{1,0:T(8,128)}, f32[2048,256]{1,0:T(8,128)S(1)}, u32[]{:S(2)}, u32[]{:S(2)}) collective-permute-start(f32[2048,256]{1,0:T(8,128)} %bitcast.10.own_at), channel_id=1, source_target_pairs={{0,8},{8,0},{1,9},{9,1},{2,10},{10,2},{3,11},{11,3},{4,12},{12,4},... | collective-permute-start | bytes 6291464 | tf_op jit(solution)/shard_map/ppermute | solution.py:370
  54.4 1.3 copy-start.13
  67.1 6.5 %copy-start.2 = (bf16[1024,256]{1,0:T(8,128)(2,1)}, bf16[1024,256]{1,0:T(8,128)(2,1)S(1)}, u32[]{:S(2)}) copy-start(bf16[1024,256]{1,0:T(8,128)(2,1)S(1)} %get-tuple-element.47.f_hi.f_hi_at) | copy-start | bytes 1572868
  67.2 6.5 %copy-start.3 = (bf16[1024,256]{1,0:T(8,128)(2,1)}, bf16[1024,256]{1,0:T(8,128)(2,1)S(1)}, u32[]{:S(2)}) copy-start(bf16[1024,256]{1,0:T(8,128)(2,1)S(1)} %get-tuple-element.48.f_lo.f_lo_at) | copy-start | bytes 1572868
  69.7 2.7 %collective-permute-start.2 = (f32[1024,256]{1,0:T(8,128)S(1)}, f32[1024,256]{1,0:T(8,128)S(1)}, u32[]{:S(2)}, u32[]{:S(2)}) collective-permute-start(f32[1024,256]{1,0:T(8,128)S(1)} %shard_map.96), channel_id=1, source_target_pairs={{0,8},{8,0},{1,9},{9,1},{2,10},{10,2},{3,11},{11,3},{4,12},{12,4},... | collective-permute-start | bytes 3145736 | tf_op jit(solution)/shard_map/ppermute | solution.py:387
  77.6 12.3 %collective-permute-start.7 = (f32[2048,256]{1,0:T(8,128)}, f32[2048,256]{1,0:T(8,128)}, u32[]{:S(2)}, u32[]{:S(2)}) collective-permute-start(f32[2048,256]{1,0:T(8,128)} %shard_map.98), channel_id=1, source_target_pairs={{0,8},{8,0},{1,9},{9,1},{2,10},{10,2},{3,11},{11,3},{4,12},{12,4},... | collective-permute-start | bytes 6291464 | tf_op jit(solution)/shard_map/ppermute | solution.py:400
  78.0 20.7 %all-to-all-start.1 = ((f32[8,128,256]{2,1,0:T(8,128)}), f32[8,128,256]{2,1,0:T(8,128)S(1)}, u32[]{:S(2)}, u32[]{:S(2)}) async-start(f32[8,128,256]{2,1,0:T(8,128)} %bitcast.60), calls=%async_computation.1 | async-start | bytes 2097152 | tf_op jit(solution)/shard_map/all_to_all | solution.py:298
  98.7 1.0 copy-start.14
  99.7 42.6 %all-to-all-start.2 = ((f32[64,32,256]{2,1,0:T(8,128)}), f32[64,32,256]{2,1,0:T(8,128)S(1)}, u32[]{:S(2)}, u32[]{:S(2)}) async-start(f32[64,32,256]{2,1,0:T(8,128)} %bitcast.33), calls=%async_computation.2 | async-start | bytes 4194304 | tf_op jit(solution)/shard_map/all_to_all | solution.py:298
  104.8 30.5 %collective-permute-start.5 = (f32[2,64,256]{2,1,0:T(8,128)S(1)}, f32[2,64,256]{2,1,0:T(8,128)S(1)}, u32[]{:S(2)}, u32[]{:S(2)}) collective-permute-start(f32[2,64,256]{2,1,0:T(8,128)S(1)} %get-tuple-element.54), channel_id=1, source_target_pairs={{0,3},{1,2},{2,1},{3,0},{4,7},{5,6},{6,5},{7,4},{8,11},{9,10},{10,... | collective-permute-start | bytes 393224 | tf_op jit(solution)/shard_map/ppermute | solution.py:324
  107.7 27.7 %collective-permute-start.4 = (f32[2,64,256]{2,1,0:T(8,128)S(1)}, f32[2,64,256]{2,1,0:T(8,128)S(1)}, u32[]{:S(2)}, u32[]{:S(2)}) collective-permute-start(f32[2,64,256]{2,1,0:T(8,128)S(1)} %get-tuple-element.55), channel_id=1, source_target_pairs={{0,2},{1,3},{2,0},{3,1},{4,6},{5,7},{6,4},{7,5},{8,10},{9,11},{10,... | collective-permute-start | bytes 393224 | tf_op jit(solution)/shard_map/ppermute | solution.py:324
  108.6 26.8 %collective-permute-start.3 = (f32[2,64,256]{2,1,0:T(8,128)S(1)}, f32[2,64,256]{2,1,0:T(8,128)S(1)}, u32[]{:S(2)}, u32[]{:S(2)}) collective-permute-start(f32[2,64,256]{2,1,0:T(8,128)S(1)} %get-tuple-element.53), channel_id=1, source_target_pairs={{0,1},{1,0},{2,3},{3,2},{4,5},{5,4},{6,7},{7,6},{8,9},{9,8},{10,11... | collective-permute-start | bytes 393224 | tf_op jit(solution)/shard_map/ppermute | solution.py:324
  137.4 4.3 %collective-permute-start.6 = (f32[64,256]{1,0:T(8,128)S(1)}, f32[64,256]{1,0:T(8,128)S(1)}, u32[]{:S(2)}, u32[]{:S(2)}) collective-permute-start(f32[64,256]{1,0:T(8,128)S(1)} %dynamic-slice_bitcast_fusion.3), channel_id=1, source_target_pairs={{0,4},{4,0},{1,5},{5,1},{2,6},{6,2},{3,7},{7,3},{8,12},{12,8},{9,1... | collective-permute-start | bytes 196616 | tf_op jit(solution)/shard_map/ppermute | solution.py:324

commit v4 on v3

--- a/solution.py
+++ b/solution.py
@@ -36,13 +36,13 @@
     return jnp.where(mask, 1.0, 0.0).astype(BF)
 
 
-def call(body, out_shape, scratch, args, smem=0, hbm=0, vmem=20):
+def call(body, out_shape, scratch, args, smem=0, hbm=0, keep=None, vmem=20):
     spaces = [pltpu.SMEM] * smem + [pltpu.HBM] * hbm
     spaces += [pltpu.VMEM] * (len(args) - smem - hbm)
     if hbm:
         fetched = [pltpu.with_memory_space_constraint(a, pltpu.HBM) for a in args[smem : smem + hbm]]
         args = tuple(args[:smem]) + tuple(fetched) + tuple(args[smem + hbm :])
-        scratch = [pltpu.SemaphoreType.DMA((hbm,))] + [pltpu.VMEM(a.shape, a.dtype) for a in fetched] + scratch
+        scratch = [pltpu.SemaphoreType.DMA((hbm,))] + [pltpu.VMEM(a.shape, a.dtype) for a in fetched[:keep]] + scratch
     return pl.pallas_call(
         body,
         out_shape=out_shape,
@@ -125,14 +125,22 @@
     lax.fori_loop(0, chunks, chunk, 0)
 
 
-def split_rels(own, other, r_hi, r_lo, copies=None):
-    count = own.shape[0]
-    for half, mats in enumerate((own, other)):
+def split_rels(halves, r_hi, r_lo, copies=None):
+    for half, mats in enumerate(halves):
+        count = mats.shape[0]
         if copies:
             copies[half].wait()
         high, low = split(mats[...])
         r_hi[half * count : (half + 1) * count, :] = high
         r_lo[half * count : (half + 1) * count, :] = low
+
+
+def keep_half(half, count, first, last, slot):
+    if half is None:
+        return last, slot
+    if half == 0:
+        return jnp.where(slot < count, last, first), jnp.minimum(slot, count - 1)
+    return jnp.where(slot >= count, last, first), jnp.maximum(slot - count, 0)
 
 
 def visits(segs, tile, total, one, low=0, high=None):
@@ -148,40 +156,49 @@
     lax.fori_loop(low, segs.shape[1] // group if high is None else high, some, 0)
 
 
-def by_relation(segs, a_hi, a_lo, r_hi, r_lo, out, dims):
+def by_relation(segs, a_hi, a_lo, r_hi, r_lo, out, dims, half=None, low=0, high=None):
     width = r_hi.shape[1]
     tile = 128
-    out[...] = jnp.zeros_like(out)
 
     def one(start, first, last, slot):
+        last, slot = keep_half(half, r_hi.shape[0] // width, first, last, slot)
         rows = pl.ds(start, tile)
         place = start + lax.broadcasted_iota(jnp.int32, (tile, 1), 0)
         mask = ones_where((place >= first) & (place < last))
-        high = a_hi[rows, :] * mask
-        both = jnp.concatenate([high, a_lo[rows, :] * mask], axis=0)
+        top = a_hi[rows, :] * mask
+        both = jnp.concatenate([top, a_lo[rows, :] * mask], axis=0)
         mat = pl.ds(pl.multiple_of(slot * width, width), width)
         main = dot(both, r_hi[mat, :], dims)
-        out[rows, :] += main[:tile] + main[tile:] + dot(high, r_lo[mat, :], dims)
-
-    visits(segs, tile, out.shape[0], one)
+        out[rows, :] += main[:tile] + main[tile:] + dot(top, r_lo[mat, :], dims)
+
+    visits(segs, tile, out.shape[0], one, low, high)
+
+
+def query_body(
+    segs, bounds, own_at, hv_hi_at, hv_lo_at, tv_at, n_hi_at, n_lo_at, rank_at,
+    query, hv_hi, hv_lo, tv, n_hi, n_lo, rank_col, sems, own, r_hi, r_lo,
+):
+    sources = (own_at, hv_hi_at, hv_lo_at, tv_at, n_hi_at, n_lo_at, rank_at)
+    copies = fetch(sources, (own, hv_hi, hv_lo, tv, n_hi, n_lo, rank_col), sems)
+    query[...] = jnp.zeros_like(query)
+    split_rels((own,), r_hi, r_lo, copies)
+    copies[1].wait()
+    copies[2].wait()
+    by_relation(segs, hv_hi, hv_lo, r_hi, r_lo, query, NN, 0, bounds[0, 0], bounds[0, 1])
+    for copy in copies[3:]:
+        copy.wait()
 
 
 def factor_body(
-    segs, own_at, other_at, hv_hi_at, hv_lo_at, rank_at, tv_at, n_hi_at, n_lo_at, meta,
-    f_hi, f_lo, d_hl, sems, own, other, hv_hi, hv_lo, rank_col, tv, n_hi, n_lo, r_hi, r_lo, query, pair, f_hl,
+    segs, bounds, partial, hv_hi, hv_lo, tv, n_hi, n_lo, rank_col, other, meta,
+    f_hi, f_lo, d_hl, r_hi, r_lo, query, pair, f_hl,
 ):
-    width = own.shape[1]
+    width = other.shape[1]
     triples = tv.shape[0]
     batch = triples // 2
-    copies = fetch(
-        (own_at, other_at, hv_hi_at, hv_lo_at, rank_at, tv_at, n_hi_at, n_lo_at),
-        (own, other, hv_hi, hv_lo, rank_col, tv, n_hi, n_lo),
-        sems,
-    )
-    split_rels(own, other, r_hi, r_lo, copies)
-    for copy in copies[2:]:
-        copy.wait()
-    by_relation(segs, hv_hi, hv_lo, r_hi, r_lo, query, NN)
+    query[...] = partial[...]
+    split_rels((other,), r_hi, r_lo)
+    by_relation(segs, hv_hi, hv_lo, r_hi, r_lo, query, NN, 1, bounds[1, 0], bounds[1, 1])
     high, low = split(query[...])
     pair[:, :width] = high
     pair[:, width:] = low
@@ -223,9 +240,7 @@
 
     def one(start, first, last, slot):
         part = pl.ds(start, tile)
-        mine = (slot < count) if half == 0 else (slot >= count)
-        last = jnp.where(mine, last, first)
-        slot = jnp.minimum(slot, count - 1) if half == 0 else jnp.maximum(slot - count, 0)
+        last, slot = keep_half(half, count, first, last, slot)
         place = start + lax.broadcasted_iota(jnp.int32, (1, tile), 1)
         mask = ones_where((place >= first) & (place < last))
         high = hvt_hi[:, part] * mask
@@ -237,20 +252,14 @@
     visits(segs, tile, f_hi.shape[0], one, bounds[half, 0], bounds[half, 1])
 
 
-def own_body(
-    by_column, bounds, by_row, hvt_hi_at, hvt_lo_at, f_hi_at, f_lo_at, own_at, other_at, meta,
-    rel_own, head_grad, sems, hvt_hi, hvt_lo, f_hi, f_lo, own, other, r_hi, r_lo, through, th_hl,
+def head_body(
+    segs, f_hi_at, f_lo_at, own_at, other_at, meta, head_grad, sems, f_hi, f_lo, own, other, r_hi, r_lo, through, th_hl
 ):
-    copies = fetch(
-        (hvt_hi_at, hvt_lo_at, f_hi_at, f_lo_at, own_at, other_at),
-        (hvt_hi, hvt_lo, f_hi, f_lo, own, other),
-        sems,
-    )
-    for copy in copies[:4]:
+    copies = fetch((f_hi_at, f_lo_at, own_at, other_at), (f_hi, f_lo, own, other), sems)
+    split_rels((own, other), r_hi, r_lo, copies[2:])
+    for copy in copies[:2]:
         copy.wait()
-    rel_body(0, by_column, bounds, hvt_hi, hvt_lo, f_hi, f_lo, rel_own)
-    split_rels(own, other, r_hi, r_lo, copies[4:])
-    head_part(by_row, meta, f_hi, f_lo, head_grad, r_hi, r_lo, through, th_hl)
+    head_part(segs, meta, f_hi, f_lo, head_grad, r_hi, r_lo, through, th_hl)
 
 
 def tail_body(half, core_ref, rows_ref, d_hl, out):
@@ -274,6 +283,7 @@
 
 def head_part(segs, meta, f_hi, f_lo, out, r_hi, r_lo, through, th_hl):
     width = out.shape[1]
+    through[...] = jnp.zeros_like(through)
     by_relation(segs, f_hi, f_lo, r_hi, r_lo, through, NT)
     high, low = split(through[...])
     th_hl[:, :width] = high
@@ -288,14 +298,20 @@
     return jax.ShapeDtypeStruct(dims, dtype)
 
 
+def half_bounds(segs, starts):
+    middle = jnp.sum((segs[0] < starts[starts.shape[0] // 2]).astype(jnp.int32))
+    end = jnp.full_like(middle, segs.shape[1] // 4)
+    return jnp.stack([jnp.stack([jnp.zeros_like(middle), (middle + 3) // 4]), jnp.stack([middle // 4, end])])
+
+
 def after(value, earlier):
     return lax.optimization_barrier((value, earlier))[0]
 
 
-def exchange_sum(value, axes):
+def exchange(value, axes):
     devices = lax.axis_size(axes)
     pieces = value.reshape(devices, value.shape[0] // devices, value.shape[1])
-    return jnp.sum(lax.all_to_all(pieces, axes, split_axis=0, concat_axis=0), axis=0)
+    return lax.all_to_all(pieces, axes, split_axis=0, concat_axis=0)
 
 
 def segments(starts, tile, total):
@@ -315,10 +331,12 @@
     return jnp.stack([first, ordered[1:], slot]).astype(jnp.int32)
 
 
-def permute_sum(value, axis):
+def permute_sum(value, axis, behind=None):
     devices = lax.axis_size(axis)
     me = lax.axis_index(axis)
     total = lax.dynamic_index_in_dim(value, me, 0, keepdims=False)
+    if behind is not None:
+        total = after(total, behind)
     for k in range(1, devices):
         piece = lax.dynamic_index_in_dim(value, me ^ k, 0, keepdims=False)
         total += lax.ppermute(piece, axis, [(i, i ^ k) for i in range(devices)])
@@ -347,10 +365,8 @@
     starts = jnp.sum((slots[None, :] < jnp.arange(rel_count)[:, None]).astype(jnp.int32), axis=1)
     by_row = segments(starts, 128, triples)
     by_column = segments(starts, 256, triples)
-    middle = jnp.sum((by_column[0] < starts[rel_count // 2]).astype(jnp.int32))
-    groups = jnp.full_like(middle, by_column.shape[1] // 4)
-    zero = jnp.zeros_like(middle)
-    bounds = jnp.stack([jnp.stack([zero, (middle + 3) // 4]), jnp.stack([middle // 4, groups])])
+    row_bounds = half_bounds(by_row, starts)
+    bounds = half_bounds(by_column, starts)
     wide = shape(triples, width, dtype=BF)
     high = shape(width, triples, dtype=BF)
     gathered = call(
@@ -366,52 +382,63 @@
         smem=1,
     )
     hv_hi, hv_lo, hvt_hi, hvt_lo, tv, n_hi, n_lo, rank_col, meta = gathered
-    meta, own, by_row, by_column, bounds = lax.optimization_barrier((meta, own, by_row, by_column, bounds))
+    meta, own, by_row, row_bounds, by_column, bounds = lax.optimization_barrier(
+        (meta, own, by_row, row_bounds, by_column, bounds)
+    )
     other = lax.ppermute(own, "c", SWAP)
-    rel_scratch = [pltpu.VMEM((2 * own.shape[0], width), BF)] * 2
+    half_scratch = [pltpu.VMEM(own.shape, BF)] * 2
+    plain = shape(triples, width)
+    ready = call(
+        query_body,
+        [plain, wide, wide, plain, wide, wide, shape(triples, 1, dtype=jnp.int32)],
+        half_scratch,
+        (by_row, row_bounds, own, hv_hi, hv_lo, tv, n_hi, n_lo, rank_col),
+        smem=2,
+        hbm=7,
+        keep=1,
+    )
     f_hi, f_lo, d_hl = call(
         factor_body,
         [wide, wide, shape(2 * triples, 2 * width, dtype=BF)],
-        rel_scratch + [pltpu.VMEM((triples, width), F32)] + [pltpu.VMEM((triples, 2 * width), BF)] * 2,
-        (by_row, own, other, hv_hi, hv_lo, rank_col, tv, n_hi, n_lo, meta),
-        smem=1,
-        hbm=8,
-        vmem=32,
-    )
+        half_scratch + [pltpu.VMEM((triples, width), F32)] + [pltpu.VMEM((triples, 2 * width), BF)] * 2,
+        (by_row, row_bounds, *ready, other, meta),
+        smem=2,
+    )
+
+    def rel_part(half, bounds):
+        out = shape(*own.shape)
+        args = (by_column, bounds, hvt_hi, hvt_lo, f_hi, f_lo)
+        return call(functools.partial(rel_body, half), out, [], args, smem=2)
 
     def tail_part(half, core):
         out = shape(tails.shape[0] // 2, width)
         return call(functools.partial(tail_body, half), out, [], (core, rows, d_hl), smem=1)
 
-    tail_theirs = tail_part(1, core)
+    rel_other = rel_part(1, bounds)
+    rel_came = lax.ppermute(rel_other, "c", SWAP)
+    rel_own = rel_part(0, after(bounds, rel_other))
+    tail_theirs = tail_part(1, after(core, rel_own))
     tail_came = lax.ppermute(tail_theirs, "c", SWAP)
-    tail_mine = tail_part(0, after(core, tail_theirs))
-    tail_sum = tail_mine + tail_came
-    bounds = after(bounds, tail_sum)
-    tail_share = exchange_sum(tail_sum, HEAD_CHIPS)
-
-    rel_other = call(
-        functools.partial(rel_body, 1),
-        shape(*own.shape),
-        [],
-        (by_column, bounds, hvt_hi, hvt_lo, f_hi, f_lo),
-        smem=2,
-    )
-    rel_came = lax.ppermute(rel_other, "c", SWAP)
-    bounds = after(bounds, rel_other)
-    rel_own, head_grad = call(
-        own_body,
-        [shape(*own.shape), shape(*heads.shape)],
-        rel_scratch + [pltpu.VMEM((triples, width), F32), pltpu.VMEM((triples, 2 * width), BF)],
-        (by_column, bounds, by_row, hvt_hi, hvt_lo, f_hi, f_lo, own, other, meta),
-        smem=3,
-        hbm=6,
+    rel_sum = rel_own + rel_came
+    rel_pieces = exchange(rel_sum, CHIPS)
+
+    tail_mine = tail_part(0, after(core, rel_sum))
+    head_grad = call(
+        head_body,
+        shape(*heads.shape),
+        [pltpu.VMEM((2 * own.shape[0], width), BF)] * 2
+        + [pltpu.VMEM((triples, width), F32), pltpu.VMEM((triples, 2 * width), BF)],
+        (after(by_row, tail_mine), f_hi, f_lo, own, other, meta),
+        smem=1,
+        hbm=4,
         vmem=32,
     )
-    rel_share = exchange_sum(rel_own + rel_came, CHIPS)
     pieces = head_grad.reshape(lax.axis_size("zl"), lax.axis_size("x"), -1, width)
     pieces = permute_sum(jnp.swapaxes(pieces, 0, 1), "x")
-    head_share = permute_sum(after(pieces, tail_share), "zl")
+    tail_sum = after(tail_mine + tail_came, (pieces, rel_pieces))
+    tail_share = jnp.sum(exchange(tail_sum, HEAD_CHIPS), axis=0)
+    rel_share = jnp.sum(rel_pieces, axis=0)
+    head_share = permute_sum(pieces, "zl", rel_share)
     return (head_share[None], tail_share[None], rel_share)
 
 

time: 144 us -> 134 us (0.931)
  waiting for transfers between devices: 45.8 us -> 28.8 us
  starting transfers between devices: 31 us -> 36.5 us
  local copies, waits for them, and re-layouts: 13.5 us -> 9.92 us
  between operations: 4.09 us -> 7.45 us
    ppermute x4, waiting for transfers between devices: 29.2 us -> 21.3 us  [permute_sum(): total += lax.ppermute(piece, axis, [(i, i ^ k) for i in range(devices)])]
    all_to_all x2, starting transfers between devices: 8.66 us -> 14.9 us  [exchange(): return lax.all_to_all(pieces, axes, split_axis=0, concat_axis=0)]
    ppermute x1, waiting for transfers between devices: 4.37 us -> 0.62 us  [per_device(): other = lax.ppermute(own, 'c', SWAP)]
    all_to_all x2, waiting for transfers between devices: 5.52 us -> 1.78 us  [exchange(): return lax.all_to_all(pieces, axes, split_axis=0, concat_axis=0)]
    all_to_all x1, waiting for transfers between devices: 5.36 us -> 2.56 us  [per_device(): lax.all_to_all(spread, CHIPS, split_axis=0, concat_axis=0)]
    unnamed x30, local copies, waits for them, and re-layouts: 9.35 us -> 6.67 us
    reduce_sum x3 -> x4, other arithmetic: 3.98 us -> 5.62 us  [the longest x2 2.56 us: half_bounds(): middle = jnp.sum((segs[0] < starts[starts.shape[0] // 2]).astype(jnp.int32))]
    pallas_call x6 -> x8, Pallas kernels: 37.7 us -> 38.4 us  [call(): pl.pallas_call(body, out_shape=out_shape, in_specs=[pl.BlockSpec(memory_s...]
  transfers between devices with their start and end apart: 11 -> 11, of which waited for: 6 -> 7; matrix products, arithmetic and copies ran while one was open for 7% -> 7% of each run, Pallas kernels for 14% -> 21%
where the time goes in v4:
time: 134 us; the launch traced here: 133 us
  Pallas kernels  38.4 us (29%)
  starting transfers between devices  36.5 us (27%)
  waiting for transfers between devices  28.8 us (21%)
  other arithmetic  12.4 us (9%)
  local copies, waits for them, and re-layouts  9.92 us (7%)
  between operations  7.45 us (6%)
    pallas_call x8, Pallas kernels, call(): pl.pallas_call(body, out_shape=out_shape, in_specs=[pl.BlockSpec(memory_s...  38.4 us
    ppermute x4, waiting for transfers between devices, permute_sum(): total += lax.ppermute(piece, axis, [(i, i ^ k) for i in range(devices)])  21.3 us
    all_to_all x2, starting transfers between devices, exchange(): return lax.all_to_all(pieces, axes, split_axis=0, concat_axis=0)  14.9 us
    all_to_all x1, starting transfers between devices, per_device(): lax.all_to_all(spread, CHIPS, split_axis=0, concat_axis=0)  11.8 us
    unnamed x30, local copies, waits for them, and re-layouts  6.67 us
    ppermute x4, starting transfers between devices, permute_sum(): total += lax.ppermute(piece, axis, [(i, i ^ k) for i in range(devices)])  4.84 us
    ppermute x1, starting transfers between devices, per_device(): lax.ppermute(index[1], TAIL, [(i, (i - 1) % behind) for i in range(behind)])  4.26 us
  transfers between devices with their start and end apart: 11, of which 7 were waited for; matrix products, arithmetic and copies ran while one was open for 7% of the time, Pallas kernels for 21%

profile of v4, /device:TPU:0, one launch (start us, length us, event | category | flops | bytes accessed | tf_op | source)
XLA Modules:
  0.0 133.4 jit_solution(6778860094706169970)
XLA Ops:
  0.6 0.8 pad_add_fusion.1
  1.4 4.3 %collective-permute-start = (s32[4,512]{1,0:T(4,128)S(1)}, s32[4,512]{1,0:T(4,128)S(1)}, u32[]{:S(2)}, u32[]{:S(2)}) collective-permute-start(s32[4,512]{1,0:T(4,128)S(1)} %get-tuple-element.77), channel_id=1, source_target_pairs={{0,7},{1,0},{2,1},{3,2},{4,3},{5,4},{6,5},{7,6},{8,15},{9,8},{10,9... | collective-permute-start | bytes 24584 | tf_op jit(solution)/shard_map/ppermute | solution.py:354
  5.7 1.4 %collective-permute-done = s32[4,512]{1,0:T(4,128)S(1)} collective-permute-done((s32[4,512]{1,0:T(4,128)S(1)}, s32[4,512]{1,0:T(4,128)S(1)}, u32[]{:S(2)}, u32[]{:S(2)}) %collective-permute-start) | collective-permute-done | bytes 8224 | tf_op jit(solution)/shard_map/ppermute | solution.py:354
  7.0 2.3 %broadcast_in_dim.41 = f32[64,32,256]{2,1,0:T(8,128)} broadcast(f32[32,256]{1,0:T(8,128)} %param.9), dimensions={1,2} | broadcast | bytes 2129920 | tf_op jit(solution)/shard_map/broadcast_in_dim | solution.py:358
  9.4 0.1 convert_reduce_fusion
  9.5 0.6 slice.37
  10.2 11.8 %all-to-all-start = ((f32[64,32,256]{2,1,0:T(8,128)}), f32[64,32,256]{2,1,0:T(8,128)}, u32[]{:S(2)}, u32[]{:S(2)}) async-start(f32[64,32,256]{2,1,0:T(8,128)} %broadcast_in_dim.41), calls=%async_computation | async-start | bytes 4194304 | tf_op jit(solution)/shard_map/all_to_all | solution.py:362
  22.1 0.2 convert_reduce_fusion.2
  22.3 0.1 select_reduce_fusion.1
  22.4 1.3 fusion.10
  27.0 0.2 convert_reduce_fusion.1
  27.1 0.1 select_reduce_fusion
  27.3 1.3 fusion.11
  31.8 0.2 copy.11.cols
  32.2 9.0 %shard_map.94 = (bf16[1024,256]{1,0:T(8,128)(2,1)S(1)}, bf16[1024,256]{1,0:T(8,128)(2,1)S(1)}, bf16[256,1024]{1,0:T(8,128)(2,1)S(1)}, bf16[256,1024]{1,0:T(8,128...) custom-call(s32[1]{0:T(128)} %bitcast.core_ref, ...), custom_call_target="tpu_custom_call" | custom-call | tf_op jit(solution)/shard_map/pallas_call | solution.py:46
  41.2 0.8 copy-done.3
  42.0 0.8 copy-done.5
  42.7 1.0 copy-done.8
  43.7 0.8 copy-done.9
  44.5 0.8 copy-done.10
  45.3 0.8 copy-done.11
  46.1 0.8 copy-done.12
  47.0 0.8 copy-done.13
  48.3 2.6 %all-to-all-done = f32[64,32,256]{2,1,0:T(8,128)} async-done(((f32[64,32,256]{2,1,0:T(8,128)}), f32[64,32,256]{2,1,0:T(8,128)}, u32[]{:S(2)}, u32[]{:S(2)}) %all-to-all-start) | async-done | bytes 2097184 | tf_op jit(solution)/shard_map/all_to_all | solution.py:362
  50.9 3.7 %shard_map.95 = (f32[1024,256]{1,0:T(8,128)S(1)}, bf16[1024,256]{1,0:T(8,128)(2,1)S(1)}, bf16[1024,256]{1,0:T(8,128)(2,1)S(1)}, f32[1024,256]{1,0:T(8,128)S(1)},...) custom-call(s32[3,24]{1,0:T(4,128)S(1)} %pad_add_fusion.2.segs, ...), custom_call_target="tpu_custom_call" | custom-call | tf_op jit(solution)/shard_map/pallas_call | solution.py:46
  54.6 0.6 collective-permute-done.1.other.other_at
  55.3 7.4 %shard_map.96 = (bf16[1024,256]{1,0:T(8,128)(2,1)S(1)}, bf16[1024,256]{1,0:T(8,128)(2,1)S(1)}, bf16[2048,512]{1,0:T(8,128)(2,1)S(1)}) custom-call(s32[3,24]{1,0:T(4,128)S(1)} %pad_add_fusion.2.segs, s32[2,2]{1,0:T(2,128)S(1)} %get-tuple-element.44.bounds, f32[1024,256]{1,0:T(8,128)S(1)} %get-tuple-element.52.partial, ...), custom_call_target="tpu_custom_call" | custom-call | tf_op jit(solution)/shard_map/pallas_call | solution.py:46
  62.7 2.6 %shard_map.97 = f32[2048,256]{1,0:T(8,128)S(1)} custom-call(s32[3,20]{1,0:T(4,128)S(1)} %pad_add_fusion.3.segs, s32[2,2]{1,0:T(2,128)S(1)} %get-tuple-element.62.bounds, bf16[256,1024]{1,0:T(8,128)(2,1)S(1)} %copy-done.4, bf16[256,1024]{1,0:T(8,128)(2,1)S(1)} %copy-done.6, bf16[1024,256]{1,0:T(8,128)(2,1)S(1)} %get-tuple-element.60.f_hi.f_hi_at, ...), custom_call_target="tpu_custom_call" | custom-call | tf_op jit(solution)/shard_map/pallas_call | solution.py:46
  65.3 0.6 collective-permute-start.2
  65.9 2.6 %shard_map.98 = f32[2048,256]{1,0:T(8,128)S(1)} custom-call(s32[3,20]{1,0:T(4,128)S(1)} %pad_add_fusion.3.segs, s32[2,2]{1,0:T(2,128)S(1)} %get-tuple-element.62.bounds, bf16[256,1024]{1,0:T(8,128)(2,1)S(1)} %copy-done.4, bf16[256,1024]{1,0:T(8,128)(2,1)S(1)} %copy-done.6, bf16[1024,256]{1,0:T(8,128)(2,1)S(1)} %get-tuple-element.60.f_hi.f_hi_at, ...), custom_call_target="tpu_custom_call" | custom-call | tf_op jit(solution)/shard_map/pallas_call | solution.py:46
  68.5 1.2 collective-permute-done.2
  69.7 1.6 %add.55 = f32[2048,256]{1,0:T(8,128)} add(f32[2048,256]{1,0:T(8,128)S(1)} %shard_map.98, f32[2048,256]{1,0:T(8,128)S(1)} %collective-permute-done.2) | non-fusion elementwise | flops 524288 | bytes 6291456 | tf_op jit(solution)/shard_map/add | solution.py:422
  71.3 8.0 %all-to-all-start.1 = ((f32[64,32,256]{2,1,0:T(8,128)}), f32[64,32,256]{2,1,0:T(8,128)}, u32[]{:S(2)}, u32[]{:S(2)}) async-start(f32[64,32,256]{2,1,0:T(8,128)} %bitcast.64), calls=%async_computation.1 | async-start | bytes 4194304 | tf_op jit(solution)/shard_map/all_to_all | solution.py:314
  79.3 3.5 %shard_map.101 = f32[1024,256]{1,0:T(8,128)} custom-call(s32[1]{0:T(128)} %bitcast.core_ref, s32[4,1024]{1,0:T(4,128)S(1)} %get-tuple-element.74.rows_ref, bf16[2048,512]{1,0:T(8,128)(2,1)S(1)} %get-tuple-element.64.d_hl), custom_call_target="tpu_custom_call" | custom-call | tf_op jit(solution)/shard_map/pallas_call | solution.py:46
  82.9 2.5 %shard_map.99 = f32[1024,256]{1,0:T(8,128)S(1)} custom-call(s32[1]{0:T(128)} %bitcast.core_ref, s32[4,1024]{1,0:T(4,128)S(1)} %get-tuple-element.74.rows_ref, bf16[2048,512]{1,0:T(8,128)(2,1)S(1)} %get-tuple-element.64.d_hl), custom_call_target="tpu_custom_call" | custom-call | tf_op jit(solution)/shard_map/pallas_call | solution.py:46
  85.4 7.1 %shard_map.100 = f32[512,256]{1,0:T(8,128)S(1)} custom-call(s32[3,24]{1,0:T(4,128)S(1)} %pad_add_fusion.2.segs, bf16[1024,256]{1,0:T(8,128)(2,1)} %copy-done.1, bf16[1024,256]{1,0:T(8,128)(2,1)} %copy-done.2, f32[2048,256]{1,0:T(8,128)} %bitcast.10.own_at, f32[2048,256]{1,0:T(8,128)} %copy-done, s32[2,1024]{1,0:T(2,128)S(1)} %get-tuple-element.59.meta), custom_call_target="tpu_custom_call" | custom-call | tf_op jit(solution)/shard_map/pallas_call | solution.py:46
  92.6 2.7 %collective-permute-start.5 = (f32[2,64,256]{2,1,0:T(8,128)S(1)}, f32[2,64,256]{2,1,0:T(8,128)S(1)}, u32[]{:S(2)}, u32[]{:S(2)}) collective-permute-start(f32[2,64,256]{2,1,0:T(8,128)S(1)} %get-tuple-element.70), channel_id=1, source_target_pairs={{0,3},{1,2},{2,1},{3,0},{4,7},{5,6},{6,5},{7,4},{8,11},{9,10},{10,... | collective-permute-start | bytes 393224 | tf_op jit(solution)/shard_map/ppermute | solution.py:342
  95.3 0.9 collective-permute-start.4
  96.2 0.6 collective-permute-start.3
  96.8 2.3 %add.66 = f32[1024,256]{1,0:T(8,128)} add(f32[1024,256]{1,0:T(8,128)S(1)} %shard_map.99, f32[1024,256]{1,0:T(8,128)} %collective-permute-done.7) | non-fusion elementwise | flops 262144 | bytes 3145728 | tf_op jit(solution)/shard_map/add | solution.py:438
  99.1 11.3 %collective-permute-done.5 = f32[2,64,256]{2,1,0:T(8,128)S(1)} collective-permute-done((f32[2,64,256]{2,1,0:T(8,128)S(1)}, f32[2,64,256]{2,1,0:T(8,128)S(1)}, u32[]{:S(2)}, u32[]{:S(2)}) %collective-permute-start.5) | collective-permute-done | bytes 131104 | tf_op jit(solution)/shard_map/ppermute | solution.py:342
  110.5 6.8 %all-to-all-start.2 = ((f32[8,128,256]{2,1,0:T(8,128)}), f32[8,128,256]{2,1,0:T(8,128)S(1)}, u32[]{:S(2)}, u32[]{:S(2)}) async-start(f32[8,128,256]{2,1,0:T(8,128)} %bitcast.36), calls=%async_computation.2 | async-start | bytes 2097152 | tf_op jit(solution)/shard_map/all_to_all | solution.py:314
  117.3 0.7 collective-permute-start.6
  118.0 2.3 %reduce_sum.108 = f32[32,256]{1,0:T(8,128)} reduce(f32[64,32,256]{2,1,0:T(8,128)} %all-to-all-done.1, f32[]{:T(128)} %constant.90.clone.1), dimensions={0}, to_apply=%region_9.10 | reduce | flops 516096 | bytes 2129924 | tf_op jit(solution)/shard_map/reduce_sum | solution.py:440
  120.3 10.0 %collective-permute-done.6 = f32[64,256]{1,0:T(8,128)S(1)} collective-permute-done((f32[64,256]{1,0:T(8,128)S(1)}, f32[64,256]{1,0:T(8,128)S(1)}, u32[]{:S(2)}, u32[]{:S(2)}) %collective-permute-start.6) | collective-permute-done | bytes 65568 | tf_op jit(solution)/shard_map/ppermute | solution.py:342
  130.3 0.6 add_bitcast_fusion
  130.9 1.8 %all-to-all-done.2 = f32[8,128,256]{2,1,0:T(8,128)S(1)} async-done(((f32[8,128,256]{2,1,0:T(8,128)}), f32[8,128,256]{2,1,0:T(8,128)S(1)}, u32[]{:S(2)}, u32[]{:S(2)}) %all-to-all-start.2) | async-done | bytes 1048608 | tf_op jit(solution)/shard_map/all_to_all | solution.py:314
  132.7 0.7 reduce_sum.109
  (50 shorter events, 1.0 us)
Async XLA Ops:
  1.4 5.6 %collective-permute-start = (s32[4,512]{1,0:T(4,128)S(1)}, s32[4,512]{1,0:T(4,128)S(1)}, u32[]{:S(2)}, u32[]{:S(2)}) collective-permute-start(s32[4,512]{1,0:T(4,128)S(1)} %get-tuple-element.77), channel_id=1, source_target_pairs={{0,7},{1,0},{2,1},{3,2},{4,3},{5,4},{6,5},{7,6},{8,15},{9,8},{10,9... | collective-permute-start | bytes 24584 | tf_op jit(solution)/shard_map/ppermute | solution.py:354
  10.2 22.0 %copy-start.7 = (f32[1,2048,256]{2,1,0:T(8,128)S(1)}, f32[1,2048,256]{2,1,0:T(8,128)}, u32[]{:S(2)}) copy-start(f32[1,2048,256]{2,1,0:T(8,128)} %param.8) | copy-start | bytes 6291460
  10.2 22.0 %copy-start.14 = (f32[1,512,256]{2,1,0:T(8,128)S(1)}, f32[1,512,256]{2,1,0:T(8,128)}, u32[]{:S(2)}) copy-start(f32[1,512,256]{2,1,0:T(8,128)} %param.7) | copy-start | bytes 1572868
  10.2 40.7 %all-to-all-start = ((f32[64,32,256]{2,1,0:T(8,128)}), f32[64,32,256]{2,1,0:T(8,128)}, u32[]{:S(2)}, u32[]{:S(2)}) async-start(f32[64,32,256]{2,1,0:T(8,128)} %broadcast_in_dim.41), calls=%async_computation | async-start | bytes 4194304 | tf_op jit(solution)/shard_map/all_to_all | solution.py:362
  41.1 0.8 copy-start.3
  42.0 0.8 copy-start.5
  42.7 1.0 copy-start.8
  43.7 0.8 copy-start.9
  44.5 0.8 copy-start.10
  45.3 0.8 copy-start.11
  46.1 0.8 copy-start.12
  47.0 0.8 copy-start.13
  50.9 4.4 %collective-permute-start.1 = (f32[2048,256]{1,0:T(8,128)}, f32[2048,256]{1,0:T(8,128)S(1)}, u32[]{:S(2)}, u32[]{:S(2)}) collective-permute-start(f32[2048,256]{1,0:T(8,128)} %bitcast.10.own_at), channel_id=1, source_target_pairs={{0,8},{8,0},{1,9},{9,1},{2,10},{10,2},{3,11},{11,3},{4,12},{12,4},... | collective-permute-start | bytes 6291464 | tf_op jit(solution)/shard_map/ppermute | solution.py:388
  55.3 7.4 %copy-start = (f32[2048,256]{1,0:T(8,128)}, f32[2048,256]{1,0:T(8,128)S(1)}, u32[]{:S(2)}) copy-start(f32[2048,256]{1,0:T(8,128)S(1)} %collective-permute-done.1.other.other_at) | copy-start | bytes 6291460
  55.3 7.4 %copy-start.4 = (bf16[256,1024]{1,0:T(8,128)(2,1)S(1)}, bf16[256,1024]{1,0:T(8,128)(2,1)}, u32[]{:S(2)}) copy-start(bf16[256,1024]{1,0:T(8,128)(2,1)} %copy-done.3) | copy-start | bytes 1572868
  55.3 7.4 %copy-start.6 = (bf16[256,1024]{1,0:T(8,128)(2,1)S(1)}, bf16[256,1024]{1,0:T(8,128)(2,1)}, u32[]{:S(2)}) copy-start(bf16[256,1024]{1,0:T(8,128)(2,1)} %copy-done.5) | copy-start | bytes 1572868
  62.6 3.2 %copy-start.1 = (bf16[1024,256]{1,0:T(8,128)(2,1)}, bf16[1024,256]{1,0:T(8,128)(2,1)S(1)}, u32[]{:S(2)}) copy-start(bf16[1024,256]{1,0:T(8,128)(2,1)S(1)} %get-tuple-element.60.f_hi.f_hi_at) | copy-start | bytes 1572868
  62.7 3.2 %copy-start.2 = (bf16[1024,256]{1,0:T(8,128)(2,1)}, bf16[1024,256]{1,0:T(8,128)(2,1)S(1)}, u32[]{:S(2)}) copy-start(bf16[1024,256]{1,0:T(8,128)(2,1)S(1)} %get-tuple-element.61.f_lo.f_lo_at) | copy-start | bytes 1572868
  65.3 4.4 %collective-permute-start.2 = (f32[2048,256]{1,0:T(8,128)S(1)}, f32[2048,256]{1,0:T(8,128)S(1)}, u32[]{:S(2)}, u32[]{:S(2)}) collective-permute-start(f32[2048,256]{1,0:T(8,128)S(1)} %shard_map.97), channel_id=1, source_target_pairs={{0,8},{8,0},{1,9},{9,1},{2,10},{10,2},{3,11},{11,3},{4,12},{12,4},... | collective-permute-start | bytes 6291464 | tf_op jit(solution)/shard_map/ppermute | solution.py:418
  71.3 39.2 %all-to-all-start.1 = ((f32[64,32,256]{2,1,0:T(8,128)}), f32[64,32,256]{2,1,0:T(8,128)}, u32[]{:S(2)}, u32[]{:S(2)}) async-start(f32[64,32,256]{2,1,0:T(8,128)} %bitcast.64), calls=%async_computation.1 | async-start | bytes 4194304 | tf_op jit(solution)/shard_map/all_to_all | solution.py:314
  82.8 14.0 %collective-permute-start.7 = (f32[1024,256]{1,0:T(8,128)}, f32[1024,256]{1,0:T(8,128)}, u32[]{:S(2)}, u32[]{:S(2)}) collective-permute-start(f32[1024,256]{1,0:T(8,128)} %shard_map.101), channel_id=1, source_target_pairs={{0,8},{8,0},{1,9},{9,1},{2,10},{10,2},{3,11},{11,3},{4,12},{12,4},... | collective-permute-start | bytes 3145736 | tf_op jit(solution)/shard_map/ppermute | solution.py:421
  92.6 17.8 %collective-permute-start.5 = (f32[2,64,256]{2,1,0:T(8,128)S(1)}, f32[2,64,256]{2,1,0:T(8,128)S(1)}, u32[]{:S(2)}, u32[]{:S(2)}) collective-permute-start(f32[2,64,256]{2,1,0:T(8,128)S(1)} %get-tuple-element.70), channel_id=1, source_target_pairs={{0,3},{1,2},{2,1},{3,0},{4,7},{5,6},{6,5},{7,4},{8,11},{9,10},{10,... | collective-permute-start | bytes 393224 | tf_op jit(solution)/shard_map/ppermute | solution.py:342
  95.3 15.1 %collective-permute-start.4 = (f32[2,64,256]{2,1,0:T(8,128)S(1)}, f32[2,64,256]{2,1,0:T(8,128)S(1)}, u32[]{:S(2)}, u32[]{:S(2)}) collective-permute-start(f32[2,64,256]{2,1,0:T(8,128)S(1)} %get-tuple-element.71), channel_id=1, source_target_pairs={{0,2},{1,3},{2,0},{3,1},{4,6},{5,7},{6,4},{7,5},{8,10},{9,11},{10,... | collective-permute-start | bytes 393224 | tf_op jit(solution)/shard_map/ppermute | solution.py:342
  96.2 14.3 %collective-permute-start.3 = (f32[2,64,256]{2,1,0:T(8,128)S(1)}, f32[2,64,256]{2,1,0:T(8,128)S(1)}, u32[]{:S(2)}, u32[]{:S(2)}) collective-permute-start(f32[2,64,256]{2,1,0:T(8,128)S(1)} %get-tuple-element.69), channel_id=1, source_target_pairs={{0,1},{1,0},{2,3},{3,2},{4,5},{5,4},{6,7},{7,6},{8,9},{9,8},{10,11... | collective-permute-start | bytes 393224 | tf_op jit(solution)/shard_map/ppermute | solution.py:342
  110.5 22.2 %all-to-all-start.2 = ((f32[8,128,256]{2,1,0:T(8,128)}), f32[8,128,256]{2,1,0:T(8,128)S(1)}, u32[]{:S(2)}, u32[]{:S(2)}) async-start(f32[8,128,256]{2,1,0:T(8,128)} %bitcast.36), calls=%async_computation.2 | async-start | bytes 2097152 | tf_op jit(solution)/shard_map/all_to_all | solution.py:314
  117.3 13.0 %collective-permute-start.6 = (f32[64,256]{1,0:T(8,128)S(1)}, f32[64,256]{1,0:T(8,128)S(1)}, u32[]{:S(2)}, u32[]{:S(2)}) collective-permute-start(f32[64,256]{1,0:T(8,128)S(1)} %get-tuple-element.72), channel_id=1, source_target_pairs={{0,4},{4,0},{1,5},{5,1},{2,6},{6,2},{3,7},{7,3},{8,12},{12,8},{9,1... | collective-permute-start | bytes 196616 | tf_op jit(solution)/shard_map/ppermute | solution.py:342

commit v5 on v4

--- a/solution.py
+++ b/solution.py
@@ -9,7 +9,8 @@
 
 BF = jnp.bfloat16
 F32 = jnp.float32
-CHIPS = ("y", "zh", "zl", "x")
+CHIPS = ("x", "zl", "zh", "y")
+OWNERS = ("y", "zh", "zl", "x")
 HEAD = ("y", "zh", "c")
 HEAD_CHIPS = ("y", "zh")
 TAIL = ("zl", "x")
@@ -125,14 +126,25 @@
     lax.fori_loop(0, chunks, chunk, 0)
 
 
+def order_of(piece):
+    return (piece % 4) * 2 + piece // 4
+
+
+def slot_order(slot):
+    return (slot & 1) * 4 + (slot >> 1)
+
+
 def split_rels(halves, r_hi, r_lo, copies=None):
     for half, mats in enumerate(halves):
-        count = mats.shape[0]
+        chips, deep = mats.shape[:2]
         if copies:
             copies[half].wait()
-        high, low = split(mats[...])
-        r_hi[half * count : (half + 1) * count, :] = high
-        r_lo[half * count : (half + 1) * count, :] = low
+        for slot in range(8):
+            for piece in range(chips // 8):
+                high, low = split(mats[order_of(piece) * 8 + slot_order(slot)])
+                start = (half * chips + slot * (chips // 8) + piece) * deep
+                r_hi[start : start + deep, :] = high
+                r_lo[start : start + deep, :] = low
 
 
 def keep_half(half, count, first, last, slot):
@@ -193,7 +205,7 @@
     segs, bounds, partial, hv_hi, hv_lo, tv, n_hi, n_lo, rank_col, other, meta,
     f_hi, f_lo, d_hl, r_hi, r_lo, query, pair, f_hl,
 ):
-    width = other.shape[1]
+    width = other.shape[2]
     triples = tv.shape[0]
     batch = triples // 2
     query[...] = partial[...]
@@ -235,7 +247,9 @@
 def rel_body(half, segs, bounds, hvt_hi, hvt_lo, f_hi, f_lo, out):
     width = f_hi.shape[1]
     tile = 256
-    count = out.shape[0] // width
+    chips, deep = out.shape[:2]
+    pieces = width // deep
+    count = chips // pieces
     out[...] = jnp.zeros_like(out)
 
     def one(start, first, last, slot):
@@ -246,8 +260,9 @@
         high = hvt_hi[:, part] * mask
         both = jnp.concatenate([high, hvt_lo[:, part] * mask], axis=0)
         main = dot(both, f_hi[part, :])
-        rows = pl.ds(pl.multiple_of(slot * width, width), width)
-        out[rows, :] += main[:width] + main[width:] + dot(high, f_lo[part, :])
+        total = main[:width] + main[width:] + dot(high, f_lo[part, :])
+        for piece in range(pieces):
+            out[slot * pieces + piece] += total[piece * deep : (piece + 1) * deep]
 
     visits(segs, tile, f_hi.shape[0], one, bounds[half, 0], bounds[half, 1])
 
@@ -309,8 +324,7 @@
 
 
 def exchange(value, axes):
-    devices = lax.axis_size(axes)
-    pieces = value.reshape(devices, value.shape[0] // devices, value.shape[1])
+    pieces = value.reshape(lax.axis_size(axes), -1, value.shape[-1])
     return lax.all_to_all(pieces, axes, split_axis=0, concat_axis=0)
 
 
@@ -359,9 +373,9 @@
     spread, next_index = lax.optimization_barrier((spread, next_index))
     rows = jnp.concatenate([index[0], next_index], axis=1)
     cols = jnp.transpose(rows)
-    own = lax.all_to_all(spread, CHIPS, split_axis=0, concat_axis=0).reshape(-1, width)
+    own = lax.all_to_all(spread, CHIPS, split_axis=0, concat_axis=0)
     slots = slot_of(rows[2], core)
-    rel_count = chips * relations.shape[0] * 2 // width
+    rel_count = 2 * lax.axis_size(HEAD_CHIPS)
     starts = jnp.sum((slots[None, :] < jnp.arange(rel_count)[:, None]).astype(jnp.int32), axis=1)
     by_row = segments(starts, 128, triples)
     by_column = segments(starts, 256, triples)
@@ -386,7 +400,8 @@
         (meta, own, by_row, row_bounds, by_column, bounds)
     )
     other = lax.ppermute(own, "c", SWAP)
-    half_scratch = [pltpu.VMEM(own.shape, BF)] * 2
+    half_rows = own.shape[0] * own.shape[1]
+    half_scratch = [pltpu.VMEM((half_rows, width), BF)] * 2
     plain = shape(triples, width)
     ready = call(
         query_body,
@@ -420,13 +435,13 @@
     tail_theirs = tail_part(1, after(core, rel_own))
     tail_came = lax.ppermute(tail_theirs, "c", SWAP)
     rel_sum = rel_own + rel_came
-    rel_pieces = exchange(rel_sum, CHIPS)
+    rel_pieces = exchange(rel_sum, OWNERS)
 
     tail_mine = tail_part(0, after(core, rel_sum))
     head_grad = call(
         head_body,
         shape(*heads.shape),
-        [pltpu.VMEM((2 * own.shape[0], width), BF)] * 2
+        [pltpu.VMEM((2 * half_rows, width), BF)] * 2
         + [pltpu.VMEM((triples, width), F32), pltpu.VMEM((triples, 2 * width), BF)],
         (after(by_row, tail_mine), f_hi, f_lo, own, other, meta),
         smem=1,
@@ -435,7 +450,7 @@
     )
     pieces = head_grad.reshape(lax.axis_size("zl"), lax.axis_size("x"), -1, width)
     pieces = permute_sum(jnp.swapaxes(pieces, 0, 1), "x")
-    tail_sum = after(tail_mine + tail_came, (pieces, rel_pieces))
+    tail_sum = after(tail_mine + tail_came, (head_grad, rel_pieces))
     tail_share = jnp.sum(exchange(tail_sum, HEAD_CHIPS), axis=0)
     rel_share = jnp.sum(rel_pieces, axis=0)
     head_share = permute_sum(pieces, "zl", rel_share)

time: 134 us -> 131 us (0.978)
  starting transfers between devices: 36.5 us -> 34 us
    all_to_all x2, waiting for transfers between devices: 1.78 us -> 18.6 us  [exchange(): return lax.all_to_all(pieces, axes, split_axis=0, concat_axis=0)]
    ppermute x4, waiting for transfers between devices: 21.3 us -> 6.1 us  [permute_sum(): total += lax.ppermute(piece, axis, [(i, i ^ k) for i in range(devices)])]
    all_to_all x2, starting transfers between devices: 14.9 us -> 13 us  [exchange(): return lax.all_to_all(pieces, axes, split_axis=0, concat_axis=0)]
    all_to_all x1, waiting for transfers between devices: 2.56 us -> 1.18 us  [per_device(): own = lax.all_to_all(spread, CHIPS, split_axis=0, concat_axis=0)]
  transfers between devices with their start and end apart: 11 -> 11, of which waited for: 7 -> 9; matrix products, arithmetic and copies ran while one was open for 7% -> 6% of each run, Pallas kernels for 21% -> 21%
where the time goes in v5:
time: 131 us; the launch traced here: 130 us
  Pallas kernels  37.6 us (29%)
  starting transfers between devices  34 us (26%)
  waiting for transfers between devices  29.5 us (23%)
  other arithmetic  11.3 us (9%)
  local copies, waits for them, and re-layouts  9.93 us (8%)
  between operations  7.52 us (6%)
    pallas_call x8, Pallas kernels, call(): pl.pallas_call(body, out_shape=out_shape, in_specs=[pl.BlockSpec(memory_s...  37.6 us
    all_to_all x2, waiting for transfers between devices, exchange(): return lax.all_to_all(pieces, axes, split_axis=0, concat_axis=0)  18.6 us
    all_to_all x2, starting transfers between devices, exchange(): return lax.all_to_all(pieces, axes, split_axis=0, concat_axis=0)  13 us
    all_to_all x1, starting transfers between devices, per_device(): own = lax.all_to_all(spread, CHIPS, split_axis=0, concat_axis=0)  11.8 us
    unnamed x30, local copies, waits for them, and re-layouts  6.67 us
    ppermute x4, waiting for transfers between devices, permute_sum(): total += lax.ppermute(piece, axis, [(i, i ^ k) for i in range(devices)])  6.1 us
    ppermute x4, starting transfers between devices, permute_sum(): total += lax.ppermute(piece, axis, [(i, i ^ k) for i in range(devices)])  4.8 us
    ppermute x1, starting transfers between devices, per_device(): lax.ppermute(index[1], TAIL, [(i, (i - 1) % behind) for i in range(behind)])  4.26 us
  transfers between devices with their start and end apart: 11, of which 9 were waited for; matrix products, arithmetic and copies ran while one was open for 6% of the time, Pallas kernels for 21%

profile of v5, /device:TPU:0, one launch (start us, length us, event | category | flops | bytes accessed | tf_op | source)
XLA Modules:
  0.0 129.8 jit_solution(13428268108661896906)
XLA Ops:
  0.6 0.8 pad_add_fusion.1
  1.4 4.3 %collective-permute-start = (s32[4,512]{1,0:T(4,128)S(1)}, s32[4,512]{1,0:T(4,128)S(1)}, u32[]{:S(2)}, u32[]{:S(2)}) collective-permute-start(s32[4,512]{1,0:T(4,128)S(1)} %get-tuple-element.77), channel_id=1, source_target_pairs={{0,7},{1,0},{2,1},{3,2},{4,3},{5,4},{6,5},{7,6},{8,15},{9,8},{10,9... | collective-permute-start | bytes 24584 | tf_op jit(solution)/shard_map/ppermute | solution.py:368
  5.7 1.4 %collective-permute-done = s32[4,512]{1,0:T(4,128)S(1)} collective-permute-done((s32[4,512]{1,0:T(4,128)S(1)}, s32[4,512]{1,0:T(4,128)S(1)}, u32[]{:S(2)}, u32[]{:S(2)}) %collective-permute-start) | collective-permute-done | bytes 8224 | tf_op jit(solution)/shard_map/ppermute | solution.py:368
  7.0 2.3 %broadcast_in_dim.41 = f32[64,32,256]{2,1,0:T(8,128)} broadcast(f32[32,256]{1,0:T(8,128)} %param.9), dimensions={1,2} | broadcast | bytes 2129920 | tf_op jit(solution)/shard_map/broadcast_in_dim | solution.py:372
  9.4 0.1 convert_reduce_fusion
  9.5 0.6 slice.37
  10.2 11.8 %all-to-all-start = ((f32[64,32,256]{2,1,0:T(8,128)}), f32[64,32,256]{2,1,0:T(8,128)}, u32[]{:S(2)}, u32[]{:S(2)}) async-start(f32[64,32,256]{2,1,0:T(8,128)} %broadcast_in_dim.41), calls=%async_computation | async-start | bytes 4194304 | tf_op jit(solution)/shard_map/all_to_all | solution.py:376
  22.1 0.2 convert_reduce_fusion.2
  22.4 1.3 fusion.10
  27.0 0.2 convert_reduce_fusion.1
  27.1 0.1 select_reduce_fusion
  27.3 1.3 fusion.11
  31.8 0.2 copy.11.cols
  32.2 9.0 %shard_map.94 = (bf16[1024,256]{1,0:T(8,128)(2,1)S(1)}, bf16[1024,256]{1,0:T(8,128)(2,1)S(1)}, bf16[256,1024]{1,0:T(8,128)(2,1)S(1)}, bf16[256,1024]{1,0:T(8,128...) custom-call(s32[1]{0:T(128)} %bitcast.core_ref, ...), custom_call_target="tpu_custom_call" | custom-call | tf_op jit(solution)/shard_map/pallas_call | solution.py:47
  41.2 0.8 copy-done.3
  42.0 0.8 copy-done.5
  42.7 1.0 copy-done.8
  43.7 0.8 copy-done.9
  44.5 0.8 copy-done.10
  45.3 0.8 copy-done.11
  46.1 0.8 copy-done.12
  47.0 0.8 copy-done.13
  48.3 1.2 all-to-all-done.own_at
  49.5 3.7 %shard_map.95 = (f32[1024,256]{1,0:T(8,128)S(1)}, bf16[1024,256]{1,0:T(8,128)(2,1)S(1)}, bf16[1024,256]{1,0:T(8,128)(2,1)S(1)}, f32[1024,256]{1,0:T(8,128)S(1)},...) custom-call(s32[3,24]{1,0:T(4,128)S(1)} %pad_add_fusion.2.segs, ...), custom_call_target="tpu_custom_call" | custom-call | tf_op jit(solution)/shard_map/pallas_call | solution.py:47
  53.2 0.7 collective-permute-done.1.other.other_at
  53.9 7.7 %shard_map.96 = (bf16[1024,256]{1,0:T(8,128)(2,1)S(1)}, bf16[1024,256]{1,0:T(8,128)(2,1)S(1)}, bf16[2048,512]{1,0:T(8,128)(2,1)S(1)}) custom-call(s32[3,24]{1,0:T(4,128)S(1)} %pad_add_fusion.2.segs, s32[2,2]{1,0:T(2,128)S(1)} %get-tuple-element.44.bounds, f32[1024,256]{1,0:T(8,128)S(1)} %get-tuple-element.52.partial, ...), custom_call_target="tpu_custom_call" | custom-call | tf_op jit(solution)/shard_map/pallas_call | solution.py:47
  61.6 2.6 %shard_map.97 = f32[64,32,256]{2,1,0:T(8,128)S(1)} custom-call(s32[3,20]{1,0:T(4,128)S(1)} %pad_add_fusion.3.segs, s32[2,2]{1,0:T(2,128)S(1)} %get-tuple-element.62.bounds, bf16[256,1024]{1,0:T(8,128)(2,1)S(1)} %copy-done.4, bf16[256,1024]{1,0:T(8,128)(2,1)S(1)} %copy-done.6, bf16[1024,256]{1,0:T(8,128)(2,1)S(1)} %get-tuple-element.60.f_hi.f_hi_at, ...), custom_call_target="tpu_custom_call" | custom-call | tf_op jit(solution)/shard_map/pallas_call | solution.py:47
  64.3 2.6 %shard_map.98 = f32[64,32,256]{2,1,0:T(8,128)S(1)} custom-call(s32[3,20]{1,0:T(4,128)S(1)} %pad_add_fusion.3.segs, s32[2,2]{1,0:T(2,128)S(1)} %get-tuple-element.62.bounds, bf16[256,1024]{1,0:T(8,128)(2,1)S(1)} %copy-done.4, bf16[256,1024]{1,0:T(8,128)(2,1)S(1)} %copy-done.6, bf16[1024,256]{1,0:T(8,128)(2,1)S(1)} %get-tuple-element.60.f_hi.f_hi_at, ...), custom_call_target="tpu_custom_call" | custom-call | tf_op jit(solution)/shard_map/pallas_call | solution.py:47
  66.9 1.6 %collective-permute-done.2 = f32[64,32,256]{2,1,0:T(8,128)S(1)} collective-permute-done((f32[64,32,256]{2,1,0:T(8,128)S(1)}, f32[64,32,256]{2,1,0:T(8,128)S(1)}, u32[]{:S(2)}, u32[]{:S(2)}) %collective-permute-start.2) | collective-permute-done | bytes 2097184 | tf_op jit(solution)/shard_map/ppermute | solution.py:433
  68.5 1.7 %add.55 = f32[64,32,256]{2,1,0:T(8,128)} add(f32[64,32,256]{2,1,0:T(8,128)S(1)} %shard_map.98, f32[64,32,256]{2,1,0:T(8,128)S(1)} %collective-permute-done.2) | non-fusion elementwise | flops 524288 | bytes 6291456 | tf_op jit(solution)/shard_map/add | solution.py:437
  70.2 9.4 %all-to-all-start.1 = ((f32[64,32,256]{2,1,0:T(8,128)}), f32[64,32,256]{2,1,0:T(8,128)}, u32[]{:S(2)}, u32[]{:S(2)}) async-start(f32[64,32,256]{2,1,0:T(8,128)} %add.55), calls=%async_computation.1 | async-start | bytes 4194304 | tf_op jit(solution)/shard_map/all_to_all | solution.py:328
  79.6 2.5 %shard_map.101 = f32[1024,256]{1,0:T(8,128)S(1)} custom-call(s32[1]{0:T(128)} %bitcast.core_ref, s32[4,1024]{1,0:T(4,128)S(1)} %get-tuple-element.74.rows_ref, bf16[2048,512]{1,0:T(8,128)(2,1)S(1)} %get-tuple-element.64.d_hl), custom_call_target="tpu_custom_call" | custom-call | tf_op jit(solution)/shard_map/pallas_call | solution.py:47
  82.2 2.5 %shard_map.99 = f32[1024,256]{1,0:T(8,128)S(1)} custom-call(s32[1]{0:T(128)} %bitcast.core_ref, s32[4,1024]{1,0:T(4,128)S(1)} %get-tuple-element.74.rows_ref, bf16[2048,512]{1,0:T(8,128)(2,1)S(1)} %get-tuple-element.64.d_hl), custom_call_target="tpu_custom_call" | custom-call | tf_op jit(solution)/shard_map/pallas_call | solution.py:47
  84.8 7.1 %shard_map.100 = f32[512,256]{1,0:T(8,128)S(1)} custom-call(s32[3,24]{1,0:T(4,128)S(1)} %pad_add_fusion.2.segs, bf16[1024,256]{1,0:T(8,128)(2,1)} %copy-done.1, bf16[1024,256]{1,0:T(8,128)(2,1)} %copy-done.2, f32[64,32,256]{2,1,0:T(8,128)} %all-to-all-done.own_at, f32[64,32,256]{2,1,0:T(8,128)} %copy-done, s32[2,1024]{1,0:T(2,128)S(1)} %get-tuple-element.59.meta), custom_call_target="tpu_custom_call" | custom-call | tf_op jit(solution)/shard_map/pallas_call | solution.py:47
  91.9 1.1 add.66
  93.0 17.4 %all-to-all-done.1 = f32[64,32,256]{2,1,0:T(8,128)} async-done(((f32[64,32,256]{2,1,0:T(8,128)}), f32[64,32,256]{2,1,0:T(8,128)}, u32[]{:S(2)}, u32[]{:S(2)}) %all-to-all-start.1) | async-done | bytes 2097184 | tf_op jit(solution)/shard_map/all_to_all | solution.py:328
  110.3 3.6 %all-to-all-start.2 = ((f32[8,128,256]{2,1,0:T(8,128)}), f32[8,128,256]{2,1,0:T(8,128)S(1)}, u32[]{:S(2)}, u32[]{:S(2)}) async-start(f32[8,128,256]{2,1,0:T(8,128)} %bitcast.34), calls=%async_computation.2 | async-start | bytes 2097152 | tf_op jit(solution)/shard_map/all_to_all | solution.py:328
  114.0 0.3 collective-permute-start.5
  114.3 1.7 %collective-permute-start.4 = (f32[2,64,256]{2,1,0:T(8,128)S(1)}, f32[2,64,256]{2,1,0:T(8,128)S(1)}, u32[]{:S(2)}, u32[]{:S(2)}) collective-permute-start(f32[2,64,256]{2,1,0:T(8,128)S(1)} %get-tuple-element.71), channel_id=1, source_target_pairs={{0,2},{1,3},{2,0},{3,1},{4,6},{5,7},{6,4},{7,5},{8,10},{9,11},{10,... | collective-permute-start | bytes 393224 | tf_op jit(solution)/shard_map/ppermute | solution.py:356
  116.1 2.1 %collective-permute-start.3 = (f32[2,64,256]{2,1,0:T(8,128)S(1)}, f32[2,64,256]{2,1,0:T(8,128)S(1)}, u32[]{:S(2)}, u32[]{:S(2)}) collective-permute-start(f32[2,64,256]{2,1,0:T(8,128)S(1)} %get-tuple-element.69), channel_id=1, source_target_pairs={{0,1},{1,0},{2,3},{3,2},{4,5},{5,4},{6,7},{7,6},{8,9},{9,8},{10,11... | collective-permute-start | bytes 393224 | tf_op jit(solution)/shard_map/ppermute | solution.py:356
  118.2 3.5 %collective-permute-done.5 = f32[2,64,256]{2,1,0:T(8,128)S(1)} collective-permute-done((f32[2,64,256]{2,1,0:T(8,128)S(1)}, f32[2,64,256]{2,1,0:T(8,128)S(1)}, u32[]{:S(2)}, u32[]{:S(2)}) %collective-permute-start.5) | collective-permute-done | bytes 131104 | tf_op jit(solution)/shard_map/ppermute | solution.py:356
  121.6 0.9 collective-permute-done.3
  122.6 0.6 collective-permute-start.6
  123.2 2.3 %reduce_sum.108 = f32[32,256]{1,0:T(8,128)} reduce(f32[64,32,256]{2,1,0:T(8,128)} %all-to-all-done.1, f32[]{:T(128)} %constant.90.clone.1), dimensions={0}, to_apply=%region_9.10 | reduce | flops 516096 | bytes 2129924 | tf_op jit(solution)/shard_map/reduce_sum | solution.py:455
  125.5 1.8 %collective-permute-done.6 = f32[64,256]{1,0:T(8,128)S(1)} collective-permute-done((f32[64,256]{1,0:T(8,128)S(1)}, f32[64,256]{1,0:T(8,128)S(1)}, u32[]{:S(2)}, u32[]{:S(2)}) %collective-permute-start.6) | collective-permute-done | bytes 65568 | tf_op jit(solution)/shard_map/ppermute | solution.py:356
  127.3 0.6 add_bitcast_fusion
  127.9 1.2 all-to-all-done.2
  129.1 0.7 reduce_sum.109
  (50 shorter events, 1.2 us)
Async XLA Ops:
  1.4 5.6 %collective-permute-start = (s32[4,512]{1,0:T(4,128)S(1)}, s32[4,512]{1,0:T(4,128)S(1)}, u32[]{:S(2)}, u32[]{:S(2)}) collective-permute-start(s32[4,512]{1,0:T(4,128)S(1)} %get-tuple-element.77), channel_id=1, source_target_pairs={{0,7},{1,0},{2,1},{3,2},{4,3},{5,4},{6,5},{7,6},{8,15},{9,8},{10,9... | collective-permute-start | bytes 24584 | tf_op jit(solution)/shard_map/ppermute | solution.py:368
  10.2 22.0 %copy-start.7 = (f32[1,2048,256]{2,1,0:T(8,128)S(1)}, f32[1,2048,256]{2,1,0:T(8,128)}, u32[]{:S(2)}) copy-start(f32[1,2048,256]{2,1,0:T(8,128)} %param.8) | copy-start | bytes 6291460
  10.2 22.0 %copy-start.14 = (f32[1,512,256]{2,1,0:T(8,128)S(1)}, f32[1,512,256]{2,1,0:T(8,128)}, u32[]{:S(2)}) copy-start(f32[1,512,256]{2,1,0:T(8,128)} %param.7) | copy-start | bytes 1572868
  10.2 39.3 %all-to-all-start = ((f32[64,32,256]{2,1,0:T(8,128)}), f32[64,32,256]{2,1,0:T(8,128)}, u32[]{:S(2)}, u32[]{:S(2)}) async-start(f32[64,32,256]{2,1,0:T(8,128)} %broadcast_in_dim.41), calls=%async_computation | async-start | bytes 4194304 | tf_op jit(solution)/shard_map/all_to_all | solution.py:376
  41.1 0.8 copy-start.3
  42.0 0.8 copy-start.5
  42.7 1.0 copy-start.8
  43.7 0.8 copy-start.9
  44.5 0.8 copy-start.10
  45.3 0.8 copy-start.11
  46.1 0.8 copy-start.12
  47.0 0.8 copy-start.13
  49.5 4.4 %collective-permute-start.1 = (f32[64,32,256]{2,1,0:T(8,128)}, f32[64,32,256]{2,1,0:T(8,128)S(1)}, u32[]{:S(2)}, u32[]{:S(2)}) collective-permute-start(f32[64,32,256]{2,1,0:T(8,128)} %all-to-all-done.own_at), channel_id=1, source_target_pairs={{0,8},{8,0},{1,9},{9,1},{2,10},{10,2},{3,11},{11,3},{4,12},{12,4},... | collective-permute-start | bytes 6291464 | tf_op jit(solution)/shard_map/ppermute | solution.py:402
  53.9 7.7 %copy-start = (f32[64,32,256]{2,1,0:T(8,128)}, f32[64,32,256]{2,1,0:T(8,128)S(1)}, u32[]{:S(2)}) copy-start(f32[64,32,256]{2,1,0:T(8,128)S(1)} %collective-permute-done.1.other.other_at) | copy-start | bytes 6291460
  53.9 7.7 %copy-start.4 = (bf16[256,1024]{1,0:T(8,128)(2,1)S(1)}, bf16[256,1024]{1,0:T(8,128)(2,1)}, u32[]{:S(2)}) copy-start(bf16[256,1024]{1,0:T(8,128)(2,1)} %copy-done.3) | copy-start | bytes 1572868
  53.9 7.8 %copy-start.6 = (bf16[256,1024]{1,0:T(8,128)(2,1)S(1)}, bf16[256,1024]{1,0:T(8,128)(2,1)}, u32[]{:S(2)}) copy-start(bf16[256,1024]{1,0:T(8,128)(2,1)} %copy-done.5) | copy-start | bytes 1572868
  61.6 2.7 %copy-start.1 = (bf16[1024,256]{1,0:T(8,128)(2,1)}, bf16[1024,256]{1,0:T(8,128)(2,1)S(1)}, u32[]{:S(2)}) copy-start(bf16[1024,256]{1,0:T(8,128)(2,1)S(1)} %get-tuple-element.60.f_hi.f_hi_at) | copy-start | bytes 1572868
  61.6 2.7 %copy-start.2 = (bf16[1024,256]{1,0:T(8,128)(2,1)}, bf16[1024,256]{1,0:T(8,128)(2,1)S(1)}, u32[]{:S(2)}) copy-start(bf16[1024,256]{1,0:T(8,128)(2,1)S(1)} %get-tuple-element.61.f_lo.f_lo_at) | copy-start | bytes 1572868
  64.2 4.2 %collective-permute-start.2 = (f32[64,32,256]{2,1,0:T(8,128)S(1)}, f32[64,32,256]{2,1,0:T(8,128)S(1)}, u32[]{:S(2)}, u32[]{:S(2)}) collective-permute-start(f32[64,32,256]{2,1,0:T(8,128)S(1)} %shard_map.97), channel_id=1, source_target_pairs={{0,8},{8,0},{1,9},{9,1},{2,10},{10,2},{3,11},{11,3},{4,12},{12,4},... | collective-permute-start | bytes 6291464 | tf_op jit(solution)/shard_map/ppermute | solution.py:433
  70.2 40.1 %all-to-all-start.1 = ((f32[64,32,256]{2,1,0:T(8,128)}), f32[64,32,256]{2,1,0:T(8,128)}, u32[]{:S(2)}, u32[]{:S(2)}) async-start(f32[64,32,256]{2,1,0:T(8,128)} %add.55), calls=%async_computation.1 | async-start | bytes 4194304 | tf_op jit(solution)/shard_map/all_to_all | solution.py:328
  82.2 9.7 %collective-permute-start.7 = (f32[1024,256]{1,0:T(8,128)S(1)}, f32[1024,256]{1,0:T(8,128)S(1)}, u32[]{:S(2)}, u32[]{:S(2)}) collective-permute-start(f32[1024,256]{1,0:T(8,128)S(1)} %shard_map.101), channel_id=1, source_target_pairs={{0,8},{8,0},{1,9},{9,1},{2,10},{10,2},{3,11},{11,3},{4,12},{12,4},... | collective-permute-start | bytes 3145736 | tf_op jit(solution)/shard_map/ppermute | solution.py:436
  110.3 18.8 %all-to-all-start.2 = ((f32[8,128,256]{2,1,0:T(8,128)}), f32[8,128,256]{2,1,0:T(8,128)S(1)}, u32[]{:S(2)}, u32[]{:S(2)}) async-start(f32[8,128,256]{2,1,0:T(8,128)} %bitcast.34), calls=%async_computation.2 | async-start | bytes 2097152 | tf_op jit(solution)/shard_map/all_to_all | solution.py:328
  114.0 7.7 %collective-permute-start.5 = (f32[2,64,256]{2,1,0:T(8,128)S(1)}, f32[2,64,256]{2,1,0:T(8,128)S(1)}, u32[]{:S(2)}, u32[]{:S(2)}) collective-permute-start(f32[2,64,256]{2,1,0:T(8,128)S(1)} %get-tuple-element.70), channel_id=1, source_target_pairs={{0,3},{1,2},{2,1},{3,0},{4,7},{5,6},{6,5},{7,4},{8,11},{9,10},{10,... | collective-permute-start | bytes 393224 | tf_op jit(solution)/shard_map/ppermute | solution.py:356
  114.3 7.3 %collective-permute-start.4 = (f32[2,64,256]{2,1,0:T(8,128)S(1)}, f32[2,64,256]{2,1,0:T(8,128)S(1)}, u32[]{:S(2)}, u32[]{:S(2)}) collective-permute-start(f32[2,64,256]{2,1,0:T(8,128)S(1)} %get-tuple-element.71), channel_id=1, source_target_pairs={{0,2},{1,3},{2,0},{3,1},{4,6},{5,7},{6,4},{7,5},{8,10},{9,11},{10,... | collective-permute-start | bytes 393224 | tf_op jit(solution)/shard_map/ppermute | solution.py:356
  116.1 6.4 %collective-permute-start.3 = (f32[2,64,256]{2,1,0:T(8,128)S(1)}, f32[2,64,256]{2,1,0:T(8,128)S(1)}, u32[]{:S(2)}, u32[]{:S(2)}) collective-permute-start(f32[2,64,256]{2,1,0:T(8,128)S(1)} %get-tuple-element.69), channel_id=1, source_target_pairs={{0,1},{1,0},{2,3},{3,2},{4,5},{5,4},{6,7},{7,6},{8,9},{9,8},{10,11... | collective-permute-start | bytes 393224 | tf_op jit(solution)/shard_map/ppermute | solution.py:356
  122.6 4.7 %collective-permute-start.6 = (f32[64,256]{1,0:T(8,128)S(1)}, f32[64,256]{1,0:T(8,128)S(1)}, u32[]{:S(2)}, u32[]{:S(2)}) collective-permute-start(f32[64,256]{1,0:T(8,128)S(1)} %get-tuple-element.72), channel_id=1, source_target_pairs={{0,4},{4,0},{1,5},{5,1},{2,6},{6,2},{3,7},{7,3},{8,12},{12,8},{9,1... | collective-permute-start | bytes 196616 | tf_op jit(solution)/shard_map/ppermute | solution.py:356

commit v6 on v5

--- a/solution.py
+++ b/solution.py
@@ -374,13 +374,6 @@
     rows = jnp.concatenate([index[0], next_index], axis=1)
     cols = jnp.transpose(rows)
     own = lax.all_to_all(spread, CHIPS, split_axis=0, concat_axis=0)
-    slots = slot_of(rows[2], core)
-    rel_count = 2 * lax.axis_size(HEAD_CHIPS)
-    starts = jnp.sum((slots[None, :] < jnp.arange(rel_count)[:, None]).astype(jnp.int32), axis=1)
-    by_row = segments(starts, 128, triples)
-    by_column = segments(starts, 256, triples)
-    row_bounds = half_bounds(by_row, starts)
-    bounds = half_bounds(by_column, starts)
     wide = shape(triples, width, dtype=BF)
     high = shape(width, triples, dtype=BF)
     gathered = call(
@@ -396,6 +389,13 @@
         smem=1,
     )
     hv_hi, hv_lo, hvt_hi, hvt_lo, tv, n_hi, n_lo, rank_col, meta = gathered
+    slots = slot_of(after(rows[2], meta), core)
+    rel_count = 2 * lax.axis_size(HEAD_CHIPS)
+    starts = jnp.sum((slots[None, :] < jnp.arange(rel_count)[:, None]).astype(jnp.int32), axis=1)
+    by_row = segments(starts, 128, triples)
+    by_column = segments(starts, 256, triples)
+    row_bounds = half_bounds(by_row, starts)
+    bounds = half_bounds(by_column, starts)
     meta, own, by_row, row_bounds, by_column, bounds = lax.optimization_barrier(
         (meta, own, by_row, row_bounds, by_column, bounds)
     )

time: 131 us -> 131 us (level)
  transfers between devices with their start and end apart: 11 -> 11, of which waited for: 9 -> 9; matrix products, arithmetic and copies ran while one was open for 6% -> 7% of each run, Pallas kernels for 21% -> 21%
where the time goes in v6:
time: 131 us; the launch traced here: 130 us
  Pallas kernels  37.9 us (29%)
  starting transfers between devices  34.6 us (26%)
  waiting for transfers between devices  28.9 us (22%)
  other arithmetic  11.5 us (9%)
  local copies, waits for them, and re-layouts  9.93 us (8%)
  between operations  7.5 us (6%)
    pallas_call x8, Pallas kernels, call(): pl.pallas_call(body, out_shape=out_shape, in_specs=[pl.BlockSpec(memory_s...  37.9 us
    all_to_all x2, waiting for transfers between devices, exchange(): return lax.all_to_all(pieces, axes, split_axis=0, concat_axis=0)  18.5 us
    all_to_all x2, starting transfers between devices, exchange(): return lax.all_to_all(pieces, axes, split_axis=0, concat_axis=0)  13.5 us
    all_to_all x1, starting transfers between devices, per_device(): own = lax.all_to_all(spread, CHIPS, split_axis=0, concat_axis=0)  11.8 us
    unnamed x30, local copies, waits for them, and re-layouts  6.67 us
    ppermute x4, waiting for transfers between devices, permute_sum(): total += lax.ppermute(piece, axis, [(i, i ^ k) for i in range(devices)])  6.1 us
    ppermute x4, starting transfers between devices, permute_sum(): total += lax.ppermute(piece, axis, [(i, i ^ k) for i in range(devices)])  4.8 us
    ppermute x1, starting transfers between devices, per_device(): lax.ppermute(index[1], TAIL, [(i, (i - 1) % behind) for i in range(behind)])  4.26 us
  transfers between devices with their start and end apart: 11, of which 9 were waited for; matrix products, arithmetic and copies ran while one was open for 7% of the time, Pallas kernels for 21%

profile of v6, /device:TPU:0, one launch (start us, length us, event | category | flops | bytes accessed | tf_op | source)
XLA Modules:
  0.0 130.3 jit_solution(1530498064766621633)
XLA Ops:
  0.6 0.8 pad_add_fusion.1
  1.4 4.3 %collective-permute-start = (s32[4,512]{1,0:T(4,128)S(1)}, s32[4,512]{1,0:T(4,128)S(1)}, u32[]{:S(2)}, u32[]{:S(2)}) collective-permute-start(s32[4,512]{1,0:T(4,128)S(1)} %get-tuple-element.79), channel_id=1, source_target_pairs={{0,7},{1,0},{2,1},{3,2},{4,3},{5,4},{6,5},{7,6},{8,15},{9,8},{10,9... | collective-permute-start | bytes 24584 | tf_op jit(solution)/shard_map/ppermute | solution.py:368
  5.7 1.4 %collective-permute-done = s32[4,512]{1,0:T(4,128)S(1)} collective-permute-done((s32[4,512]{1,0:T(4,128)S(1)}, s32[4,512]{1,0:T(4,128)S(1)}, u32[]{:S(2)}, u32[]{:S(2)}) %collective-permute-start) | collective-permute-done | bytes 8224 | tf_op jit(solution)/shard_map/ppermute | solution.py:368
  7.0 2.3 %broadcast_in_dim.41 = f32[64,32,256]{2,1,0:T(8,128)} broadcast(f32[32,256]{1,0:T(8,128)} %param.9), dimensions={1,2} | broadcast | bytes 2129920 | tf_op jit(solution)/shard_map/broadcast_in_dim | solution.py:372
  9.4 0.2 copy.11.cols
  9.6 11.8 %all-to-all-start = ((f32[64,32,256]{2,1,0:T(8,128)}), f32[64,32,256]{2,1,0:T(8,128)}, u32[]{:S(2)}, u32[]{:S(2)}) async-start(f32[64,32,256]{2,1,0:T(8,128)} %broadcast_in_dim.41), calls=%async_computation | async-start | bytes 4194304 | tf_op jit(solution)/shard_map/all_to_all | solution.py:376
  21.5 9.0 %shard_map.94 = (bf16[1024,256]{1,0:T(8,128)(2,1)S(1)}, bf16[1024,256]{1,0:T(8,128)(2,1)S(1)}, bf16[256,1024]{1,0:T(8,128)(2,1)S(1)}, bf16[256,1024]{1,0:T(8,128...) custom-call(s32[1]{0:T(128)} %bitcast.core_ref, ...), custom_call_target="tpu_custom_call" | custom-call | tf_op jit(solution)/shard_map/pallas_call | solution.py:47
  30.5 0.8 copy-done.3
  31.3 0.8 copy-done.5
  32.1 1.0 copy-done.8
  33.1 0.8 copy-done.9
  33.9 0.8 copy-done.10
  34.7 0.8 copy-done.11
  35.5 0.8 copy-done.12
  36.3 0.8 copy-done.13
  37.2 0.1 convert_reduce_fusion
  37.4 0.2 convert_reduce_fusion.2
  37.7 0.6 slice.37
  38.3 1.3 fusion.9
  42.9 0.2 convert_reduce_fusion.1
  43.1 0.1 select_reduce_fusion
  43.2 1.3 fusion.10
  48.3 0.6 all-to-all-done.own_at
  49.0 3.7 %shard_map.95 = (f32[1024,256]{1,0:T(8,128)S(1)}, bf16[1024,256]{1,0:T(8,128)(2,1)S(1)}, bf16[1024,256]{1,0:T(8,128)(2,1)S(1)}, f32[1024,256]{1,0:T(8,128)S(1)},...) custom-call(s32[3,24]{1,0:T(4,128)S(1)} %pad_add_fusion.2.segs, ...), custom_call_target="tpu_custom_call" | custom-call | tf_op jit(solution)/shard_map/pallas_call | solution.py:47
  52.7 0.7 collective-permute-done.1.other.other_at
  53.4 7.9 %shard_map.96 = (bf16[1024,256]{1,0:T(8,128)(2,1)S(1)}, bf16[1024,256]{1,0:T(8,128)(2,1)S(1)}, bf16[2048,512]{1,0:T(8,128)(2,1)S(1)}) custom-call(s32[3,24]{1,0:T(4,128)S(1)} %pad_add_fusion.2.segs, s32[2,2]{1,0:T(2,128)S(1)} %get-tuple-element.46.bounds, f32[1024,256]{1,0:T(8,128)S(1)} %get-tuple-element.54.partial, ...), custom_call_target="tpu_custom_call" | custom-call | tf_op jit(solution)/shard_map/pallas_call | solution.py:47
  61.3 2.6 %shard_map.97 = f32[64,32,256]{2,1,0:T(8,128)S(1)} custom-call(s32[3,20]{1,0:T(4,128)S(1)} %pad_add_fusion.3.segs, s32[2,2]{1,0:T(2,128)S(1)} %get-tuple-element.64.bounds, bf16[256,1024]{1,0:T(8,128)(2,1)S(1)} %copy-done.4, bf16[256,1024]{1,0:T(8,128)(2,1)S(1)} %copy-done.6, bf16[1024,256]{1,0:T(8,128)(2,1)S(1)} %get-tuple-element.62.f_hi.f_hi_at, ...), custom_call_target="tpu_custom_call" | custom-call | tf_op jit(solution)/shard_map/pallas_call | solution.py:47
  64.0 2.6 %shard_map.98 = f32[64,32,256]{2,1,0:T(8,128)S(1)} custom-call(s32[3,20]{1,0:T(4,128)S(1)} %pad_add_fusion.3.segs, s32[2,2]{1,0:T(2,128)S(1)} %get-tuple-element.64.bounds, bf16[256,1024]{1,0:T(8,128)(2,1)S(1)} %copy-done.4, bf16[256,1024]{1,0:T(8,128)(2,1)S(1)} %copy-done.6, bf16[1024,256]{1,0:T(8,128)(2,1)S(1)} %get-tuple-element.62.f_hi.f_hi_at, ...), custom_call_target="tpu_custom_call" | custom-call | tf_op jit(solution)/shard_map/pallas_call | solution.py:47
  66.6 1.6 %collective-permute-done.2 = f32[64,32,256]{2,1,0:T(8,128)S(1)} collective-permute-done((f32[64,32,256]{2,1,0:T(8,128)S(1)}, f32[64,32,256]{2,1,0:T(8,128)S(1)}, u32[]{:S(2)}, u32[]{:S(2)}) %collective-permute-start.2) | collective-permute-done | bytes 2097184 | tf_op jit(solution)/shard_map/ppermute | solution.py:433
  68.2 1.9 %add.54 = f32[64,32,256]{2,1,0:T(8,128)} add(f32[64,32,256]{2,1,0:T(8,128)S(1)} %shard_map.98, f32[64,32,256]{2,1,0:T(8,128)S(1)} %collective-permute-done.2) | non-fusion elementwise | flops 524288 | bytes 6291456 | tf_op jit(solution)/shard_map/add | solution.py:437
  70.1 9.9 %all-to-all-start.1 = ((f32[64,32,256]{2,1,0:T(8,128)}), f32[64,32,256]{2,1,0:T(8,128)}, u32[]{:S(2)}, u32[]{:S(2)}) async-start(f32[64,32,256]{2,1,0:T(8,128)} %add.54), calls=%async_computation.1 | async-start | bytes 4194304 | tf_op jit(solution)/shard_map/all_to_all | solution.py:328
  80.0 2.5 %shard_map.101 = f32[1024,256]{1,0:T(8,128)S(1)} custom-call(s32[1]{0:T(128)} %bitcast.core_ref, s32[4,1024]{1,0:T(4,128)S(1)} %get-tuple-element.76.rows_ref, bf16[2048,512]{1,0:T(8,128)(2,1)S(1)} %get-tuple-element.66.d_hl), custom_call_target="tpu_custom_call" | custom-call | tf_op jit(solution)/shard_map/pallas_call | solution.py:47
  82.7 2.5 %shard_map.99 = f32[1024,256]{1,0:T(8,128)S(1)} custom-call(s32[1]{0:T(128)} %bitcast.core_ref, s32[4,1024]{1,0:T(4,128)S(1)} %get-tuple-element.76.rows_ref, bf16[2048,512]{1,0:T(8,128)(2,1)S(1)} %get-tuple-element.66.d_hl), custom_call_target="tpu_custom_call" | custom-call | tf_op jit(solution)/shard_map/pallas_call | solution.py:47
  85.2 7.1 %shard_map.100 = f32[512,256]{1,0:T(8,128)S(1)} custom-call(s32[3,24]{1,0:T(4,128)S(1)} %pad_add_fusion.2.segs, bf16[1024,256]{1,0:T(8,128)(2,1)} %copy-done.1, bf16[1024,256]{1,0:T(8,128)(2,1)} %copy-done.2, f32[64,32,256]{2,1,0:T(8,128)} %all-to-all-done.own_at, f32[64,32,256]{2,1,0:T(8,128)} %copy-done, s32[2,1024]{1,0:T(2,128)S(1)} %get-tuple-element.61.meta), custom_call_target="tpu_custom_call" | custom-call | tf_op jit(solution)/shard_map/pallas_call | solution.py:47
  92.3 1.1 add.65
  93.4 17.3 %all-to-all-done.1 = f32[64,32,256]{2,1,0:T(8,128)} async-done(((f32[64,32,256]{2,1,0:T(8,128)}), f32[64,32,256]{2,1,0:T(8,128)}, u32[]{:S(2)}, u32[]{:S(2)}) %all-to-all-start.1) | async-done | bytes 2097184 | tf_op jit(solution)/shard_map/all_to_all | solution.py:328
  110.8 3.6 %all-to-all-start.2 = ((f32[8,128,256]{2,1,0:T(8,128)}), f32[8,128,256]{2,1,0:T(8,128)S(1)}, u32[]{:S(2)}, u32[]{:S(2)}) async-start(f32[8,128,256]{2,1,0:T(8,128)} %bitcast.34), calls=%async_computation.2 | async-start | bytes 2097152 | tf_op jit(solution)/shard_map/all_to_all | solution.py:328
  114.4 0.3 collective-permute-start.5
  114.7 1.7 %collective-permute-start.4 = (f32[2,64,256]{2,1,0:T(8,128)S(1)}, f32[2,64,256]{2,1,0:T(8,128)S(1)}, u32[]{:S(2)}, u32[]{:S(2)}) collective-permute-start(f32[2,64,256]{2,1,0:T(8,128)S(1)} %get-tuple-element.73), channel_id=1, source_target_pairs={{0,2},{1,3},{2,0},{3,1},{4,6},{5,7},{6,4},{7,5},{8,10},{9,11},{10,... | collective-permute-start | bytes 393224 | tf_op jit(solution)/shard_map/ppermute | solution.py:356
  116.5 2.1 %collective-permute-start.3 = (f32[2,64,256]{2,1,0:T(8,128)S(1)}, f32[2,64,256]{2,1,0:T(8,128)S(1)}, u32[]{:S(2)}, u32[]{:S(2)}) collective-permute-start(f32[2,64,256]{2,1,0:T(8,128)S(1)} %get-tuple-element.71), channel_id=1, source_target_pairs={{0,1},{1,0},{2,3},{3,2},{4,5},{5,4},{6,7},{7,6},{8,9},{9,8},{10,11... | collective-permute-start | bytes 393224 | tf_op jit(solution)/shard_map/ppermute | solution.py:356
  118.6 3.5 %collective-permute-done.5 = f32[2,64,256]{2,1,0:T(8,128)S(1)} collective-permute-done((f32[2,64,256]{2,1,0:T(8,128)S(1)}, f32[2,64,256]{2,1,0:T(8,128)S(1)}, u32[]{:S(2)}, u32[]{:S(2)}) %collective-permute-start.5) | collective-permute-done | bytes 131104 | tf_op jit(solution)/shard_map/ppermute | solution.py:356
  122.1 0.9 collective-permute-done.3
  123.0 0.6 collective-permute-start.6
  123.6 2.3 %reduce_sum.108 = f32[32,256]{1,0:T(8,128)} reduce(f32[64,32,256]{2,1,0:T(8,128)} %all-to-all-done.1, f32[]{:T(128)} %constant.90.clone.1), dimensions={0}, to_apply=%region_9.10 | reduce | flops 516096 | bytes 2129924 | tf_op jit(solution)/shard_map/reduce_sum | solution.py:455
  125.9 1.8 %collective-permute-done.6 = f32[64,256]{1,0:T(8,128)S(1)} collective-permute-done((f32[64,256]{1,0:T(8,128)S(1)}, f32[64,256]{1,0:T(8,128)S(1)}, u32[]{:S(2)}, u32[]{:S(2)}) %collective-permute-start.6) | collective-permute-done | bytes 65568 | tf_op jit(solution)/shard_map/ppermute | solution.py:356
  127.7 0.6 add_bitcast_fusion
  128.3 1.2 all-to-all-done.2
  129.5 0.7 reduce_sum.109
  (51 shorter events, 1.2 us)
Async XLA Ops:
  1.4 5.6 %collective-permute-start = (s32[4,512]{1,0:T(4,128)S(1)}, s32[4,512]{1,0:T(4,128)S(1)}, u32[]{:S(2)}, u32[]{:S(2)}) collective-permute-start(s32[4,512]{1,0:T(4,128)S(1)} %get-tuple-element.79), channel_id=1, source_target_pairs={{0,7},{1,0},{2,1},{3,2},{4,3},{5,4},{6,5},{7,6},{8,15},{9,8},{10,9... | collective-permute-start | bytes 24584 | tf_op jit(solution)/shard_map/ppermute | solution.py:368
  9.6 11.9 %copy-start.7 = (f32[1,2048,256]{2,1,0:T(8,128)S(1)}, f32[1,2048,256]{2,1,0:T(8,128)}, u32[]{:S(2)}) copy-start(f32[1,2048,256]{2,1,0:T(8,128)} %param.8) | copy-start | bytes 6291460
  9.6 11.9 %copy-start.14 = (f32[1,512,256]{2,1,0:T(8,128)S(1)}, f32[1,512,256]{2,1,0:T(8,128)}, u32[]{:S(2)}) copy-start(f32[1,512,256]{2,1,0:T(8,128)} %param.7) | copy-start | bytes 1572868
  9.6 39.4 %all-to-all-start = ((f32[64,32,256]{2,1,0:T(8,128)}), f32[64,32,256]{2,1,0:T(8,128)}, u32[]{:S(2)}, u32[]{:S(2)}) async-start(f32[64,32,256]{2,1,0:T(8,128)} %broadcast_in_dim.41), calls=%async_computation | async-start | bytes 4194304 | tf_op jit(solution)/shard_map/all_to_all | solution.py:376
  30.5 0.8 copy-start.3
  31.3 0.8 copy-start.5
  32.1 1.0 copy-start.8
  33.1 0.8 copy-start.9
  33.9 0.8 copy-start.10
  34.7 0.8 copy-start.11
  35.5 0.8 copy-start.12
  36.3 0.8 copy-start.13
  49.0 4.4 %collective-permute-start.1 = (f32[64,32,256]{2,1,0:T(8,128)}, f32[64,32,256]{2,1,0:T(8,128)S(1)}, u32[]{:S(2)}, u32[]{:S(2)}) collective-permute-start(f32[64,32,256]{2,1,0:T(8,128)} %all-to-all-done.own_at), channel_id=1, source_target_pairs={{0,8},{8,0},{1,9},{9,1},{2,10},{10,2},{3,11},{11,3},{4,12},{12,4},... | collective-permute-start | bytes 6291464 | tf_op jit(solution)/shard_map/ppermute | solution.py:402
  53.4 7.9 %copy-start = (f32[64,32,256]{2,1,0:T(8,128)}, f32[64,32,256]{2,1,0:T(8,128)S(1)}, u32[]{:S(2)}) copy-start(f32[64,32,256]{2,1,0:T(8,128)S(1)} %collective-permute-done.1.other.other_at) | copy-start | bytes 6291460
  53.4 7.9 %copy-start.4 = (bf16[256,1024]{1,0:T(8,128)(2,1)S(1)}, bf16[256,1024]{1,0:T(8,128)(2,1)}, u32[]{:S(2)}) copy-start(bf16[256,1024]{1,0:T(8,128)(2,1)} %copy-done.3) | copy-start | bytes 1572868
  53.4 7.9 %copy-start.6 = (bf16[256,1024]{1,0:T(8,128)(2,1)S(1)}, bf16[256,1024]{1,0:T(8,128)(2,1)}, u32[]{:S(2)}) copy-start(bf16[256,1024]{1,0:T(8,128)(2,1)} %copy-done.5) | copy-start | bytes 1572868
  61.3 2.8 %copy-start.1 = (bf16[1024,256]{1,0:T(8,128)(2,1)}, bf16[1024,256]{1,0:T(8,128)(2,1)S(1)}, u32[]{:S(2)}) copy-start(bf16[1024,256]{1,0:T(8,128)(2,1)S(1)} %get-tuple-element.62.f_hi.f_hi_at) | copy-start | bytes 1572868
  61.3 2.8 %copy-start.2 = (bf16[1024,256]{1,0:T(8,128)(2,1)}, bf16[1024,256]{1,0:T(8,128)(2,1)S(1)}, u32[]{:S(2)}) copy-start(bf16[1024,256]{1,0:T(8,128)(2,1)S(1)} %get-tuple-element.63.f_lo.f_lo_at) | copy-start | bytes 1572868
  63.9 4.2 %collective-permute-start.2 = (f32[64,32,256]{2,1,0:T(8,128)S(1)}, f32[64,32,256]{2,1,0:T(8,128)S(1)}, u32[]{:S(2)}, u32[]{:S(2)}) collective-permute-start(f32[64,32,256]{2,1,0:T(8,128)S(1)} %shard_map.97), channel_id=1, source_target_pairs={{0,8},{8,0},{1,9},{9,1},{2,10},{10,2},{3,11},{11,3},{4,12},{12,4},... | collective-permute-start | bytes 6291464 | tf_op jit(solution)/shard_map/ppermute | solution.py:433
  70.1 40.7 %all-to-all-start.1 = ((f32[64,32,256]{2,1,0:T(8,128)}), f32[64,32,256]{2,1,0:T(8,128)}, u32[]{:S(2)}, u32[]{:S(2)}) async-start(f32[64,32,256]{2,1,0:T(8,128)} %add.54), calls=%async_computation.1 | async-start | bytes 4194304 | tf_op jit(solution)/shard_map/all_to_all | solution.py:328
  82.6 9.8 %collective-permute-start.7 = (f32[1024,256]{1,0:T(8,128)S(1)}, f32[1024,256]{1,0:T(8,128)S(1)}, u32[]{:S(2)}, u32[]{:S(2)}) collective-permute-start(f32[1024,256]{1,0:T(8,128)S(1)} %shard_map.101), channel_id=1, source_target_pairs={{0,8},{8,0},{1,9},{9,1},{2,10},{10,2},{3,11},{11,3},{4,12},{12,4},... | collective-permute-start | bytes 3145736 | tf_op jit(solution)/shard_map/ppermute | solution.py:436
  110.8 18.8 %all-to-all-start.2 = ((f32[8,128,256]{2,1,0:T(8,128)}), f32[8,128,256]{2,1,0:T(8,128)S(1)}, u32[]{:S(2)}, u32[]{:S(2)}) async-start(f32[8,128,256]{2,1,0:T(8,128)} %bitcast.34), calls=%async_computation.2 | async-start | bytes 2097152 | tf_op jit(solution)/shard_map/all_to_all | solution.py:328
  114.4 7.7 %collective-permute-start.5 = (f32[2,64,256]{2,1,0:T(8,128)S(1)}, f32[2,64,256]{2,1,0:T(8,128)S(1)}, u32[]{:S(2)}, u32[]{:S(2)}) collective-permute-start(f32[2,64,256]{2,1,0:T(8,128)S(1)} %get-tuple-element.72), channel_id=1, source_target_pairs={{0,3},{1,2},{2,1},{3,0},{4,7},{5,6},{6,5},{7,4},{8,11},{9,10},{10,... | collective-permute-start | bytes 393224 | tf_op jit(solution)/shard_map/ppermute | solution.py:356
  114.7 7.3 %collective-permute-start.4 = (f32[2,64,256]{2,1,0:T(8,128)S(1)}, f32[2,64,256]{2,1,0:T(8,128)S(1)}, u32[]{:S(2)}, u32[]{:S(2)}) collective-permute-start(f32[2,64,256]{2,1,0:T(8,128)S(1)} %get-tuple-element.73), channel_id=1, source_target_pairs={{0,2},{1,3},{2,0},{3,1},{4,6},{5,7},{6,4},{7,5},{8,10},{9,11},{10,... | collective-permute-start | bytes 393224 | tf_op jit(solution)/shard_map/ppermute | solution.py:356
  116.5 6.4 %collective-permute-start.3 = (f32[2,64,256]{2,1,0:T(8,128)S(1)}, f32[2,64,256]{2,1,0:T(8,128)S(1)}, u32[]{:S(2)}, u32[]{:S(2)}) collective-permute-start(f32[2,64,256]{2,1,0:T(8,128)S(1)} %get-tuple-element.71), channel_id=1, source_target_pairs={{0,1},{1,0},{2,3},{3,2},{4,5},{5,4},{6,7},{7,6},{8,9},{9,8},{10,11... | collective-permute-start | bytes 393224 | tf_op jit(solution)/shard_map/ppermute | solution.py:356
  123.0 4.7 %collective-permute-start.6 = (f32[64,256]{1,0:T(8,128)S(1)}, f32[64,256]{1,0:T(8,128)S(1)}, u32[]{:S(2)}, u32[]{:S(2)}) collective-permute-start(f32[64,256]{1,0:T(8,128)S(1)} %get-tuple-element.74), channel_id=1, source_target_pairs={{0,4},{4,0},{1,5},{5,1},{2,6},{6,2},{3,7},{7,3},{8,12},{12,8},{9,1... | collective-permute-start | bytes 196616 | tf_op jit(solution)/shard_map/ppermute | solution.py:356

commit v7 on v5

--- a/solution.py
+++ b/solution.py
@@ -221,6 +221,7 @@
         high, low = both[:, :width], both[:, width:]
         q = high + low
         q2 = (high.astype(BF), low.astype(BF))
+        both_q = both.astype(BF)
         n2 = (n_hi[rows, :], n_lo[rows, :])
         weights = split(jax.nn.sigmoid(dot3(q2, n2, NT)) * (1.0 / batch))
         vec = tv[rows, :]
@@ -231,7 +232,8 @@
         high, low = split(coef * q)
         d_hl[rows, :width] = high
         d_hl[rows, width:] = low
-        high, low = split(dot3(weights, q2, TN))
+        wide = dot(weights[0], both_q, TN)
+        high, low = split(wide[:, :width] + wide[:, width:] + dot(weights[1], q2[0], TN))
         below = slice(triples + s * batch, triples + (s + 1) * batch)
         d_hl[below, :width] = high
         d_hl[below, width:] = low

time: 131 us -> 131 us (level)
  no operation moved by 1% of the time
where the time goes in v7:
time: 131 us; the launch traced here: 130 us
  Pallas kernels  37.3 us (28%)
  starting transfers between devices  34.4 us (26%)
  waiting for transfers between devices  29.8 us (23%)
  other arithmetic  11.3 us (9%)
  local copies, waits for them, and re-layouts  9.93 us (8%)
  between operations  7.49 us (6%)
    pallas_call x8, Pallas kernels, call(): pl.pallas_call(body, out_shape=out_shape, in_specs=[pl.BlockSpec(memory_s...  37.3 us
    all_to_all x2, waiting for transfers between devices, exchange(): return lax.all_to_all(pieces, axes, split_axis=0, concat_axis=0)  18.7 us
    all_to_all x2, starting transfers between devices, exchange(): return lax.all_to_all(pieces, axes, split_axis=0, concat_axis=0)  13 us
    all_to_all x1, starting transfers between devices, per_device(): own = lax.all_to_all(spread, CHIPS, split_axis=0, concat_axis=0)  11.8 us
    ppermute x4, waiting for transfers between devices, permute_sum(): total += lax.ppermute(piece, axis, [(i, i ^ k) for i in range(devices)])  6.68 us
    unnamed x30, local copies, waits for them, and re-layouts  6.67 us
    ppermute x4, starting transfers between devices, permute_sum(): total += lax.ppermute(piece, axis, [(i, i ^ k) for i in range(devices)])  4.55 us
    ppermute x1, starting transfers between devices, per_device(): lax.ppermute(index[1], TAIL, [(i, (i - 1) % behind) for i in range(behind)])  4.26 us
  transfers between devices with their start and end apart: 11, of which 9 were waited for; matrix products, arithmetic and copies ran while one was open for 6% of the time, Pallas kernels for 21%

profile of v7, /device:TPU:0, one launch (start us, length us, event | category | flops | bytes accessed | tf_op | source)
XLA Modules:
  0.0 130.2 jit_solution(1747902594793239486)
XLA Ops:
  0.6 0.8 pad_add_fusion.1
  1.4 4.3 %collective-permute-start = (s32[4,512]{1,0:T(4,128)S(1)}, s32[4,512]{1,0:T(4,128)S(1)}, u32[]{:S(2)}, u32[]{:S(2)}) collective-permute-start(s32[4,512]{1,0:T(4,128)S(1)} %get-tuple-element.77), channel_id=1, source_target_pairs={{0,7},{1,0},{2,1},{3,2},{4,3},{5,4},{6,5},{7,6},{8,15},{9,8},{10,9... | collective-permute-start | bytes 24584 | tf_op jit(solution)/shard_map/ppermute | solution.py:370
  5.7 1.4 %collective-permute-done = s32[4,512]{1,0:T(4,128)S(1)} collective-permute-done((s32[4,512]{1,0:T(4,128)S(1)}, s32[4,512]{1,0:T(4,128)S(1)}, u32[]{:S(2)}, u32[]{:S(2)}) %collective-permute-start) | collective-permute-done | bytes 8224 | tf_op jit(solution)/shard_map/ppermute | solution.py:370
  7.0 2.3 %broadcast_in_dim.41 = f32[64,32,256]{2,1,0:T(8,128)} broadcast(f32[32,256]{1,0:T(8,128)} %param.9), dimensions={1,2} | broadcast | bytes 2129920 | tf_op jit(solution)/shard_map/broadcast_in_dim | solution.py:374
  9.5 0.6 slice.37
  10.2 11.8 %all-to-all-start = ((f32[64,32,256]{2,1,0:T(8,128)}), f32[64,32,256]{2,1,0:T(8,128)}, u32[]{:S(2)}, u32[]{:S(2)}) async-start(f32[64,32,256]{2,1,0:T(8,128)} %broadcast_in_dim.41), calls=%async_computation | async-start | bytes 4194304 | tf_op jit(solution)/shard_map/all_to_all | solution.py:378
  22.1 0.2 convert_reduce_fusion.2
  22.4 1.3 fusion.10
  27.0 0.2 convert_reduce_fusion.1
  27.3 1.3 fusion.11
  31.8 0.2 copy.11.cols
  32.2 9.0 %shard_map.94 = (bf16[1024,256]{1,0:T(8,128)(2,1)S(1)}, bf16[1024,256]{1,0:T(8,128)(2,1)S(1)}, bf16[256,1024]{1,0:T(8,128)(2,1)S(1)}, bf16[256,1024]{1,0:T(8,128...) custom-call(s32[1]{0:T(128)} %bitcast.core_ref, ...), custom_call_target="tpu_custom_call" | custom-call | tf_op jit(solution)/shard_map/pallas_call | solution.py:47
  41.2 0.8 copy-done.3
  42.0 0.8 copy-done.5
  42.7 1.0 copy-done.8
  43.7 0.8 copy-done.9
  44.5 0.8 copy-done.10
  45.3 0.8 copy-done.11
  46.1 0.8 copy-done.12
  47.0 0.8 copy-done.13
  48.3 1.2 all-to-all-done.own_at
  49.5 3.7 %shard_map.95 = (f32[1024,256]{1,0:T(8,128)S(1)}, bf16[1024,256]{1,0:T(8,128)(2,1)S(1)}, bf16[1024,256]{1,0:T(8,128)(2,1)S(1)}, f32[1024,256]{1,0:T(8,128)S(1)},...) custom-call(s32[3,24]{1,0:T(4,128)S(1)} %pad_add_fusion.2.segs, ...), custom_call_target="tpu_custom_call" | custom-call | tf_op jit(solution)/shard_map/pallas_call | solution.py:47
  53.2 0.7 collective-permute-done.1.other.other_at
  53.9 7.3 %shard_map.96 = (bf16[1024,256]{1,0:T(8,128)(2,1)S(1)}, bf16[1024,256]{1,0:T(8,128)(2,1)S(1)}, bf16[2048,512]{1,0:T(8,128)(2,1)S(1)}) custom-call(s32[3,24]{1,0:T(4,128)S(1)} %pad_add_fusion.2.segs, s32[2,2]{1,0:T(2,128)S(1)} %get-tuple-element.44.bounds, f32[1024,256]{1,0:T(8,128)S(1)} %get-tuple-element.52.partial, ...), custom_call_target="tpu_custom_call" | custom-call | tf_op jit(solution)/shard_map/pallas_call | solution.py:47
  61.2 2.6 %shard_map.97 = f32[64,32,256]{2,1,0:T(8,128)S(1)} custom-call(s32[3,20]{1,0:T(4,128)S(1)} %pad_add_fusion.3.segs, s32[2,2]{1,0:T(2,128)S(1)} %get-tuple-element.62.bounds, bf16[256,1024]{1,0:T(8,128)(2,1)S(1)} %copy-done.4, bf16[256,1024]{1,0:T(8,128)(2,1)S(1)} %copy-done.6, bf16[1024,256]{1,0:T(8,128)(2,1)S(1)} %get-tuple-element.60.f_hi.f_hi_at, ...), custom_call_target="tpu_custom_call" | custom-call | tf_op jit(solution)/shard_map/pallas_call | solution.py:47
  63.9 0.6 collective-permute-start.2
  64.5 2.6 %shard_map.98 = f32[64,32,256]{2,1,0:T(8,128)S(1)} custom-call(s32[3,20]{1,0:T(4,128)S(1)} %pad_add_fusion.3.segs, s32[2,2]{1,0:T(2,128)S(1)} %get-tuple-element.62.bounds, bf16[256,1024]{1,0:T(8,128)(2,1)S(1)} %copy-done.4, bf16[256,1024]{1,0:T(8,128)(2,1)S(1)} %copy-done.6, bf16[1024,256]{1,0:T(8,128)(2,1)S(1)} %get-tuple-element.60.f_hi.f_hi_at, ...), custom_call_target="tpu_custom_call" | custom-call | tf_op jit(solution)/shard_map/pallas_call | solution.py:47
  67.0 1.2 collective-permute-done.2
  68.2 1.7 %add.55 = f32[64,32,256]{2,1,0:T(8,128)} add(f32[64,32,256]{2,1,0:T(8,128)S(1)} %shard_map.98, f32[64,32,256]{2,1,0:T(8,128)S(1)} %collective-permute-done.2) | non-fusion elementwise | flops 524288 | bytes 6291456 | tf_op jit(solution)/shard_map/add | solution.py:439
  70.0 9.4 %all-to-all-start.1 = ((f32[64,32,256]{2,1,0:T(8,128)}), f32[64,32,256]{2,1,0:T(8,128)}, u32[]{:S(2)}, u32[]{:S(2)}) async-start(f32[64,32,256]{2,1,0:T(8,128)} %add.55), calls=%async_computation.1 | async-start | bytes 4194304 | tf_op jit(solution)/shard_map/all_to_all | solution.py:330
  79.4 2.5 %shard_map.101 = f32[1024,256]{1,0:T(8,128)S(1)} custom-call(s32[1]{0:T(128)} %bitcast.core_ref, s32[4,1024]{1,0:T(4,128)S(1)} %get-tuple-element.74.rows_ref, bf16[2048,512]{1,0:T(8,128)(2,1)S(1)} %get-tuple-element.64.d_hl), custom_call_target="tpu_custom_call" | custom-call | tf_op jit(solution)/shard_map/pallas_call | solution.py:47
  81.9 0.2 collective-permute-start.7
  82.1 2.5 %shard_map.99 = f32[1024,256]{1,0:T(8,128)S(1)} custom-call(s32[1]{0:T(128)} %bitcast.core_ref, s32[4,1024]{1,0:T(4,128)S(1)} %get-tuple-element.74.rows_ref, bf16[2048,512]{1,0:T(8,128)(2,1)S(1)} %get-tuple-element.64.d_hl), custom_call_target="tpu_custom_call" | custom-call | tf_op jit(solution)/shard_map/pallas_call | solution.py:47
  84.6 7.1 %shard_map.100 = f32[512,256]{1,0:T(8,128)S(1)} custom-call(s32[3,24]{1,0:T(4,128)S(1)} %pad_add_fusion.2.segs, bf16[1024,256]{1,0:T(8,128)(2,1)} %copy-done.1, bf16[1024,256]{1,0:T(8,128)(2,1)} %copy-done.2, f32[64,32,256]{2,1,0:T(8,128)} %all-to-all-done.own_at, f32[64,32,256]{2,1,0:T(8,128)} %copy-done, s32[2,1024]{1,0:T(2,128)S(1)} %get-tuple-element.59.meta), custom_call_target="tpu_custom_call" | custom-call | tf_op jit(solution)/shard_map/pallas_call | solution.py:47
  91.7 1.1 add.66
  92.8 17.7 %all-to-all-done.1 = f32[64,32,256]{2,1,0:T(8,128)} async-done(((f32[64,32,256]{2,1,0:T(8,128)}), f32[64,32,256]{2,1,0:T(8,128)}, u32[]{:S(2)}, u32[]{:S(2)}) %all-to-all-start.1) | async-done | bytes 2097184 | tf_op jit(solution)/shard_map/all_to_all | solution.py:330
  110.5 3.6 %all-to-all-start.2 = ((f32[8,128,256]{2,1,0:T(8,128)}), f32[8,128,256]{2,1,0:T(8,128)S(1)}, u32[]{:S(2)}, u32[]{:S(2)}) async-start(f32[8,128,256]{2,1,0:T(8,128)} %bitcast.34), calls=%async_computation.2 | async-start | bytes 2097152 | tf_op jit(solution)/shard_map/all_to_all | solution.py:330
  114.1 0.3 collective-permute-start.5
  114.4 1.6 %collective-permute-start.4 = (f32[2,64,256]{2,1,0:T(8,128)S(1)}, f32[2,64,256]{2,1,0:T(8,128)S(1)}, u32[]{:S(2)}, u32[]{:S(2)}) collective-permute-start(f32[2,64,256]{2,1,0:T(8,128)S(1)} %get-tuple-element.71), channel_id=1, source_target_pairs={{0,2},{1,3},{2,0},{3,1},{4,6},{5,7},{6,4},{7,5},{8,10},{9,11},{10,... | collective-permute-start | bytes 393224 | tf_op jit(solution)/shard_map/ppermute | solution.py:358
  116.1 2.3 %collective-permute-start.3 = (f32[2,64,256]{2,1,0:T(8,128)S(1)}, f32[2,64,256]{2,1,0:T(8,128)S(1)}, u32[]{:S(2)}, u32[]{:S(2)}) collective-permute-start(f32[2,64,256]{2,1,0:T(8,128)S(1)} %get-tuple-element.69), channel_id=1, source_target_pairs={{0,1},{1,0},{2,3},{3,2},{4,5},{5,4},{6,7},{7,6},{8,9},{9,8},{10,11... | collective-permute-start | bytes 393224 | tf_op jit(solution)/shard_map/ppermute | solution.py:358
  118.3 4.0 %collective-permute-done.5 = f32[2,64,256]{2,1,0:T(8,128)S(1)} collective-permute-done((f32[2,64,256]{2,1,0:T(8,128)S(1)}, f32[2,64,256]{2,1,0:T(8,128)S(1)}, u32[]{:S(2)}, u32[]{:S(2)}) %collective-permute-start.5) | collective-permute-done | bytes 131104 | tf_op jit(solution)/shard_map/ppermute | solution.py:358
  122.4 0.6 collective-permute-done.3
  123.1 0.4 collective-permute-start.6
  123.4 2.3 %reduce_sum.108 = f32[32,256]{1,0:T(8,128)} reduce(f32[64,32,256]{2,1,0:T(8,128)} %all-to-all-done.1, f32[]{:T(128)} %constant.90.clone.1), dimensions={0}, to_apply=%region_9.10 | reduce | flops 516096 | bytes 2129924 | tf_op jit(solution)/shard_map/reduce_sum | solution.py:457
  125.8 2.0 %collective-permute-done.6 = f32[64,256]{1,0:T(8,128)S(1)} collective-permute-done((f32[64,256]{1,0:T(8,128)S(1)}, f32[64,256]{1,0:T(8,128)S(1)}, u32[]{:S(2)}, u32[]{:S(2)}) %collective-permute-start.6) | collective-permute-done | bytes 65568 | tf_op jit(solution)/shard_map/ppermute | solution.py:358
  127.8 0.6 add_bitcast_fusion
  128.4 1.0 all-to-all-done.2
  129.4 0.7 reduce_sum.109
  (50 shorter events, 1.2 us)
Async XLA Ops:
  1.4 5.6 %collective-permute-start = (s32[4,512]{1,0:T(4,128)S(1)}, s32[4,512]{1,0:T(4,128)S(1)}, u32[]{:S(2)}, u32[]{:S(2)}) collective-permute-start(s32[4,512]{1,0:T(4,128)S(1)} %get-tuple-element.77), channel_id=1, source_target_pairs={{0,7},{1,0},{2,1},{3,2},{4,3},{5,4},{6,5},{7,6},{8,15},{9,8},{10,9... | collective-permute-start | bytes 24584 | tf_op jit(solution)/shard_map/ppermute | solution.py:370
  10.2 22.0 %copy-start.7 = (f32[1,2048,256]{2,1,0:T(8,128)S(1)}, f32[1,2048,256]{2,1,0:T(8,128)}, u32[]{:S(2)}) copy-start(f32[1,2048,256]{2,1,0:T(8,128)} %param.8) | copy-start | bytes 6291460
  10.2 22.0 %copy-start.14 = (f32[1,512,256]{2,1,0:T(8,128)S(1)}, f32[1,512,256]{2,1,0:T(8,128)}, u32[]{:S(2)}) copy-start(f32[1,512,256]{2,1,0:T(8,128)} %param.7) | copy-start | bytes 1572868
  10.2 39.3 %all-to-all-start = ((f32[64,32,256]{2,1,0:T(8,128)}), f32[64,32,256]{2,1,0:T(8,128)}, u32[]{:S(2)}, u32[]{:S(2)}) async-start(f32[64,32,256]{2,1,0:T(8,128)} %broadcast_in_dim.41), calls=%async_computation | async-start | bytes 4194304 | tf_op jit(solution)/shard_map/all_to_all | solution.py:378
  41.1 0.8 copy-start.3
  42.0 0.8 copy-start.5
  42.7 1.0 copy-start.8
  43.7 0.8 copy-start.9
  44.5 0.8 copy-start.10
  45.3 0.8 copy-start.11
  46.1 0.8 copy-start.12
  47.0 0.8 copy-start.13
  49.5 4.4 %collective-permute-start.1 = (f32[64,32,256]{2,1,0:T(8,128)}, f32[64,32,256]{2,1,0:T(8,128)S(1)}, u32[]{:S(2)}, u32[]{:S(2)}) collective-permute-start(f32[64,32,256]{2,1,0:T(8,128)} %all-to-all-done.own_at), channel_id=1, source_target_pairs={{0,8},{8,0},{1,9},{9,1},{2,10},{10,2},{3,11},{11,3},{4,12},{12,4},... | collective-permute-start | bytes 6291464 | tf_op jit(solution)/shard_map/ppermute | solution.py:404
  53.9 7.3 %copy-start = (f32[64,32,256]{2,1,0:T(8,128)}, f32[64,32,256]{2,1,0:T(8,128)S(1)}, u32[]{:S(2)}) copy-start(f32[64,32,256]{2,1,0:T(8,128)S(1)} %collective-permute-done.1.other.other_at) | copy-start | bytes 6291460
  53.9 7.4 %copy-start.4 = (bf16[256,1024]{1,0:T(8,128)(2,1)S(1)}, bf16[256,1024]{1,0:T(8,128)(2,1)}, u32[]{:S(2)}) copy-start(bf16[256,1024]{1,0:T(8,128)(2,1)} %copy-done.3) | copy-start | bytes 1572868
  53.9 7.4 %copy-start.6 = (bf16[256,1024]{1,0:T(8,128)(2,1)S(1)}, bf16[256,1024]{1,0:T(8,128)(2,1)}, u32[]{:S(2)}) copy-start(bf16[256,1024]{1,0:T(8,128)(2,1)} %copy-done.5) | copy-start | bytes 1572868
  61.2 3.3 %copy-start.1 = (bf16[1024,256]{1,0:T(8,128)(2,1)}, bf16[1024,256]{1,0:T(8,128)(2,1)S(1)}, u32[]{:S(2)}) copy-start(bf16[1024,256]{1,0:T(8,128)(2,1)S(1)} %get-tuple-element.60.f_hi.f_hi_at) | copy-start | bytes 1572868
  61.2 3.2 %copy-start.2 = (bf16[1024,256]{1,0:T(8,128)(2,1)}, bf16[1024,256]{1,0:T(8,128)(2,1)S(1)}, u32[]{:S(2)}) copy-start(bf16[1024,256]{1,0:T(8,128)(2,1)S(1)} %get-tuple-element.61.f_lo.f_lo_at) | copy-start | bytes 1572868
  63.9 4.4 %collective-permute-start.2 = (f32[64,32,256]{2,1,0:T(8,128)S(1)}, f32[64,32,256]{2,1,0:T(8,128)S(1)}, u32[]{:S(2)}, u32[]{:S(2)}) collective-permute-start(f32[64,32,256]{2,1,0:T(8,128)S(1)} %shard_map.97), channel_id=1, source_target_pairs={{0,8},{8,0},{1,9},{9,1},{2,10},{10,2},{3,11},{11,3},{4,12},{12,4},... | collective-permute-start | bytes 6291464 | tf_op jit(solution)/shard_map/ppermute | solution.py:435
  70.0 40.5 %all-to-all-start.1 = ((f32[64,32,256]{2,1,0:T(8,128)}), f32[64,32,256]{2,1,0:T(8,128)}, u32[]{:S(2)}, u32[]{:S(2)}) async-start(f32[64,32,256]{2,1,0:T(8,128)} %add.55), calls=%async_computation.1 | async-start | bytes 4194304 | tf_op jit(solution)/shard_map/all_to_all | solution.py:330
  81.9 9.8 %collective-permute-start.7 = (f32[1024,256]{1,0:T(8,128)S(1)}, f32[1024,256]{1,0:T(8,128)S(1)}, u32[]{:S(2)}, u32[]{:S(2)}) collective-permute-start(f32[1024,256]{1,0:T(8,128)S(1)} %shard_map.101), channel_id=1, source_target_pairs={{0,8},{8,0},{1,9},{9,1},{2,10},{10,2},{3,11},{11,3},{4,12},{12,4},... | collective-permute-start | bytes 3145736 | tf_op jit(solution)/shard_map/ppermute | solution.py:438
  110.5 18.9 %all-to-all-start.2 = ((f32[8,128,256]{2,1,0:T(8,128)}), f32[8,128,256]{2,1,0:T(8,128)S(1)}, u32[]{:S(2)}, u32[]{:S(2)}) async-start(f32[8,128,256]{2,1,0:T(8,128)} %bitcast.34), calls=%async_computation.2 | async-start | bytes 2097152 | tf_op jit(solution)/shard_map/all_to_all | solution.py:330
  114.1 8.2 %collective-permute-start.5 = (f32[2,64,256]{2,1,0:T(8,128)S(1)}, f32[2,64,256]{2,1,0:T(8,128)S(1)}, u32[]{:S(2)}, u32[]{:S(2)}) collective-permute-start(f32[2,64,256]{2,1,0:T(8,128)S(1)} %get-tuple-element.70), channel_id=1, source_target_pairs={{0,3},{1,2},{2,1},{3,0},{4,7},{5,6},{6,5},{7,4},{8,11},{9,10},{10,... | collective-permute-start | bytes 393224 | tf_op jit(solution)/shard_map/ppermute | solution.py:358
  114.4 7.9 %collective-permute-start.4 = (f32[2,64,256]{2,1,0:T(8,128)S(1)}, f32[2,64,256]{2,1,0:T(8,128)S(1)}, u32[]{:S(2)}, u32[]{:S(2)}) collective-permute-start(f32[2,64,256]{2,1,0:T(8,128)S(1)} %get-tuple-element.71), channel_id=1, source_target_pairs={{0,2},{1,3},{2,0},{3,1},{4,6},{5,7},{6,4},{7,5},{8,10},{9,11},{10,... | collective-permute-start | bytes 393224 | tf_op jit(solution)/shard_map/ppermute | solution.py:358
  116.1 6.9 %collective-permute-start.3 = (f32[2,64,256]{2,1,0:T(8,128)S(1)}, f32[2,64,256]{2,1,0:T(8,128)S(1)}, u32[]{:S(2)}, u32[]{:S(2)}) collective-permute-start(f32[2,64,256]{2,1,0:T(8,128)S(1)} %get-tuple-element.69), channel_id=1, source_target_pairs={{0,1},{1,0},{2,3},{3,2},{4,5},{5,4},{6,7},{7,6},{8,9},{9,8},{10,11... | collective-permute-start | bytes 393224 | tf_op jit(solution)/shard_map/ppermute | solution.py:358
  123.1 4.7 %collective-permute-start.6 = (f32[64,256]{1,0:T(8,128)S(1)}, f32[64,256]{1,0:T(8,128)S(1)}, u32[]{:S(2)}, u32[]{:S(2)}) collective-permute-start(f32[64,256]{1,0:T(8,128)S(1)} %get-tuple-element.72), channel_id=1, source_target_pairs={{0,4},{4,0},{1,5},{5,1},{2,6},{6,2},{3,7},{7,3},{8,12},{12,8},{9,1... | collective-permute-start | bytes 196616 | tf_op jit(solution)/shard_map/ppermute | solution.py:358
